TPU v7x, 32 devices: a whole 2x2x4 slice. The times are simulated.
32 devices in a mesh: group: 2 (over y), ctx: 4 (over z), head: 4 (over x, core).
Axes of the slice: x: 2, y: 2, z: 4, core: 2. Of those that a mesh axis runs over, the one named last changes fastest.
Arguments:
- query: bfloat16 [1024, 4096], P(('group', 'ctx'), 'head'), parts along dimension 0, may hold values from -8 to 8
- keys: bfloat16 [1024, 512], P(('group', 'ctx'), 'head'), parts along dimension 0, may hold values from -6 to 6
- values: bfloat16 [1024, 512], P(('group', 'ctx'), 'head'), parts along dimension 0, may hold values from -6 to 6
- residual: bfloat16 [1024, 2048], P(('group', 'ctx', 'head')), parts along dimension 0, may hold values from -15 to 15
- o_weight: bfloat16 [4096, 2048], P('head', 'ctx'), may hold values from -0.09375 to 0.09375
- gain: float32 [2048], replicated, may hold values from 0.1 to 1.9
- routes: int32 [1024, 8], P(('group', 'ctx', 'head')), parts along dimension 0, may hold values from 0 to 15, all different within a row; in each aligned block of 32 rows (0 to 31, 32 to 63, ...) at most 32 rows name the same one
- gates: float32 [1024, 8], P(('group', 'ctx', 'head')), parts along dimension 0, may hold values from 0.05 to 1
- w_gate: bfloat16 [16, 2048, 768], P(('ctx', 'head')), may hold values from -0.125 to 0.125
- w_up: bfloat16 [16, 2048, 768], P(('ctx', 'head')), may hold values from -0.125 to 0.125
- w_down: bfloat16 [16, 768, 2048], P(('ctx', 'head')), may hold values from -0.625 to 0.625
Outputs:
- mixed: bfloat16 [1024, 2048], P(('group', 'ctx', 'head')), parts along dimension 0
- expert_mix: bfloat16 [1024, 2048], P(('group', 'ctx', 'head')), parts along dimension 0
There are 2 independent parts, one for each index of `group`. A program takes and returns all parts, laid end to end along the dimension named above; an argument that names none is the same for every part. Nothing has to cross between parts.
Inputs may be any that keep to these rules, and one draw needn't show every extreme that they name: `routes`: the 8 experts of a token are distinct. In each aligned block of 32 tokens (the tokens of one owner device), no expert is named more than 32 times, a bound that some block reaches.
All inputs are finite; a program needn't handle non-finite values.
Results may differ from a plain program's by a relative error of at most 0.019.
Values may be sent and summed in bfloat16 or wider, within the bound.
No kernel may reach another device: no remote copies, remote signals or barrier semaphores. Data moves between devices by JAX's collectives and lax.ppermute only.
A program may use at most 128 MiB of HBM per device.

v0:
```python
import jax
import jax.numpy as jnp
from jax import lax
from jax.sharding import PartitionSpec as P

HEAD_DIMENSION = 128


def expert_apply(arrived, gate_proj, up_proj, down_proj):
    shape_in = arrived.shape
    flat_rows = arrived.reshape(-1, shape_in[-1])
    gate_act = jnp.dot(flat_rows, gate_proj, preferred_element_type=jnp.float32)
    up_act = jnp.dot(flat_rows, up_proj, preferred_element_type=jnp.float32)
    hidden = (jax.nn.silu(gate_act) * up_act).astype(jnp.bfloat16)
    output = jnp.dot(hidden, down_proj, preferred_element_type=jnp.float32).astype(jnp.bfloat16)
    return output.reshape(shape_in)


def body(query, keys, values, residual, o_weight, gain, routes, gates, w_gate, w_up, w_down):
    head_size = HEAD_DIMENSION
    query_rows = query.shape[0]
    kv_heads = keys.shape[1] // head_size
    q_heads = query.shape[1] // head_size
    head_replicas = q_heads // kv_heads
    scale = head_size ** (-0.5)
    queries = query.reshape(query_rows, kv_heads, head_replicas, head_size)
    first_pos = lax.axis_index("ctx") * query_rows
    query_pos = first_pos + jnp.arange(query_rows, dtype=jnp.int32)
    last_pos = first_pos + query_rows - 1

    def accumulate(carry, pieces):
        run_max, run_sum, run_acc = carry
        key_piece, value_piece = pieces
        width = key_piece.shape[0]
        key_pos = jnp.arange(width, dtype=jnp.int32)
        visible = key_pos[None, :] <= query_pos[:, None]
        scores = (
            jnp.einsum(
                "veqi,zei->eqvz",
                queries,
                key_piece.reshape(width, kv_heads, head_size),
                preferred_element_type=jnp.float32,
            )
            * scale
        )
        scores = jnp.where(visible, scores, -1e30)
        new_max = jnp.maximum(run_max, jnp.max(scores, axis=-1))
        weights = jnp.where(visible, jnp.exp(scores - new_max[..., None]), 0.0)
        new_sum = jnp.sum(weights, axis=-1)
        update = jnp.einsum(
            "pexa,apo->pexo",
            weights.astype(jnp.bfloat16),
            value_piece.reshape(width, kv_heads, head_size),
            preferred_element_type=jnp.float32,
        )
        return (new_max, new_sum, update)

    start_state = (
        jnp.full((kv_heads, head_replicas, query_rows), -1e30, jnp.float32),
        jnp.zeros((kv_heads, head_replicas, query_rows), jnp.float32),
        jnp.zeros((kv_heads, head_replicas, query_rows, head_size), jnp.float32),
    )
    pieces = (
        lax.all_gather(keys, "ctx", axis=0, tiled=True),
        lax.all_gather(values, "ctx", axis=0, tiled=True),
    )
    run_max, run_sum, run_acc = lax.cond(
        jnp.int32(0) > last_pos, lambda: start_state, lambda: accumulate(start_state, pieces)
    )
    attended = (
        (run_acc / run_sum[..., None])
        .transpose(2, 0, 1, 3)
        .reshape(query_rows, q_heads * head_size)
        .astype(jnp.bfloat16)
    )
    head_terms = jnp.dot(
        attended,
        lax.all_gather(o_weight, "ctx", axis=1, tiled=True),
        preferred_element_type=jnp.float32,
    )
    summed = lax.psum_scatter(
        head_terms.astype(jnp.bfloat16), "head", scatter_dimension=0, tiled=True
    ).astype(jnp.float32)
    mixed = (summed + residual.astype(jnp.float32)).astype(jnp.bfloat16)
    mixed_f = mixed.astype(jnp.float32)
    normed = (
        mixed_f * lax.rsqrt(jnp.mean(mixed_f * mixed_f, axis=-1, keepdims=True) + 1e-06) * gain
    ).astype(jnp.bfloat16)
    own_rows = residual.shape[0]
    model_dim = residual.shape[1]
    top_count = routes.shape[1]
    ctx_count = lax.axis_size("ctx")
    head_count = lax.axis_size("head")
    devices = ctx_count * head_count
    capacity = min(own_rows, max(2, 2 * own_rows * top_count // devices))
    expert_ids = routes.reshape(-1)
    onehot = (expert_ids[:, None] == jnp.arange(devices, dtype=jnp.int32)[None, :]).astype(
        jnp.int32
    )
    slots = jnp.sum((jnp.cumsum(onehot, axis=0) - 1) * onehot, axis=1)
    target = expert_ids * capacity + slots
    outgoing = (
        jnp.zeros((devices * capacity, model_dim), jnp.bfloat16)
        .at[target]
        .set(jnp.repeat(normed, top_count, axis=0))
    )
    outgoing = outgoing.reshape(devices, capacity, model_dim)
    gate_proj = w_gate[0]
    up_proj = w_up[0]
    down_proj = w_down[0]
    computed = expert_apply(
        lax.all_to_all(outgoing, ("ctx", "head"), split_axis=0, concat_axis=0, tiled=True),
        gate_proj,
        up_proj,
        down_proj,
    )
    returned = lax.all_to_all(computed, ("ctx", "head"), split_axis=0, concat_axis=0, tiled=True)
    selected_entries = returned.reshape(devices * capacity, model_dim)[target]
    selected_entries = selected_entries.astype(jnp.float32).reshape(own_rows, top_count, model_dim)
    weight_norm = gates / jnp.sum(gates, axis=-1, keepdims=True)
    expert_mix = jnp.sum(selected_entries * weight_norm[..., None], axis=1).astype(jnp.bfloat16)
    return (mixed, expert_mix)


def solution(mesh):
    return jax.shard_map(
        body,
        mesh=mesh,
        in_specs=(
            P(("group", "ctx"), "head"),
            P(("group", "ctx"), "head"),
            P(("group", "ctx"), "head"),
            P(("group", "ctx", "head"), None),
            P("head", "ctx"),
            P(),
            P(("group", "ctx", "head"), None),
            P(("group", "ctx", "head"), None),
            P(("ctx", "head"), None, None),
            P(("ctx", "head"), None, None),
            P(("ctx", "head"), None, None),
        ),
        out_specs=(P(("group", "ctx", "head"), None), P(("group", "ctx", "head"), None)),
        check_vma=False,
    )
```

profile of v0, /device:TPU:11, one launch (start us, length us, event | category | flops | bytes accessed | tf_op | source)
XLA Modules:
  0.0 255.7 jit_solution(5889170970731669494)
XLA Ops:
  7.2 0.7 all-gather.2.cloned.1.call-update
  8.0 11.0 %all_gather.10 = bf16[512,128]{1,0:T(8,128)(2,1)S(1)} all-gather(bf16[128,128]{1,0:T(8,128)(2,1)} %param.15), channel_id=1, replica_groups=mesh['group'=2,'ctx'=4,'head'=4] {'ctx'}, dimensions={0}, use_global_device_ids=true | all-gather | bytes 163840 | tf_op jit(solution)/shard_map/all_gather | solution.py:65
  19.0 14.5 %all_gather.9 = bf16[512,128]{1,0:T(8,128)(2,1)S(1)} all-gather(bf16[128,128]{1,0:T(8,128)(2,1)} %param.14), channel_id=1, replica_groups=mesh['group'=2,'ctx'=4,'head'=4] {'ctx'}, dimensions={0}, use_global_device_ids=true | all-gather | bytes 163840 | tf_op jit(solution)/shard_map/all_gather | solution.py:64
  33.5 2.6 %conditional.1 = (f32[1,8,128]{2,1,0:T(8,128)S(1)}, f32[1,8,128,128]{2,3,1,0:T(8,128)S(1)}) conditional(s32[]{:T(128)} %convert_element_type.54, (s32[]{:T(128)}, s32[128]{0:T(128)S(1)}, bf16[128,1024]{1,0:T(8,128)(2,1)}, bf16[512,128]{1,0:T(8,128)(2,1)S(1)}, bf16[512,128]{1,0:T(8,128)(2,1)S(1)}) %tuple.16, () %tuple.17), branch_computations={%region_0.3_spmd, %region_3.4_spmd} | conditional | flops 275315840 | bytes 7628308 | solution.py:67
  33.5 0.1 iota_compare_fusion
  33.6 1.4 fusion
  35.0 0.6 convolution_bitcast_fusion
  35.6 0.5 fusion.2
  36.2 0.1 divide_convert_fusion
  36.2 55.0 %all-gather.2.cloned.1.call-done = bf16[1024,2048]{1,0:T(8,128)(2,1)} async-done(((bf16[1024,512]{1,0:T(8,128)(2,1)}), bf16[1024,2048]{1,0:T(8,128)(2,1)}) %all-gather.2.cloned.1.call-update) | async-done | bytes 4194320 | tf_op jit(solution)/shard_map/all_gather | solution.py:78
  91.2 3.8 %convolution_convert_fusion = bf16[128,2048]{1,0:T(8,128)(2,1)} fusion(bf16[128,1024]{0,1:T(8,128)(2,1)S(1)} %bitcast.93, bf16[1024,2048]{1,0:T(8,128)(2,1)} %all-gather.2.cloned.1.call-done), kind=kOutput, calls=%fused_computation.32 | convolution fusion | flops 537133056 | bytes 4980736 | tf_op jit(solution)/shard_map/dot_general | solution.py:76
  95.0 0.1 copy.21
  95.1 0.1 eq.29
  95.2 0.1 eq.25
  95.3 0.6 reduce-window.6
  95.9 0.2 slice_reduce_fusion
  96.1 0.1 copy.20
  96.2 0.1 mul.68
  96.3 0.1 fusion.40
  96.4 20.1 %reduce-scatter.2.cloned.1.call-done = bf16[32,2048]{1,0:T(8,128)(2,1)} async-done(((bf16[128,2048]{1,0:T(8,128)(2,1)}), bf16[32,2048]{1,0:T(8,128)(2,1)}) %reduce-scatter.2.cloned.1.call-update) | async-done | bytes 131088 | tf_op jit(solution)/shard_map/reduce_scatter | solution.py:81
  116.5 1.1 fusion.36
  117.6 0.1 fusion.38
  117.7 3.7 %scatter_custom_fusion = bf16[512,2048]{1,0:T(8,128)(2,1)} fusion(s32[256]{0:T(256)S(1)} %bitcast.96, bf16[]{:T(256)} %constant.28.clone.1, bf16[32,2048]{1,0:T(8,128)(2,1)S(1)} %fusion.38), kind=kCustom, calls=%fused_computation.36 | custom fusion | bytes 2228226 | tf_op jit(solution)/shard_map/scatter | solution.py:105
  121.5 54.1 %all_to_all.10 = bf16[16,32,2048]{2,1,0:T(8,128)(2,1)S(1)} all-to-all(bf16[16,32,2048]{2,1,0:T(8,128)(2,1)} %bitcast.89), channel_id=1, replica_groups=mesh['group'=2,'ctx'=4,'head'=4] {'ctx','head'}, dimensions={0} | all-to-all | bytes 4194304 | tf_op jit(solution)/shard_map/all_to_all | solution.py:112
  175.5 1.3 copy-done.1
  176.8 3.0 %fusion.22 = f32[512,768]{1,0:T(8,128)} fusion(bf16[512,2048]{1,0:T(8,128)(2,1)S(1)} %bitcast.91, bf16[1,2048,768]{2,1,0:T(8,128)(2,1)S(1)} %copy-done.7), kind=kOutput, calls=%fused_computation.29 | convolution fusion | flops 1610612736 | bytes 6815744 | tf_op jit(solution)/shard_map/dot_general | solution.py:12
  179.8 8.3 %fusion.24 = bf16[512,2048]{1,0:T(8,128)(2,1)} fusion(bf16[1,768,2048]{2,1,0:T(8,128)(2,1)S(1)} %copy-done, f32[512,768]{1,0:T(8,128)} %fusion.22, bf16[512,2048]{1,0:T(8,128)(2,1)} %bitcast.92, bf16[1,2048,768]{2,1,0:T(8,128)(2,1)} %param.22), kind=kOutput, calls=%fused_computation.31 | convolution fusion | flops 3224633344 | bytes 12058624 | tf_op jit(solution)/shard_map/dot_general | solution.py:15
  188.1 5.2 %all-to-all-start.1 = ((bf16[16,32,2048]{2,1,0:T(8,128)(2,1)}), bf16[16,32,2048]{2,1,0:T(8,128)(2,1)}, u32[]{:S(2)}, u32[]{:S(2)}) async-start(bf16[16,32,2048]{2,1,0:T(8,128)(2,1)} %bitcast.90), calls=%async_computation.2 | async-start | bytes 4194304 | tf_op jit(solution)/shard_map/all_to_all | solution.py:117
  193.3 0.1 copy.24
  193.4 47.4 %all-to-all-done.1 = bf16[16,32,2048]{2,1,0:T(8,128)(2,1)} async-done(((bf16[16,32,2048]{2,1,0:T(8,128)(2,1)}), bf16[16,32,2048]{2,1,0:T(8,128)(2,1)}, u32[]{:S(2)}, u32[]{:S(2)}) %all-to-all-start.1) | async-done | bytes 2097184 | tf_op jit(solution)/shard_map/all_to_all | solution.py:117
  240.8 5.2 %gather_fusion = bf16[256,2048]{1,0:T(8,128)(2,1)} fusion(bf16[512,2048]{1,0:T(8,128)(2,1)} %bitcast.20, s32[1024]{0:T(1024)S(1)} %pad_clamp_fusion), kind=kCustom, calls=%fused_computation | custom fusion | bytes 2098176 | tf_op jit(solution)/shard_map/gather | solution.py:118
  246.0 2.9 %fusion.27 = bf16[32,2048]{1,0:T(8,128)(2,1)} fusion(bf16[256,2048]{1,0:T(8,128)(2,1)} %gather_fusion, f32[32,8]{1,0:T(8,128)S(1)} %copy.24), kind=kLoop, calls=%fused_computation.34 | loop fusion | flops 1507328 | bytes 1180672 | tf_op jit(solution)/shard_map/reduce_sum | solution.py:121
  (30 shorter events, 0.2 us)
Async XLA Ops:
  7.2 172.6 %copy-start = (bf16[1,768,2048]{2,1,0:T(8,128)(2,1)S(1)}, bf16[1,768,2048]{2,1,0:T(8,128)(2,1)}, u32[]{:S(2)}) copy-start(bf16[1,768,2048]{2,1,0:T(8,128)(2,1)} %param.23) | copy-start | bytes 9437188
  7.2 84.0 %all-gather.2.cloned.1.call-start = ((), (), s32[]{:S(2)}) async-start(), calls=%async_computation.3 | async-start | bytes 5242880 | tf_op jit(solution)/shard_map/all_gather | solution.py:78
  7.9 108.6 %reduce-scatter.2.cloned.1.call-start = ((), (), s32[]{:S(2)}) async-start(), calls=%async_computation.4 | async-start | bytes 655360 | tf_op jit(solution)/shard_map/reduce_scatter | solution.py:81
  91.2 3.8 %copy-start.4 = (s32[32,8]{0,1:T(8,128)S(1)}, s32[32,8]{0,1:T(8,128)}, u32[]{:S(2)}) copy-start(s32[32,8]{0,1:T(8,128)} %param.19) | copy-start | bytes 3076
  91.2 25.3 %copy-start.3 = (bf16[32,2048]{1,0:T(8,128)(2,1)S(1)}, bf16[32,2048]{1,0:T(8,128)(2,1)}, u32[]{:S(2)}) copy-start(bf16[32,2048]{1,0:T(8,128)(2,1)} %param.16) | copy-start | bytes 393220
  91.2 26.4 %copy-start.6 = (f32[2048]{0:T(1024)S(1)}, f32[2048]{0:T(1024)}, u32[]{:S(2)}) copy-start(f32[2048]{0:T(1024)} %param.18) | copy-start | bytes 24580
  117.6 58.0 %copy-start.2 = (bf16[32,2048]{1,0:T(8,128)(2,1)}, bf16[32,2048]{1,0:T(8,128)(2,1)S(1)}, u32[]{:S(2)}) copy-start(bf16[32,2048]{1,0:T(8,128)(2,1)S(1)} %get-tuple-element.28) | copy-start | bytes 393220
  121.5 55.4 %copy-start.7 = (bf16[1,2048,768]{2,1,0:T(8,128)(2,1)S(1)}, bf16[1,2048,768]{2,1,0:T(8,128)(2,1)}, u32[]{:S(2)}) copy-start(bf16[1,2048,768]{2,1,0:T(8,128)(2,1)} %param.21) | copy-start | bytes 9437188
  175.5 1.3 copy-start.1
  188.1 5.2 %copy-start.5 = (f32[32,8]{0,1:T(8,128)S(1)}, f32[32,8]{0,1:T(8,128)}, u32[]{:S(2)}) copy-start(f32[32,8]{0,1:T(8,128)} %param.20) | copy-start | bytes 3076
  188.1 52.7 %all-to-all-start.1 = ((bf16[16,32,2048]{2,1,0:T(8,128)(2,1)}), bf16[16,32,2048]{2,1,0:T(8,128)(2,1)}, u32[]{:S(2)}, u32[]{:S(2)}) async-start(bf16[16,32,2048]{2,1,0:T(8,128)(2,1)} %bitcast.90), calls=%async_computation.2 | async-start | bytes 4194304 | tf_op jit(solution)/shard_map/all_to_all | solution.py:117
Sparse Core Ops, SparseCore 0:
  9.6 81.6 all-gather.1
  95.1 21.3 reduce-scatter.1
where the time goes:
time: 256 us
  waiting for transfers between devices  123 us (48%)
  blocking collectives  79.6 us (31%)
  matrix products  17.1 us (7%)
  between operations  14.1 us (6%)
  local copies, waits for them, and re-layouts  11 us (4%)
  other arithmetic  5.41 us (2%)
  starting transfers between devices  5.23 us (2%)
    all_gather x1, waiting for transfers between devices, body(): lax.all_gather(o_weight, 'ctx', axis=1, tiled=True)  55 us
    all_to_all x1, blocking collectives, body(): lax.all_to_all(outgoing, ('ctx', 'head'), split_axis=0, concat_axis=0, ti...  54.1 us
    all_to_all x1, waiting for transfers between devices, body(): lax.all_to_all(computed, ('ctx', 'head'), split_axis=0, concat_axis=0, ti...  47.4 us
    reduce_scatter x1, waiting for transfers between devices, body(): lax.psum_scatter(head_terms.astype(jnp.bfloat16), 'head', scatter_dimensi...  20.1 us
    all_gather x1, blocking collectives, body(): lax.all_gather(keys, 'ctx', axis=0, tiled=True)  14.5 us
    all_gather x1, blocking collectives, body(): lax.all_gather(values, 'ctx', axis=0, tiled=True)  11 us
    dot_general x1, matrix products, expert_apply(): jnp.dot(hidden, down_proj, preferred_element_type=jnp.float32)  8.28 us
    gather x1, local copies, waits for them, and re-layouts, body(): selected_entries = returned.reshape(devices * capacity, model_dim)[target]  5.21 us
  transfers between devices with their start and end apart: 3, of which 3 were waited for; matrix products, arithmetic and copies ran while one was open for 2% of the time, Pallas kernels for 0%

commit v1 on v0

v1 whole, which is shorter than its diff:
```python
import functools

import jax
import jax.numpy as jnp
from jax import lax
from jax.experimental import pallas as pl
from jax.experimental.pallas import tpu as pltpu
from jax.sharding import PartitionSpec as P

HEAD_DIMENSION = 128
CHUNKS = ((0, 1, 2, 3),)


def expert_apply(arrived, gate_proj, up_proj, down_proj):
    shape_in = arrived.shape
    flat_rows = arrived.reshape(-1, shape_in[-1])
    gate_act = jnp.dot(flat_rows, gate_proj, preferred_element_type=jnp.float32)
    up_act = jnp.dot(flat_rows, up_proj, preferred_element_type=jnp.float32)
    hidden = (jax.nn.silu(gate_act) * up_act).astype(jnp.bfloat16)
    output = jnp.dot(hidden, down_proj, preferred_element_type=jnp.float32).astype(jnp.bfloat16)
    return output.reshape(shape_in)


def sparse_body(query, keys, values, residual, o_weight, gain, routes, gates, w_gate, w_up, w_down):
    head_size = HEAD_DIMENSION
    query_rows = query.shape[0]
    kv_heads = keys.shape[1] // head_size
    q_heads = query.shape[1] // head_size
    head_replicas = q_heads // kv_heads
    scale = head_size ** (-0.5)
    queries = query.reshape(query_rows, kv_heads, head_replicas, head_size)
    first_pos = lax.axis_index("ctx") * query_rows
    query_pos = first_pos + jnp.arange(query_rows, dtype=jnp.int32)
    key_all = lax.all_gather(keys, "ctx", axis=0, tiled=True)
    value_all = lax.all_gather(values, "ctx", axis=0, tiled=True)
    width = key_all.shape[0]
    visible = jnp.arange(width, dtype=jnp.int32)[None, :] <= query_pos[:, None]
    scores = (
        jnp.einsum(
            "veqi,zei->eqvz",
            queries,
            key_all.reshape(width, kv_heads, head_size),
            preferred_element_type=jnp.float32,
        )
        * scale
    )
    scores = jnp.where(visible, scores, -1e30)
    top = jnp.max(scores, axis=-1)
    weights = jnp.where(visible, jnp.exp(scores - top[..., None]), 0.0)
    total = jnp.sum(weights, axis=-1)
    summed_values = jnp.einsum(
        "pexa,apo->pexo",
        weights.astype(jnp.bfloat16),
        value_all.reshape(width, kv_heads, head_size),
        preferred_element_type=jnp.float32,
    )
    attended = (
        (summed_values / total[..., None])
        .transpose(2, 0, 1, 3)
        .reshape(query_rows, q_heads * head_size)
        .astype(jnp.bfloat16)
    )
    head_terms = jnp.dot(
        attended,
        lax.all_gather(o_weight, "ctx", axis=1, tiled=True),
        preferred_element_type=jnp.float32,
    )
    summed = lax.psum_scatter(
        head_terms.astype(jnp.bfloat16), "head", scatter_dimension=0, tiled=True
    ).astype(jnp.float32)
    mixed = (summed + residual.astype(jnp.float32)).astype(jnp.bfloat16)
    mixed_f = mixed.astype(jnp.float32)
    normed = (
        mixed_f * lax.rsqrt(jnp.mean(mixed_f * mixed_f, axis=-1, keepdims=True) + 1e-06) * gain
    ).astype(jnp.bfloat16)
    own_rows = residual.shape[0]
    model_dim = residual.shape[1]
    top_count = routes.shape[1]
    devices = lax.axis_size("ctx") * lax.axis_size("head")
    capacity = slots_per_expert(own_rows, top_count, devices)
    expert_ids = routes.reshape(-1)
    onehot = (expert_ids[:, None] == jnp.arange(devices, dtype=jnp.int32)[None, :]).astype(
        jnp.int32
    )
    slots = jnp.sum((jnp.cumsum(onehot, axis=0) - 1) * onehot, axis=1)
    target = expert_ids * capacity + slots
    outgoing = (
        jnp.zeros((devices * capacity, model_dim), jnp.bfloat16)
        .at[target]
        .set(jnp.repeat(normed, top_count, axis=0))
    )
    outgoing = outgoing.reshape(devices, capacity, model_dim)
    computed = expert_apply(
        lax.all_to_all(outgoing, ("ctx", "head"), split_axis=0, concat_axis=0, tiled=True),
        w_gate[0],
        w_up[0],
        w_down[0],
    )
    returned = lax.all_to_all(computed, ("ctx", "head"), split_axis=0, concat_axis=0, tiled=True)
    selected_entries = returned.reshape(devices * capacity, model_dim)[target]
    selected_entries = selected_entries.astype(jnp.float32).reshape(own_rows, top_count, model_dim)
    weight_norm = gates / jnp.sum(gates, axis=-1, keepdims=True)
    expert_mix = jnp.sum(selected_entries * weight_norm[..., None], axis=1).astype(jnp.bfloat16)
    return (mixed, expert_mix)


def slots_per_expert(own_rows, top_count, devices):
    return min(own_rows, max(2, 2 * own_rows * top_count // devices))


def place():
    return lax.axis_index("ctx"), lax.axis_index("head")


def shift(x, by):
    n = lax.axis_size("ctx")
    return lax.ppermute(x, "ctx", [(i, (i + by) % n) for i in range(n)])


def swap(x, mask):
    n = lax.axis_size("head")
    return lax.ppermute(x, "head", [(i, i ^ mask) for i in range(n)])


def attend_kernel(steps, n_ctx, n_head, *refs):
    n = len(steps)
    q_refs, kv_refs, w_ref = refs[:n], refs[n : n + n_ctx], refs[n + n_ctx]
    own_ref = refs[n + n_ctx + 1]
    send_refs = refs[n + n_ctx + 2 : n + n_ctx + 1 + n_head]
    k_all, v_all, att, prod = refs[n + n_ctx + 1 + n_head :]
    hd = HEAD_DIMENSION
    rows = q_refs[0].shape[0]
    width = kv_refs[0].shape[0]
    own_rows = rows // n_head
    c, h = place()
    key_pos = []
    for m in range(n_ctx):
        k_all[m * width : (m + 1) * width, :] = kv_refs[m][:, :hd]
        v_all[m * width : (m + 1) * width, :] = kv_refs[m][:, hd:]
        block = lax.rem(c - m + n_ctx, n_ctx)
        key_pos.append(block * width + lax.broadcasted_iota(jnp.int32, (rows, width), 1))
    key_pos = jnp.concatenate(key_pos, axis=1)
    row_pos = lax.broadcasted_iota(jnp.int32, (rows, 1), 0)
    scale = hd**-0.5
    for i, step in enumerate(steps):
        first = lax.rem(c - step + n_ctx, n_ctx) * rows
        visible = key_pos <= first + row_pos
        for g in range(q_refs[i].shape[1] // hd):
            cols = slice(g * hd, (g + 1) * hd)
            scores = lax.dot_general(
                q_refs[i][:, cols],
                k_all[...],
                (((1,), (1,)), ((), ())),
                preferred_element_type=jnp.float32,
            )
            scores = jnp.where(visible, scores, -1e30)
            top = jnp.max(scores, axis=-1, keepdims=True)
            weights = jnp.exp((scores - top) * scale)
            total = jnp.sum(weights, axis=-1, keepdims=True)
            summed = jnp.dot(
                weights.astype(jnp.bfloat16), v_all[...], preferred_element_type=jnp.float32
            )
            att[:, cols] = (summed / total).astype(jnp.bfloat16)
        prod[...] = jnp.dot(att[...], w_ref[...], preferred_element_type=jnp.float32)
        own_ref[i] = prod[pl.ds(pl.multiple_of(h * own_rows, own_rows), own_rows), :]
        for j in range(1, n_head):
            other = jnp.bitwise_xor(h, j)
            start = pl.multiple_of(other * own_rows, own_rows)
            send_refs[j - 1][i] = prod[pl.ds(start, own_rows), :].astype(jnp.bfloat16)


def attend(steps, q_list, kv_list, o_weight):
    n_ctx, n_head = lax.axis_size("ctx"), lax.axis_size("head")
    rows, q_cols = q_list[0].shape
    width = kv_list[0].shape[0]
    out_cols = o_weight.shape[1]
    n = len(steps)
    piece = (n, rows // n_head, out_cols)
    vmem = pl.BlockSpec(memory_space=pltpu.VMEM)
    flops = 4 * n * rows * q_cols * width * n_ctx + 2 * n * rows * q_cols * out_cols
    return pl.pallas_call(
        functools.partial(attend_kernel, steps, n_ctx, n_head),
        out_shape=[jax.ShapeDtypeStruct(piece, jnp.float32)]
        + [jax.ShapeDtypeStruct(piece, jnp.bfloat16)] * (n_head - 1),
        in_specs=[vmem] * (n + n_ctx + 1),
        out_specs=[vmem] * n_head,
        scratch_shapes=[
            pltpu.VMEM((width * n_ctx, HEAD_DIMENSION), jnp.bfloat16),
            pltpu.VMEM((width * n_ctx, HEAD_DIMENSION), jnp.bfloat16),
            pltpu.VMEM((rows, q_cols), jnp.bfloat16),
            pltpu.VMEM((rows, out_cols), jnp.float32),
        ],
        cost_estimate=pl.CostEstimate(
            flops=flops, bytes_accessed=2 * q_cols * out_cols, transcendentals=flops // 512
        ),
        name="attend",
    )(*q_list, *kv_list, o_weight)


def expert_kernel(chunks, n_ctx, n_head, *refs):
    n_pieces = len(chunks) * n_head * n_ctx
    pieces, refs = refs[:n_pieces], refs[n_pieces:]
    share_refs, refs = refs[:n_head], refs[n_head:]
    gain_ref, gate_ref, up_ref, down_ref = refs[:4]
    keep_ref, send_ref, mixed_ref = refs[4:7]
    x_ref, acc_ref, share_ref = refs[7:]
    step = pl.program_id(0)
    own_rows = mixed_ref.shape[0]
    cols = pieces[0].shape[-1]
    c, h = place()

    def row_block(j, t):
        return (((j % 2) * (n_head // 2) + j // 2) * n_ctx + t) * own_rows

    @pl.when(step == 0)
    def _():
        expert = c * n_head + h
        for j in range(n_head):
            lanes = lax.broadcasted_iota(jnp.int32, share_refs[j].shape[1:], 1)
            for t in range(n_ctx):
                start = row_block(j, t)
                shares = jnp.where(lanes == expert, share_refs[j][t], 0.0)
                share_ref[start : start + own_rows, :] = jnp.sum(shares, axis=-1, keepdims=True)
        for j in range(n_head):
            for t in range(n_ctx):
                start = row_block(j, t)
                blocks = []
                square = jnp.zeros((own_rows, 1), jnp.float32)
                for m in range(n_ctx):
                    s = (t - m) % n_ctx
                    for k, steps in enumerate(chunks):
                        if s in steps:
                            ref = pieces[(k * n_head + j) * n_ctx + m]
                            block = ref[steps.index(s)]
                    block_f = block.astype(jnp.float32)
                    square += jnp.sum(block_f * block_f, axis=-1, keepdims=True)
                    col = lax.rem(c - m + n_ctx, n_ctx)
                    blocks.append((block_f, col))
                    if j == 0 and t == 0:
                        mixed_ref[:, pl.ds(pl.multiple_of(col * cols, cols), cols)] = block
                root = lax.rsqrt(square / (cols * n_ctx) + 1e-06)
                for block_f, col in blocks:
                    at = pl.ds(pl.multiple_of(col * cols, cols), cols)
                    x_ref[start : start + own_rows, at] = (
                        block_f * root * gain_ref[:, at]
                    ).astype(jnp.bfloat16)

    gate = jnp.dot(x_ref[...], gate_ref[0], preferred_element_type=jnp.float32)
    up = jnp.dot(x_ref[...], up_ref[0], preferred_element_type=jnp.float32)
    hidden = (gate * jax.nn.sigmoid(gate) * up).astype(jnp.bfloat16)
    out = jnp.dot(hidden, down_ref[0], preferred_element_type=jnp.float32)

    @pl.when(step == 0)
    def _():
        acc_ref[...] = out

    @pl.when((step > 0) & (step < pl.num_programs(0) - 1))
    def _():
        acc_ref[...] += out

    @pl.when(step == pl.num_programs(0) - 1)
    def _():
        final = ((acc_ref[...] + out) * share_ref[...]).astype(jnp.bfloat16)
        half = final.shape[0] // 2
        keep_ref[...] = final[:half].reshape(keep_ref.shape)
        send_ref[...] = final[half:].reshape(send_ref.shape)


def experts(chunks, pieces, shares, gain, w_gate, w_up, w_down, own_rows):
    n_ctx, n_head = lax.axis_size("ctx"), lax.axis_size("head")
    dim, hidden = w_gate.shape[1:]
    rows = own_rows * n_ctx * n_head
    tile = hidden // 3
    vmem = pl.BlockSpec(memory_space=pltpu.VMEM)
    out_half = jax.ShapeDtypeStruct((n_head // 2, n_ctx, own_rows, dim), jnp.bfloat16)
    return pl.pallas_call(
        functools.partial(expert_kernel, chunks, n_ctx, n_head),
        grid=(hidden // tile,),
        out_shape=[out_half, out_half, jax.ShapeDtypeStruct((own_rows, dim), jnp.bfloat16)],
        in_specs=[vmem] * (len(pieces) + len(shares) + 1)
        + [
            pl.BlockSpec((1, dim, tile), lambda f: (0, 0, f)),
            pl.BlockSpec((1, dim, tile), lambda f: (0, 0, f)),
            pl.BlockSpec((1, tile, dim), lambda f: (0, f, 0)),
        ],
        out_specs=[vmem] * 3,
        scratch_shapes=[
            pltpu.VMEM((rows, dim), jnp.bfloat16),
            pltpu.VMEM((rows, dim), jnp.float32),
            pltpu.VMEM((rows, 1), jnp.float32),
        ],
        cost_estimate=pl.CostEstimate(
            flops=6 * rows * dim * hidden, bytes_accessed=6 * dim * hidden, transcendentals=0
        ),
        name="experts",
    )(*pieces, *shares, gain.reshape(1, -1), w_gate, w_up, w_down)


def dense_body(query, keys, values, residual, o_weight, gain, routes, gates, w_gate, w_up, w_down):
    n_ctx, n_head = lax.axis_size("ctx"), lax.axis_size("head")
    own_rows, dim = residual.shape
    cols = o_weight.shape[1]
    c, h = place()

    kv_list = [jnp.concatenate([keys, values], axis=1)]
    q_list = [query]
    for _ in range(n_ctx - 1):
        kv_list.append(shift(kv_list[-1], 1))
        q_list.append(shift(q_list[-1], 1))

    share = gates / jnp.sum(gates, axis=-1, keepdims=True)
    ids = jnp.arange(n_ctx * n_head, dtype=jnp.int32)
    table = jnp.sum(jnp.where(routes[..., None] == ids, share[..., None], 0.0), axis=1)
    table = jnp.stack([table] + [shift(table, t) for t in range(1, n_ctx)])
    shares = [table]
    bit = n_head // 2
    while bit:
        shares = shares + [swap(s, bit) for s in shares]
        bit //= 2
    order = head_order(n_head)
    shares = [shares[order.index(j)] for j in range(n_head)]

    by_tile = residual.reshape(own_rows, n_ctx, cols)
    skip = []
    for s in range(n_ctx):
        part = lax.dynamic_index_in_dim(by_tile, lax.rem(c + s, n_ctx), axis=1, keepdims=False)
        skip.append(shift(part, s) if s else part)

    pieces = []
    for steps in CHUNKS:
        own, *sends = attend(steps, [q_list[s] for s in steps], kv_list, o_weight)
        total = own
        for j, send in enumerate(sends, 1):
            total = total + swap(send, j).astype(jnp.float32)
        total = total + jnp.stack([skip[s] for s in steps]).astype(jnp.float32)
        piece = total.astype(jnp.bfloat16)
        got = [[piece] + [shift(piece, m) for m in range(1, n_ctx)]]
        bit = n_head // 2
        while bit:
            got = got + [[swap(x, bit) for x in row] for row in got]
            bit //= 2
        pieces += [x for j in range(n_head) for x in got[order.index(j)]]

    keep, send, mixed = experts(CHUNKS, pieces, shares, gain, w_gate, w_up, w_down, own_rows)

    both = keep.astype(jnp.float32) + swap(send, 1).astype(jnp.float32)
    across = swap(both[1].astype(jnp.bfloat16), 2)
    column = (both[0] + across.astype(jnp.float32)).astype(jnp.bfloat16)
    result = column[0].astype(jnp.float32)
    for t in range(1, n_ctx):
        result = result + shift(column[t], -t).astype(jnp.float32)
    return (mixed, result.astype(jnp.bfloat16))


def head_order(n_head):
    order = [0]
    bit = n_head // 2
    while bit:
        order = order + [j ^ bit for j in order]
        bit //= 2
    return order


def body(*args):
    residual, routes = args[3], args[6]
    own_rows, dim = residual.shape
    n_ctx, n_head = lax.axis_size("ctx"), lax.axis_size("head")
    dense = slots_per_expert(own_rows, routes.shape[1], n_ctx * n_head) == own_rows
    dense = dense and n_ctx == 4 and n_head == 4 and (dim // n_ctx) % 128 == 0
    return (dense_body if dense else sparse_body)(*args)


def solution(mesh):
    return jax.shard_map(
        body,
        mesh=mesh,
        in_specs=(
            P(("group", "ctx"), "head"),
            P(("group", "ctx"), "head"),
            P(("group", "ctx"), "head"),
            P(("group", "ctx", "head"), None),
            P("head", "ctx"),
            P(),
            P(("group", "ctx", "head"), None),
            P(("group", "ctx", "head"), None),
            P(("ctx", "head"), None, None),
            P(("ctx", "head"), None, None),
            P(("ctx", "head"), None, None),
        ),
        out_specs=(P(("group", "ctx", "head"), None), P(("group", "ctx", "head"), None)),
        check_vma=False,
    )
```

time: 256 us -> 139 us (0.54)
  the two profiles are of different devices: /device:TPU:11 before, /device:TPU:0 now
where the time goes in v1:
time: 139 us; the launch traced here: 138 us
  waiting for transfers between devices  76.7 us (55%)
  starting transfers between devices  26.5 us (19%)
  Pallas kernels  23.7 us (17%)
  other arithmetic  5.59 us (4%)
  local copies, waits for them, and re-layouts  4.83 us (3%)
    ppermute x18, waiting for transfers between devices, shift(): return lax.ppermute(x, 'ctx', [(i, (i + by) % n) for i in range(n)])  45.1 us
    ppermute x20, waiting for transfers between devices, swap(): return lax.ppermute(x, 'head', [(i, i ^ mask) for i in range(n)])  31.6 us
    ppermute x18, starting transfers between devices, shift(): return lax.ppermute(x, 'ctx', [(i, (i + by) % n) for i in range(n)])  17.6 us
    pallas_call x1, Pallas kernels, attend(): pl.pallas_call(functools.partial(attend_kernel, steps, n_ctx, n_head), ou...  11.8 us
    pallas_call x1, Pallas kernels, experts(): pl.pallas_call(functools.partial(expert_kernel, chunks, n_ctx, n_head), g...  11.8 us
    ppermute x20, starting transfers between devices, swap(): return lax.ppermute(x, 'head', [(i, i ^ mask) for i in range(n)])  8.94 us
  transfers between devices with their start and end apart: 38, of which 18 were waited for; matrix products, arithmetic and copies ran while one was open for 4% of the time, Pallas kernels for 9%

profile of v1, /device:TPU:0, one launch (start us, length us, event | category | flops | bytes accessed | tf_op | source)
XLA Modules:
  0.0 138.4 jit_solution(13353830057934939195)
XLA Ops:
  0.6 3.1 %collective-permute-start = (bf16[128,1024]{1,0:T(8,128)(2,1)}, bf16[128,1024]{1,0:T(8,128)(2,1)S(1)}, u32[]{:S(2)}, u32[]{:S(2)}) collective-permute-start(bf16[128,1024]{1,0:T(8,128)(2,1)} %refs_0_.1), channel_id=1, source_target_pairs={{0,4},{4,8},{8,12},{12,0},{1,5},{5,9},{9,13},{13,1},{2,6},{6,10},{... | collective-permute-start | bytes 786440 | tf_op jit(solution)/shard_map/ppermute | solution.py:117
  3.7 8.5 %collective-permute-done.refs_1_ = bf16[128,1024]{1,0:T(8,128)(2,1)S(1)} collective-permute-done((bf16[128,1024]{1,0:T(8,128)(2,1)}, bf16[128,1024]{1,0:T(8,128)(2,1)S(1)}, u32[]{:S(2)}, u32[]{:S(2)}) %collective-permute-start) | collective-permute-done | bytes 262176 | tf_op jit(solution)/shard_map/ppermute | solution.py:117
  13.8 1.3 collective-permute-start.3
  15.9 6.4 %collective-permute-done.1.refs_2_ = bf16[128,1024]{1,0:T(8,128)(2,1)S(1)} collective-permute-done((bf16[128,1024]{1,0:T(8,128)(2,1)S(1)}, bf16[128,1024]{1,0:T(8,128)(2,1)S(1)}, u32[]{:S(2)}, u32[]{:S(2)}) %collective-permute-start.1) | collective-permute-done | bytes 262176 | tf_op jit(solution)/shard_map/ppermute | solution.py:117
  23.8 3.8 %collective-permute-start.29 = (f32[32,16]{1,0:T(8,128)S(1)}, f32[32,16]{1,0:T(8,128)S(1)}, u32[]{:S(2)}, u32[]{:S(2)}) collective-permute-start(f32[32,16]{1,0:T(8,128)S(1)} %copy.23), channel_id=1, source_target_pairs={{0,12},{4,0},{8,4},{12,8},{1,13},{5,1},{9,5},{13,9},{2,14},{6,2},{... | collective-permute-start | bytes 6152 | tf_op jit(solution)/shard_map/ppermute | solution.py:117
  28.2 2.0 %collective-permute-start.27 = (f32[32,16]{1,0:T(8,128)S(1)}, f32[32,16]{1,0:T(8,128)S(1)}, u32[]{:S(2)}, u32[]{:S(2)}) collective-permute-start(f32[32,16]{1,0:T(8,128)S(1)} %copy.23), channel_id=1, source_target_pairs={{0,4},{4,8},{8,12},{12,0},{1,5},{5,9},{9,13},{13,1},{2,6},{6,10},{... | collective-permute-start | bytes 6152 | tf_op jit(solution)/shard_map/ppermute | solution.py:117
  30.2 1.0 reshape.17
  32.5 5.5 %collective-permute-done.5.refs_7_ = bf16[128,256]{1,0:T(8,128)(2,1)S(1)} collective-permute-done((bf16[128,256]{1,0:T(8,128)(2,1)S(1)}, bf16[128,256]{1,0:T(8,128)(2,1)S(1)}, u32[]{:S(2)}, u32[]{:S(2)}) %collective-permute-start.5) | collective-permute-done | bytes 65568 | tf_op jit(solution)/shard_map/ppermute | solution.py:117
  39.3 11.8 %attend.1 = (f32[4,32,512]{2,1,0:T(8,128)}, bf16[4,32,512]{2,1,0:T(8,128)(2,1)}, bf16[4,32,512]{2,1,0:T(8,128)(2,1)}, bf16[4,32,512]{2,1,0:T(8,128)(2,1)}) custom-call(bf16[128,1024]{1,0:T(8,128)(2,1)} %refs_0_.1, bf16[128,1024]{1,0:T(8,128)(2,1)} %copy-done.3, bf16[128,1024]{1,0:T(8,128)(2,1)} %copy-done.4, bf16[128,1024]{1,0:T(8,128)(2,1)} %copy-done.5, ...), custom_call_target="tpu_custom_call" | custom-call | flops 1610612736 | bytes 1048576 | tf_op jit(solution)/shard_map/attend/pallas_call | solution.py:181
  51.2 1.1 collective-permute-start.7
  53.1 1.1 collective-permute-start.31
  54.2 7.3 %collective-permute-done.31.refs_18_ = f32[4,32,16]{2,1,0:T(8,128)S(1)} collective-permute-done((f32[4,32,16]{2,1,0:T(8,128)S(1)}, f32[4,32,16]{2,1,0:T(8,128)S(1)}, u32[]{:S(2)}, u32[]{:S(2)}) %collective-permute-start.31) | collective-permute-done | bytes 8224 | tf_op jit(solution)/shard_map/ppermute | solution.py:122
  61.5 1.5 %collective-permute-start.9 = (bf16[32,512]{1,0:T(8,128)(2,1)S(1)}, bf16[32,512]{1,0:T(8,128)(2,1)S(1)}, u32[]{:S(2)}, u32[]{:S(2)}) collective-permute-start(bf16[32,512]{1,0:T(8,128)(2,1)S(1)} %bitcast.46), channel_id=1, source_target_pairs={{0,4},{4,8},{8,12},{12,0},{1,5},{5,9},{9,13},{13,1},{2,6},{6,10},{... | collective-permute-start | bytes 98312 | tf_op jit(solution)/shard_map/ppermute | solution.py:117
  63.0 4.2 %collective-permute-done.9 = bf16[32,512]{1,0:T(8,128)(2,1)S(1)} collective-permute-done((bf16[32,512]{1,0:T(8,128)(2,1)S(1)}, bf16[32,512]{1,0:T(8,128)(2,1)S(1)}, u32[]{:S(2)}, u32[]{:S(2)}) %collective-permute-start.9) | collective-permute-done | bytes 32800 | tf_op jit(solution)/shard_map/ppermute | solution.py:117
  68.0 1.0 add_convert_fusion.refs_0_
  69.0 1.1 collective-permute-start.19
  70.1 2.2 %collective-permute-start.14 = (bf16[4,32,512]{2,1,0:T(8,128)(2,1)S(1)}, bf16[4,32,512]{2,1,0:T(8,128)(2,1)S(1)}, u32[]{:S(2)}, u32[]{:S(2)}) collective-permute-start(bf16[4,32,512]{2,1,0:T(8,128)(2,1)S(1)} %add_convert_fusion.refs_0_), channel_id=1, source_target_pairs={{0,12},{4,0},{8,4},{12,8},{1,13},{5,1},{9,5},{13,9},{2,14},{6,2},{... | collective-permute-start | bytes 393224 | tf_op jit(solution)/shard_map/ppermute | solution.py:117
  73.2 1.8 %collective-permute-done.19.refs_8_ = bf16[4,32,512]{2,1,0:T(8,128)(2,1)S(1)} collective-permute-done((bf16[4,32,512]{2,1,0:T(8,128)(2,1)S(1)}, bf16[4,32,512]{2,1,0:T(8,128)(2,1)S(1)}, u32[]{:S(2)}, u32[]{:S(2)}) %collective-permute-start.19) | collective-permute-done | bytes 131104 | tf_op jit(solution)/shard_map/ppermute | solution.py:122
  75.0 1.3 collective-permute-done.14.refs_3_
  77.3 7.2 %collective-permute-done.13.refs_2_ = bf16[4,32,512]{2,1,0:T(8,128)(2,1)S(1)} collective-permute-done((bf16[4,32,512]{2,1,0:T(8,128)(2,1)S(1)}, bf16[4,32,512]{2,1,0:T(8,128)(2,1)S(1)}, u32[]{:S(2)}, u32[]{:S(2)}) %collective-permute-start.13) | collective-permute-done | bytes 131104 | tf_op jit(solution)/shard_map/ppermute | solution.py:117
  85.5 1.1 collective-permute-start.20
  87.1 3.7 %collective-permute-done.21.refs_10_ = bf16[4,32,512]{2,1,0:T(8,128)(2,1)S(1)} collective-permute-done((bf16[4,32,512]{2,1,0:T(8,128)(2,1)S(1)}, bf16[4,32,512]{2,1,0:T(8,128)(2,1)S(1)}, u32[]{:S(2)}, u32[]{:S(2)}) %collective-permute-start.21) | collective-permute-done | bytes 131104 | tf_op jit(solution)/shard_map/ppermute | solution.py:122
  90.9 1.7 %collective-permute-done.20.refs_9_ = bf16[4,32,512]{2,1,0:T(8,128)(2,1)S(1)} collective-permute-done((bf16[4,32,512]{2,1,0:T(8,128)(2,1)S(1)}, bf16[4,32,512]{2,1,0:T(8,128)(2,1)S(1)}, u32[]{:S(2)}, u32[]{:S(2)}) %collective-permute-start.20) | collective-permute-done | bytes 131104 | tf_op jit(solution)/shard_map/ppermute | solution.py:122
  92.6 1.3 collective-permute-done.24.refs_13_
  94.6 11.8 %experts.1 = (bf16[2,4,32,2048]{3,2,1,0:T(8,128)(2,1)}, bf16[2,4,32,2048]{3,2,1,0:T(8,128)(2,1)}, bf16[32,2048]{1,0:T(8,128)(2,1)}) custom-call(bf16[4,32,512]{2,1,0:T(8,128)(2,1)} %copy-done, bf16[4,32,512]{2,1,0:T(8,128)(2,1)} %copy-done.10, bf16[4,32,512]{2,1,0:T(8,128)(2,1)} %copy-done.9, bf16[4,32,512]{2,1,0:T(8,128)(2,1)} %copy-done.7, ...), custom_call_target="tpu_custom_call" | custom-call | flops 4831838208 | bytes 9437184 | tf_op jit(solution)/shard_map/experts/pallas_call | solution.py:276
  106.6 2.7 %collective-permute-done.33 = bf16[2,4,32,2048]{3,2,1,0:T(8,128)(2,1)S(1)} collective-permute-done((bf16[2,4,32,2048]{3,2,1,0:T(8,128)(2,1)}, bf16[2,4,32,2048]{3,2,1,0:T(8,128)(2,1)S(1)}, u32[]{:S(2)}, u32[]{:S(2)}) %collective-permute-start.33) | collective-permute-done | bytes 1048608 | tf_op jit(solution)/shard_map/ppermute | solution.py:122
  109.3 1.6 %convert_add_fusion = f32[2,4,32,2048]{3,2,1,0:T(8,128)S(1)} fusion(bf16[2,4,32,2048]{3,2,1,0:T(8,128)(2,1)S(1)} %collective-permute-done.33, bf16[2,4,32,2048]{3,2,1,0:T(8,128)(2,1)} %get-tuple-element.14), kind=kLoop, calls=%fused_computation | loop fusion | flops 1572864 | bytes 4194304 | tf_op jit(solution)/shard_map/add | solution.py:346
  111.0 1.0 collective-permute-start.34
  112.0 13.0 %collective-permute-done.34 = bf16[4,32,2048]{2,1,0:T(8,128)(2,1)S(1)} collective-permute-done((bf16[4,32,2048]{2,1,0:T(8,128)(2,1)S(1)}, bf16[4,32,2048]{2,1,0:T(8,128)(2,1)S(1)}, u32[]{:S(2)}, u32[]{:S(2)}) %collective-permute-start.34) | collective-permute-done | bytes 524320 | tf_op jit(solution)/shard_map/ppermute | solution.py:122
  125.2 2.0 %collective-permute-start.37 = (bf16[32,2048]{1,0:T(8,128)(2,1)S(1)}, bf16[32,2048]{1,0:T(8,128)(2,1)S(1)}, u32[]{:S(2)}, u32[]{:S(2)}) collective-permute-start(bf16[32,2048]{1,0:T(8,128)(2,1)S(1)} %get-tuple-element.17), channel_id=1, source_target_pairs={{0,4},{4,8},{8,12},{12,0},{1,5},{5,9},{9,13},{13,1},{2,6},{6,10},{... | collective-permute-start | bytes 393224 | tf_op jit(solution)/shard_map/ppermute | solution.py:117
  127.3 5.3 %collective-permute-done.35 = bf16[32,2048]{1,0:T(8,128)(2,1)S(1)} collective-permute-done((bf16[32,2048]{1,0:T(8,128)(2,1)S(1)}, bf16[32,2048]{1,0:T(8,128)(2,1)S(1)}, u32[]{:S(2)}, u32[]{:S(2)}) %collective-permute-start.35) | collective-permute-done | bytes 131104 | tf_op jit(solution)/shard_map/ppermute | solution.py:117
  133.5 4.1 %collective-permute-done.36 = bf16[32,2048]{1,0:T(8,128)(2,1)S(1)} collective-permute-done((bf16[32,2048]{1,0:T(8,128)(2,1)S(1)}, bf16[32,2048]{1,0:T(8,128)(2,1)S(1)}, u32[]{:S(2)}, u32[]{:S(2)}) %collective-permute-start.36) | collective-permute-done | bytes 131104 | tf_op jit(solution)/shard_map/ppermute | solution.py:117
  (119 shorter events, 14.5 us)
Async XLA Ops:
  0.6 11.6 %collective-permute-start = (bf16[128,1024]{1,0:T(8,128)(2,1)}, bf16[128,1024]{1,0:T(8,128)(2,1)S(1)}, u32[]{:S(2)}, u32[]{:S(2)}) collective-permute-start(bf16[128,1024]{1,0:T(8,128)(2,1)} %refs_0_.1), channel_id=1, source_target_pairs={{0,4},{4,8},{8,12},{12,0},{1,5},{5,9},{9,13},{13,1},{2,6},{6,10},{... | collective-permute-start | bytes 786440 | tf_op jit(solution)/shard_map/ppermute | solution.py:117
  12.3 10.0 %collective-permute-start.1 = (bf16[128,1024]{1,0:T(8,128)(2,1)S(1)}, bf16[128,1024]{1,0:T(8,128)(2,1)S(1)}, u32[]{:S(2)}, u32[]{:S(2)}) collective-permute-start(bf16[128,1024]{1,0:T(8,128)(2,1)S(1)} %collective-permute-done.refs_1_), channel_id=1, source_target_pairs={{0,4},{4,8},{8,12},{12,0},{1,5},{5,9},{9,13},{13,1},{2,6},{6,10},{... | collective-permute-start | bytes 786440 | tf_op jit(solution)/shard_map/ppermute | solution.py:117
  13.8 9.1 %collective-permute-start.3 = (bf16[128,256]{1,0:T(8,128)(2,1)S(1)}, bf16[128,256]{1,0:T(8,128)(2,1)S(1)}, u32[]{:S(2)}, u32[]{:S(2)}) collective-permute-start(bf16[128,256]{1,0:T(8,128)(2,1)S(1)} %constant_dynamic-update-slice_fusion.refs_4_), channel_id=1, source_target_pairs={{0,4},{4,8},{8,12},{12,0},{1,5},{5,9},{9,13},{13,1},{2,6},{6,10},{... | collective-permute-start | bytes 196616 | tf_op jit(solution)/shard_map/ppermute | solution.py:117
  22.3 15.8 %collective-permute-start.2 = (bf16[128,1024]{1,0:T(8,128)(2,1)S(1)}, bf16[128,1024]{1,0:T(8,128)(2,1)S(1)}, u32[]{:S(2)}, u32[]{:S(2)}) collective-permute-start(bf16[128,1024]{1,0:T(8,128)(2,1)S(1)} %collective-permute-done.1.refs_2_), channel_id=1, source_target_pairs={{0,4},{4,8},{8,12},{12,0},{1,5},{5,9},{9,13},{13,1},{2,6},{6,10},{... | collective-permute-start | bytes 786440 | tf_op jit(solution)/shard_map/ppermute | solution.py:117
  23.0 9.0 %collective-permute-start.4 = (bf16[128,256]{1,0:T(8,128)(2,1)S(1)}, bf16[128,256]{1,0:T(8,128)(2,1)S(1)}, u32[]{:S(2)}, u32[]{:S(2)}) collective-permute-start(bf16[128,256]{1,0:T(8,128)(2,1)S(1)} %collective-permute-done.3.refs_5_), channel_id=1, source_target_pairs={{0,4},{4,8},{8,12},{12,0},{1,5},{5,9},{9,13},{13,1},{2,6},{6,10},{... | collective-permute-start | bytes 196616 | tf_op jit(solution)/shard_map/ppermute | solution.py:117
  23.8 27.4 %collective-permute-start.29 = (f32[32,16]{1,0:T(8,128)S(1)}, f32[32,16]{1,0:T(8,128)S(1)}, u32[]{:S(2)}, u32[]{:S(2)}) collective-permute-start(f32[32,16]{1,0:T(8,128)S(1)} %copy.23), channel_id=1, source_target_pairs={{0,12},{4,0},{8,4},{12,8},{1,13},{5,1},{9,5},{13,9},{2,14},{6,2},{... | collective-permute-start | bytes 6152 | tf_op jit(solution)/shard_map/ppermute | solution.py:117
  27.6 24.7 %collective-permute-start.28 = (f32[32,16]{1,0:T(8,128)S(1)}, f32[32,16]{1,0:T(8,128)S(1)}, u32[]{:S(2)}, u32[]{:S(2)}) collective-permute-start(f32[32,16]{1,0:T(8,128)S(1)} %copy.23), channel_id=1, source_target_pairs={{0,8},{4,12},{8,0},{12,4},{1,9},{5,13},{9,1},{13,5},{2,10},{6,14},... | collective-permute-start | bytes 6152 | tf_op jit(solution)/shard_map/ppermute | solution.py:117
  28.2 24.9 %collective-permute-start.27 = (f32[32,16]{1,0:T(8,128)S(1)}, f32[32,16]{1,0:T(8,128)S(1)}, u32[]{:S(2)}, u32[]{:S(2)}) collective-permute-start(f32[32,16]{1,0:T(8,128)S(1)} %copy.23), channel_id=1, source_target_pairs={{0,4},{4,8},{8,12},{12,0},{1,5},{5,9},{9,13},{13,1},{2,6},{6,10},{... | collective-permute-start | bytes 6152 | tf_op jit(solution)/shard_map/ppermute | solution.py:117
  31.9 6.1 %collective-permute-start.5 = (bf16[128,256]{1,0:T(8,128)(2,1)S(1)}, bf16[128,256]{1,0:T(8,128)(2,1)S(1)}, u32[]{:S(2)}, u32[]{:S(2)}) collective-permute-start(bf16[128,256]{1,0:T(8,128)(2,1)S(1)} %collective-permute-done.4.refs_6_), channel_id=1, source_target_pairs={{0,4},{4,8},{8,12},{12,0},{1,5},{5,9},{9,13},{13,1},{2,6},{6,10},{... | collective-permute-start | bytes 196616 | tf_op jit(solution)/shard_map/ppermute | solution.py:117
  38.0 25.0 %collective-permute-start.11 = (bf16[32,512]{1,0:T(8,128)(2,1)S(1)}, bf16[32,512]{1,0:T(8,128)(2,1)S(1)}, u32[]{:S(2)}, u32[]{:S(2)}) collective-permute-start(bf16[32,512]{1,0:T(8,128)(2,1)S(1)} %bitcast.42), channel_id=1, source_target_pairs={{0,12},{4,0},{8,4},{12,8},{1,13},{5,1},{9,5},{13,9},{2,14},{6,2},{... | collective-permute-start | bytes 98312 | tf_op jit(solution)/shard_map/ppermute | solution.py:117
  51.2 16.8 %collective-permute-start.6 = (bf16[4,32,512]{2,1,0:T(8,128)(2,1)}, bf16[4,32,512]{2,1,0:T(8,128)(2,1)S(1)}, u32[]{:S(2)}, u32[]{:S(2)}) collective-permute-start(bf16[4,32,512]{2,1,0:T(8,128)(2,1)} %get-tuple-element.10), channel_id=1, source_target_pairs={{0,1},{1,0},{2,3},{3,2},{4,5},{5,4},{6,7},{7,6},{8,9},{9,8},{10,11... | collective-permute-start | bytes 393224 | tf_op jit(solution)/shard_map/ppermute | solution.py:122
  51.2 16.8 %collective-permute-start.7 = (bf16[4,32,512]{2,1,0:T(8,128)(2,1)}, bf16[4,32,512]{2,1,0:T(8,128)(2,1)S(1)}, u32[]{:S(2)}, u32[]{:S(2)}) collective-permute-start(bf16[4,32,512]{2,1,0:T(8,128)(2,1)} %get-tuple-element.11), channel_id=1, source_target_pairs={{0,2},{1,3},{2,0},{3,1},{4,6},{5,7},{6,4},{7,5},{8,10},{9,11},{10,... | collective-permute-start | bytes 393224 | tf_op jit(solution)/shard_map/ppermute | solution.py:122
  52.3 15.6 %collective-permute-start.8 = (bf16[4,32,512]{2,1,0:T(8,128)(2,1)}, bf16[4,32,512]{2,1,0:T(8,128)(2,1)S(1)}, u32[]{:S(2)}, u32[]{:S(2)}) collective-permute-start(bf16[4,32,512]{2,1,0:T(8,128)(2,1)} %get-tuple-element.12), channel_id=1, source_target_pairs={{0,3},{1,2},{2,1},{3,0},{4,7},{5,6},{6,5},{7,4},{8,11},{9,10},{10,... | collective-permute-start | bytes 393224 | tf_op jit(solution)/shard_map/ppermute | solution.py:122
  53.1 8.4 %collective-permute-start.31 = (f32[4,32,16]{2,1,0:T(8,128)S(1)}, f32[4,32,16]{2,1,0:T(8,128)S(1)}, u32[]{:S(2)}, u32[]{:S(2)}) collective-permute-start(f32[4,32,16]{2,1,0:T(8,128)S(1)} %pad_maximum_fusion.refs_16_), channel_id=1, source_target_pairs={{0,2},{1,3},{2,0},{3,1},{4,6},{5,7},{6,4},{7,5},{8,10},{9,11},{10,... | collective-permute-start | bytes 24584 | tf_op jit(solution)/shard_map/ppermute | solution.py:122
  61.5 5.7 %collective-permute-start.9 = (bf16[32,512]{1,0:T(8,128)(2,1)S(1)}, bf16[32,512]{1,0:T(8,128)(2,1)S(1)}, u32[]{:S(2)}, u32[]{:S(2)}) collective-permute-start(bf16[32,512]{1,0:T(8,128)(2,1)S(1)} %bitcast.46), channel_id=1, source_target_pairs={{0,4},{4,8},{8,12},{12,0},{1,5},{5,9},{9,13},{13,1},{2,6},{6,10},{... | collective-permute-start | bytes 98312 | tf_op jit(solution)/shard_map/ppermute | solution.py:117
  67.2 5.1 %collective-permute-start.30 = (f32[4,32,16]{2,1,0:T(8,128)S(1)}, f32[4,32,16]{2,1,0:T(8,128)S(1)}, u32[]{:S(2)}, u32[]{:S(2)}) collective-permute-start(f32[4,32,16]{2,1,0:T(8,128)S(1)} %pad_maximum_fusion.refs_16_), channel_id=1, source_target_pairs={{0,1},{1,0},{2,3},{3,2},{4,5},{5,4},{6,7},{7,6},{8,9},{9,8},{10,11... | collective-permute-start | bytes 24584 | tf_op jit(solution)/shard_map/ppermute | solution.py:122
  69.0 6.0 %collective-permute-start.19 = (bf16[4,32,512]{2,1,0:T(8,128)(2,1)S(1)}, bf16[4,32,512]{2,1,0:T(8,128)(2,1)S(1)}, u32[]{:S(2)}, u32[]{:S(2)}) collective-permute-start(bf16[4,32,512]{2,1,0:T(8,128)(2,1)S(1)} %add_convert_fusion.refs_0_), channel_id=1, source_target_pairs={{0,2},{1,3},{2,0},{3,1},{4,6},{5,7},{6,4},{7,5},{8,10},{9,11},{10,... | collective-permute-start | bytes 393224 | tf_op jit(solution)/shard_map/ppermute | solution.py:122
  70.1 6.2 %collective-permute-start.14 = (bf16[4,32,512]{2,1,0:T(8,128)(2,1)S(1)}, bf16[4,32,512]{2,1,0:T(8,128)(2,1)S(1)}, u32[]{:S(2)}, u32[]{:S(2)}) collective-permute-start(bf16[4,32,512]{2,1,0:T(8,128)(2,1)S(1)} %add_convert_fusion.refs_0_), channel_id=1, source_target_pairs={{0,12},{4,0},{8,4},{12,8},{1,13},{5,1},{9,5},{13,9},{2,14},{6,2},{... | collective-permute-start | bytes 393224 | tf_op jit(solution)/shard_map/ppermute | solution.py:117
  72.4 12.1 %collective-permute-start.13 = (bf16[4,32,512]{2,1,0:T(8,128)(2,1)S(1)}, bf16[4,32,512]{2,1,0:T(8,128)(2,1)S(1)}, u32[]{:S(2)}, u32[]{:S(2)}) collective-permute-start(bf16[4,32,512]{2,1,0:T(8,128)(2,1)S(1)} %add_convert_fusion.refs_0_), channel_id=1, source_target_pairs={{0,8},{4,12},{8,0},{12,4},{1,9},{5,13},{9,1},{13,5},{2,10},{6,14},... | collective-permute-start | bytes 393224 | tf_op jit(solution)/shard_map/ppermute | solution.py:117
  72.5 13.0 %collective-permute-start.12 = (bf16[4,32,512]{2,1,0:T(8,128)(2,1)S(1)}, bf16[4,32,512]{2,1,0:T(8,128)(2,1)S(1)}, u32[]{:S(2)}, u32[]{:S(2)}) collective-permute-start(bf16[4,32,512]{2,1,0:T(8,128)(2,1)S(1)} %add_convert_fusion.refs_0_), channel_id=1, source_target_pairs={{0,4},{4,8},{8,12},{12,0},{1,5},{5,9},{9,13},{13,1},{2,6},{6,10},{... | collective-permute-start | bytes 393224 | tf_op jit(solution)/shard_map/ppermute | solution.py:117
  75.0 11.5 %collective-permute-start.23 = (bf16[4,32,512]{2,1,0:T(8,128)(2,1)S(1)}, bf16[4,32,512]{2,1,0:T(8,128)(2,1)S(1)}, u32[]{:S(2)}, u32[]{:S(2)}) collective-permute-start(bf16[4,32,512]{2,1,0:T(8,128)(2,1)S(1)} %collective-permute-done.19.refs_8_), channel_id=1, source_target_pairs={{0,1},{1,0},{2,3},{3,2},{4,5},{5,4},{6,7},{7,6},{8,9},{9,8},{10,11... | collective-permute-start | bytes 393224 | tf_op jit(solution)/shard_map/ppermute | solution.py:122
  76.3 10.2 %collective-permute-start.22 = (bf16[4,32,512]{2,1,0:T(8,128)(2,1)S(1)}, bf16[4,32,512]{2,1,0:T(8,128)(2,1)S(1)}, u32[]{:S(2)}, u32[]{:S(2)}) collective-permute-start(bf16[4,32,512]{2,1,0:T(8,128)(2,1)S(1)} %collective-permute-done.14.refs_3_), channel_id=1, source_target_pairs={{0,2},{1,3},{2,0},{3,1},{4,6},{5,7},{6,4},{7,5},{8,10},{9,11},{10,... | collective-permute-start | bytes 393224 | tf_op jit(solution)/shard_map/ppermute | solution.py:122
  77.3 9.8 %collective-permute-start.18 = (bf16[4,32,512]{2,1,0:T(8,128)(2,1)S(1)}, bf16[4,32,512]{2,1,0:T(8,128)(2,1)S(1)}, u32[]{:S(2)}, u32[]{:S(2)}) collective-permute-start(bf16[4,32,512]{2,1,0:T(8,128)(2,1)S(1)} %collective-permute-done.14.refs_3_), channel_id=1, source_target_pairs={{0,1},{1,0},{2,3},{3,2},{4,5},{5,4},{6,7},{7,6},{8,9},{9,8},{10,11... | collective-permute-start | bytes 393224 | tf_op jit(solution)/shard_map/ppermute | solution.py:122
  84.5 6.4 %collective-permute-start.21 = (bf16[4,32,512]{2,1,0:T(8,128)(2,1)S(1)}, bf16[4,32,512]{2,1,0:T(8,128)(2,1)S(1)}, u32[]{:S(2)}, u32[]{:S(2)}) collective-permute-start(bf16[4,32,512]{2,1,0:T(8,128)(2,1)S(1)} %collective-permute-done.13.refs_2_), channel_id=1, source_target_pairs={{0,2},{1,3},{2,0},{3,1},{4,6},{5,7},{6,4},{7,5},{8,10},{9,11},{10,... | collective-permute-start | bytes 393224 | tf_op jit(solution)/shard_map/ppermute | solution.py:122
  85.5 7.1 %collective-permute-start.20 = (bf16[4,32,512]{2,1,0:T(8,128)(2,1)S(1)}, bf16[4,32,512]{2,1,0:T(8,128)(2,1)S(1)}, u32[]{:S(2)}, u32[]{:S(2)}) collective-permute-start(bf16[4,32,512]{2,1,0:T(8,128)(2,1)S(1)} %collective-permute-done.12.refs_1_), channel_id=1, source_target_pairs={{0,2},{1,3},{2,0},{3,1},{4,6},{5,7},{6,4},{7,5},{8,10},{9,11},{10,... | collective-permute-start | bytes 393224 | tf_op jit(solution)/shard_map/ppermute | solution.py:122
  86.5 6.0 %collective-permute-start.17 = (bf16[4,32,512]{2,1,0:T(8,128)(2,1)S(1)}, bf16[4,32,512]{2,1,0:T(8,128)(2,1)S(1)}, u32[]{:S(2)}, u32[]{:S(2)}) collective-permute-start(bf16[4,32,512]{2,1,0:T(8,128)(2,1)S(1)} %collective-permute-done.13.refs_2_), channel_id=1, source_target_pairs={{0,1},{1,0},{2,3},{3,2},{4,5},{5,4},{6,7},{7,6},{8,9},{9,8},{10,11... | collective-permute-start | bytes 393224 | tf_op jit(solution)/shard_map/ppermute | solution.py:122
  86.6 6.0 %collective-permute-start.16 = (bf16[4,32,512]{2,1,0:T(8,128)(2,1)S(1)}, bf16[4,32,512]{2,1,0:T(8,128)(2,1)S(1)}, u32[]{:S(2)}, u32[]{:S(2)}) collective-permute-start(bf16[4,32,512]{2,1,0:T(8,128)(2,1)S(1)} %collective-permute-done.12.refs_1_), channel_id=1, source_target_pairs={{0,1},{1,0},{2,3},{3,2},{4,5},{5,4},{6,7},{7,6},{8,9},{9,8},{10,11... | collective-permute-start | bytes 393224 | tf_op jit(solution)/shard_map/ppermute | solution.py:122
  87.1 5.5 %collective-permute-start.26 = (bf16[4,32,512]{2,1,0:T(8,128)(2,1)S(1)}, bf16[4,32,512]{2,1,0:T(8,128)(2,1)S(1)}, u32[]{:S(2)}, u32[]{:S(2)}) collective-permute-start(bf16[4,32,512]{2,1,0:T(8,128)(2,1)S(1)} %collective-permute-done.22.refs_11_), channel_id=1, source_target_pairs={{0,1},{1,0},{2,3},{3,2},{4,5},{5,4},{6,7},{7,6},{8,9},{9,8},{10,11... | collective-permute-start | bytes 393224 | tf_op jit(solution)/shard_map/ppermute | solution.py:122
  111.0 14.0 %collective-permute-start.34 = (bf16[4,32,2048]{2,1,0:T(8,128)(2,1)S(1)}, bf16[4,32,2048]{2,1,0:T(8,128)(2,1)S(1)}, u32[]{:S(2)}, u32[]{:S(2)}) collective-permute-start(bf16[4,32,2048]{2,1,0:T(8,128)(2,1)S(1)} %fusion.2), channel_id=1, source_target_pairs={{0,2},{1,3},{2,0},{3,1},{4,6},{5,7},{6,4},{7,5},{8,10},{9,11},{10,... | collective-permute-start | bytes 1572872 | tf_op jit(solution)/shard_map/ppermute | solution.py:122
  125.2 7.4 %collective-permute-start.35 = (bf16[32,2048]{1,0:T(8,128)(2,1)S(1)}, bf16[32,2048]{1,0:T(8,128)(2,1)S(1)}, u32[]{:S(2)}, u32[]{:S(2)}) collective-permute-start(bf16[32,2048]{1,0:T(8,128)(2,1)S(1)} %get-tuple-element.16), channel_id=1, source_target_pairs={{0,12},{4,0},{8,4},{12,8},{1,13},{5,1},{9,5},{13,9},{2,14},{6,2},{... | collective-permute-start | bytes 393224 | tf_op jit(solution)/shard_map/ppermute | solution.py:117
  125.2 8.3 %collective-permute-start.37 = (bf16[32,2048]{1,0:T(8,128)(2,1)S(1)}, bf16[32,2048]{1,0:T(8,128)(2,1)S(1)}, u32[]{:S(2)}, u32[]{:S(2)}) collective-permute-start(bf16[32,2048]{1,0:T(8,128)(2,1)S(1)} %get-tuple-element.17), channel_id=1, source_target_pairs={{0,4},{4,8},{8,12},{12,0},{1,5},{5,9},{9,13},{13,1},{2,6},{6,10},{... | collective-permute-start | bytes 393224 | tf_op jit(solution)/shard_map/ppermute | solution.py:117
  127.3 10.4 %collective-permute-start.36 = (bf16[32,2048]{1,0:T(8,128)(2,1)S(1)}, bf16[32,2048]{1,0:T(8,128)(2,1)S(1)}, u32[]{:S(2)}, u32[]{:S(2)}) collective-permute-start(bf16[32,2048]{1,0:T(8,128)(2,1)S(1)} %get-tuple-element.18), channel_id=1, source_target_pairs={{0,8},{4,12},{8,0},{12,4},{1,9},{5,13},{9,1},{13,5},{2,10},{6,14},... | collective-permute-start | bytes 393224 | tf_op jit(solution)/shard_map/ppermute | solution.py:117
  (33 other events, 354.2 us)

commit v2 on v0

v2 whole, which is shorter than its diff:
```python
import functools

import jax
import jax.numpy as jnp
from jax import lax
from jax.experimental import pallas as pl
from jax.experimental.pallas import tpu as pltpu
from jax.sharding import PartitionSpec as P


HEAD_DIMENSION = 128
LANES = 64


def expert_apply(arrived, gate_proj, up_proj, down_proj):
    shape_in = arrived.shape
    flat_rows = arrived.reshape(-1, shape_in[-1])
    gate_act = jnp.dot(flat_rows, gate_proj, preferred_element_type=jnp.float32)
    up_act = jnp.dot(flat_rows, up_proj, preferred_element_type=jnp.float32)
    hidden = (jax.nn.silu(gate_act) * up_act).astype(jnp.bfloat16)
    output = jnp.dot(hidden, down_proj, preferred_element_type=jnp.float32).astype(jnp.bfloat16)
    return output.reshape(shape_in)


def sparse_body(query, keys, values, residual, o_weight, gain, routes, gates, w_gate, w_up, w_down):
    head_size = HEAD_DIMENSION
    query_rows = query.shape[0]
    kv_heads = keys.shape[1] // head_size
    q_heads = query.shape[1] // head_size
    head_replicas = q_heads // kv_heads
    scale = head_size ** (-0.5)
    queries = query.reshape(query_rows, kv_heads, head_replicas, head_size)
    first_pos = lax.axis_index("ctx") * query_rows
    query_pos = first_pos + jnp.arange(query_rows, dtype=jnp.int32)
    key_all = lax.all_gather(keys, "ctx", axis=0, tiled=True)
    value_all = lax.all_gather(values, "ctx", axis=0, tiled=True)
    width = key_all.shape[0]
    visible = jnp.arange(width, dtype=jnp.int32)[None, :] <= query_pos[:, None]
    scores = (
        jnp.einsum(
            "veqi,zei->eqvz",
            queries,
            key_all.reshape(width, kv_heads, head_size),
            preferred_element_type=jnp.float32,
        )
        * scale
    )
    scores = jnp.where(visible, scores, -1e30)
    top = jnp.max(scores, axis=-1)
    weights = jnp.where(visible, jnp.exp(scores - top[..., None]), 0.0)
    total = jnp.sum(weights, axis=-1)
    summed_values = jnp.einsum(
        "pexa,apo->pexo",
        weights.astype(jnp.bfloat16),
        value_all.reshape(width, kv_heads, head_size),
        preferred_element_type=jnp.float32,
    )
    attended = (
        (summed_values / total[..., None])
        .transpose(2, 0, 1, 3)
        .reshape(query_rows, q_heads * head_size)
        .astype(jnp.bfloat16)
    )
    head_terms = jnp.dot(
        attended,
        lax.all_gather(o_weight, "ctx", axis=1, tiled=True),
        preferred_element_type=jnp.float32,
    )
    summed = lax.psum_scatter(
        head_terms.astype(jnp.bfloat16), "head", scatter_dimension=0, tiled=True
    ).astype(jnp.float32)
    mixed = (summed + residual.astype(jnp.float32)).astype(jnp.bfloat16)
    mixed_f = mixed.astype(jnp.float32)
    normed = (
        mixed_f * lax.rsqrt(jnp.mean(mixed_f * mixed_f, axis=-1, keepdims=True) + 1e-06) * gain
    ).astype(jnp.bfloat16)
    own_rows = residual.shape[0]
    model_dim = residual.shape[1]
    top_count = routes.shape[1]
    devices = lax.axis_size("ctx") * lax.axis_size("head")
    capacity = slots_per_expert(own_rows, top_count, devices)
    expert_ids = routes.reshape(-1)
    onehot = (expert_ids[:, None] == jnp.arange(devices, dtype=jnp.int32)[None, :]).astype(
        jnp.int32
    )
    slots = jnp.sum((jnp.cumsum(onehot, axis=0) - 1) * onehot, axis=1)
    target = expert_ids * capacity + slots
    outgoing = (
        jnp.zeros((devices * capacity, model_dim), jnp.bfloat16)
        .at[target]
        .set(jnp.repeat(normed, top_count, axis=0))
    )
    outgoing = outgoing.reshape(devices, capacity, model_dim)
    computed = expert_apply(
        lax.all_to_all(outgoing, ("ctx", "head"), split_axis=0, concat_axis=0, tiled=True),
        w_gate[0],
        w_up[0],
        w_down[0],
    )
    returned = lax.all_to_all(computed, ("ctx", "head"), split_axis=0, concat_axis=0, tiled=True)
    selected_entries = returned.reshape(devices * capacity, model_dim)[target]
    selected_entries = selected_entries.astype(jnp.float32).reshape(own_rows, top_count, model_dim)
    weight_norm = gates / jnp.sum(gates, axis=-1, keepdims=True)
    expert_mix = jnp.sum(selected_entries * weight_norm[..., None], axis=1).astype(jnp.bfloat16)
    return (mixed, expert_mix)


def slots_per_expert(own_rows, top_count, devices):
    return min(own_rows, max(2, 2 * own_rows * top_count // devices))


def place():
    return lax.axis_index("ctx"), lax.axis_index("head")


def ring_at(position):
    return position ^ (position >> 1)


def behind(steps):
    n = lax.axis_size("ctx")
    c = lax.axis_index("ctx")
    return ring_at(jnp.bitwise_and(ring_at(c) - steps + n, n - 1))


def shift(x, by):
    n = lax.axis_size("ctx")
    pairs = [(ring_at(i), ring_at((i + by) % n)) for i in range(n)]
    return lax.ppermute(x, "ctx", pairs)


def swap(x, mask):
    n = lax.axis_size("head")
    return lax.ppermute(x, "head", [(i, i ^ mask) for i in range(n)])


def call(kernel, args, out_shape, scratch, flops, moved, limit):
    vmem = pl.BlockSpec(memory_space=pltpu.VMEM)
    return pl.pallas_call(
        kernel,
        out_shape=out_shape,
        in_specs=[vmem] * len(args),
        out_specs=[vmem] * len(out_shape),
        scratch_shapes=scratch,
        cost_estimate=pl.CostEstimate(flops=flops, bytes_accessed=moved, transcendentals=0),
        compiler_params=pltpu.CompilerParams(vmem_limit_bytes=limit << 20),
    )(*args)


def prepare_kernel(n_ctx, k_ref, v_ref, skip_ref, route_ref, gate_ref, *out_refs):
    hd = HEAD_DIMENSION
    gates = gate_ref[...].T
    routes = route_ref[...].T
    share = gates / jnp.sum(gates, axis=-1, keepdims=True)
    own_rows, dim = skip_ref.shape
    lanes = lax.broadcasted_iota(jnp.int32, (own_rows, 2 * LANES), 1)
    table = jnp.zeros((own_rows, 2 * LANES), jnp.float32)
    for k in range(gates.shape[1]):
        table += jnp.where(lanes % LANES == routes[:, k : k + 1], share[:, k : k + 1], 0.0)
    high = table.astype(jnp.bfloat16).astype(jnp.float32)
    packed = jnp.where(lanes < LANES, high, table - high).astype(jnp.bfloat16)
    rows = k_ref.shape[0]
    width = 2 * hd
    for s, out_ref in enumerate(out_refs):
        out_ref[:rows, :hd] = k_ref[...]
        out_ref[:rows, hd:] = v_ref[...]
        first = behind(-s) * (dim // n_ctx)
        at = rows
        for i in range(dim // n_ctx // width):
            cols = pl.ds(pl.multiple_of(first + i * width, width), width)
            out_ref[at : at + own_rows, :] = skip_ref[:, cols]
            at += own_rows
        out_ref[at:, : 2 * LANES] = packed
        out_ref[at:, 2 * LANES :] = jnp.zeros((own_rows, width - 2 * LANES), jnp.bfloat16)


def prepare(keys, values, residual, routes, gates):
    n_ctx = lax.axis_size("ctx")
    own_rows, dim = residual.shape
    rows = keys.shape[0] + own_rows * (dim // n_ctx // (2 * HEAD_DIMENSION) + 1)
    part = jax.ShapeDtypeStruct((rows, 2 * HEAD_DIMENSION), jnp.bfloat16)
    args = (keys, values, residual, routes.T, gates.T)
    kernel = functools.partial(prepare_kernel, n_ctx)
    return call(kernel, args, [part] * n_ctx, [], 0, 1 << 18, 4)


def attend_kernel(steps, n_before, n_ctx, n_head, *refs):
    n = len(steps)
    q_refs, refs = refs[:n], refs[n:]
    part_refs, refs = refs[:n_ctx], refs[n_ctx:]
    w_ref, refs = refs[0], refs[1:]
    if n_before:
        before, refs = refs[:n_head], refs[n_head:]
    out_refs, (k_all, v_all, queries, att, prod) = refs[:n_head], refs[n_head:]
    hd = HEAD_DIMENSION
    rows, q_cols = q_refs[0].shape
    own_rows = rows // n_head
    heads = q_cols // hd
    together = 4
    _, h = place()
    key_pos = []
    for m in range(n_ctx):
        k_all[m * rows : (m + 1) * rows, :] = part_refs[m][:rows, :hd]
        v_all[m * rows : (m + 1) * rows, :] = part_refs[m][:rows, hd:]
        key_pos.append(behind(m) * rows + lax.broadcasted_iota(jnp.int32, (rows, rows), 1))
    key_pos = jnp.concatenate(key_pos, axis=1)
    row_pos = lax.broadcasted_iota(jnp.int32, (rows, 1), 0)
    scale = hd**-0.5
    for j in range(n_head if n_before else 0):
        out_refs[j][:n_before] = before[j][...]
    for i, step in enumerate(steps):
        visible = key_pos <= behind(step) * rows + row_pos
        for g in range(heads):
            queries[g * rows : (g + 1) * rows, :] = q_refs[i][:, g * hd : (g + 1) * hd]
        for g in range(0, heads, together):
            scores = lax.dot_general(
                queries[g * rows : (g + together) * rows, :],
                k_all[...],
                (((1,), (1,)), ((), ())),
                preferred_element_type=jnp.float32,
            ).reshape(together, rows, -1)
            scores = jnp.where(visible[None], scores, -1e30)
            top = jnp.max(scores, axis=-1, keepdims=True)
            weights = jnp.exp((scores - top) * scale)
            total = jnp.sum(weights, axis=-1, keepdims=True)
            summed = jnp.dot(
                weights.astype(jnp.bfloat16).reshape(together * rows, -1),
                v_all[...],
                preferred_element_type=jnp.float32,
            ).reshape(together, rows, hd)
            done = (summed * (1.0 / total)).astype(jnp.bfloat16)
            for k in range(together):
                att[:, (g + k) * hd : (g + k + 1) * hd] = done[k]
        prod[...] = jnp.dot(att[...], w_ref[...], preferred_element_type=jnp.float32)
        for j in range(n_head):
            start = pl.multiple_of(jnp.bitwise_xor(h, j) * own_rows, own_rows)
            block = prod[pl.ds(start, own_rows), :]
            out_refs[j][n_before + i] = block.astype(out_refs[j].dtype)


def attend(steps, q_list, parts, o_weight, before):
    n_ctx, n_head = lax.axis_size("ctx"), lax.axis_size("head")
    rows, q_cols = q_list[0].shape
    out_cols = o_weight.shape[1]
    n = len(steps)
    n_before = before[0].shape[0] if before else 0
    piece = (n_before + n, rows // n_head, out_cols)
    out_shape = [jax.ShapeDtypeStruct(piece, jnp.float32)]
    out_shape += [jax.ShapeDtypeStruct(piece, jnp.bfloat16)] * (n_head - 1)
    kernel = functools.partial(attend_kernel, steps, n_before, n_ctx, n_head)
    scratch = [
        pltpu.VMEM((rows * n_ctx, HEAD_DIMENSION), jnp.bfloat16),
        pltpu.VMEM((rows * n_ctx, HEAD_DIMENSION), jnp.bfloat16),
        pltpu.VMEM((rows * q_cols // HEAD_DIMENSION, HEAD_DIMENSION), jnp.bfloat16),
        pltpu.VMEM((rows, q_cols), jnp.bfloat16),
        pltpu.VMEM((rows, out_cols), jnp.float32),
    ]
    flops = n * (4 * rows * q_cols * rows * n_ctx + 2 * rows * q_cols * out_cols)
    args = (*q_list, *parts, o_weight, *before)
    return call(kernel, args, out_shape, scratch, flops, 2 * q_cols * out_cols, 16)


def combine_kernel(n_ctx, sizes, n_head, *refs):
    sums, refs = refs[: n_head * len(sizes)], refs[n_head * len(sizes) :]
    part_refs, (piece_ref, shared_ref) = refs[:n_ctx], refs[n_ctx:]
    own_rows, cols = piece_ref.shape[1:]
    width = part_refs[0].shape[1]
    base = part_refs[0].shape[0] - own_rows * (cols // width + 1)
    s = 0
    for k, size in enumerate(sizes):
        for i in range(size):
            total = sums[k * n_head][i]
            for j in range(1, n_head):
                total += sums[k * n_head + j][i].astype(jnp.float32)
            for b in range(cols // width):
                at = slice(b * width, (b + 1) * width)
                first = base + b * own_rows
                skip = part_refs[s][first : first + own_rows, :].astype(jnp.float32)
                block = (total[:, at] + skip).astype(jnp.bfloat16)
                piece_ref[s, :, at] = block
                shared_ref[s, :, at] = block
            shared_ref[s, :, cols:] = part_refs[s][base + cols // width * own_rows :, : 2 * LANES]
            s += 1


def combine(sums, parts, sizes):
    n_ctx, n_head = lax.axis_size("ctx"), lax.axis_size("head")
    _, own_rows, cols = sums[0].shape
    out_shape = [
        jax.ShapeDtypeStruct((n_ctx, own_rows, cols), jnp.bfloat16),
        jax.ShapeDtypeStruct((n_ctx, own_rows, cols + 2 * LANES), jnp.bfloat16),
    ]
    kernel = functools.partial(combine_kernel, n_ctx, sizes, n_head)
    return call(kernel, (*sums, *parts), out_shape, [], 0, 1 << 20, 4)


def expert_kernel(n_ctx, halves, *refs):
    pieces, refs = refs[:n_ctx], refs[n_ctx:]
    gain_ref, refs = refs[0], refs[1:]
    weights, refs = (refs[:3], refs[3:6]), refs[6:]
    outs, (x_ref, acc_ref, share_ref) = refs[:-3], refs[-3:]
    own_rows, cols = pieces[1].shape[1:]
    c, h = place()

    for t in range(n_ctx):
        blocks = []
        square = jnp.zeros((own_rows, 1), jnp.float32)
        for m in range(n_ctx):
            block = pieces[m][(t - m) % n_ctx, :, :cols]
            block_f = block.astype(jnp.float32)
            square += jnp.sum(block_f * block_f, axis=-1, keepdims=True)
            at = pl.ds(pl.multiple_of(behind(m) * cols, cols), cols)
            blocks.append((block_f, at))
            if halves is None and t == 0:
                outs[1][:, at] = block
        root = lax.rsqrt(square / (cols * n_ctx) + 1e-06)
        here = slice(t * own_rows, (t + 1) * own_rows)
        for block_f, at in blocks:
            x_ref[here, at] = (block_f * root * gain_ref[:, at]).astype(jnp.bfloat16)
        share_ref[here, :] = pieces[0][t, :, cols:].astype(jnp.float32)

    lanes = lax.broadcasted_iota(jnp.int32, share_ref.shape, 1) % LANES
    for i, (gate_ref, up_ref, down_ref) in enumerate(weights):
        expert = c * lax.axis_size("head") + jnp.bitwise_xor(h, i)
        share = jnp.sum(jnp.where(lanes == expert, share_ref[...], 0.0), axis=-1, keepdims=True)
        gate = jnp.dot(x_ref[...], gate_ref[0], preferred_element_type=jnp.float32)
        up = jnp.dot(x_ref[...], up_ref[0], preferred_element_type=jnp.float32)
        hidden = (gate * jax.nn.sigmoid(gate) * up).astype(jnp.bfloat16)
        out = jnp.dot(hidden, down_ref[0], preferred_element_type=jnp.float32) * share
        if i == 0:
            acc_ref[...] = out
        elif halves is None:
            outs[0][...] = (acc_ref[...] + out).reshape(outs[0].shape)
        else:
            total = (acc_ref[...] + out).astype(jnp.bfloat16)
            for out_ref, half in zip(outs, halves):
                for at, t in enumerate(half):
                    out_ref[at] = total[t * own_rows : (t + 1) * own_rows, :]


def experts(pieces, gain, weights, halves):
    n_ctx, own_rows, _ = pieces[0].shape
    _, dim, hidden = weights[0].shape
    rows = own_rows * n_ctx
    if halves is None:
        out_shape = [
            jax.ShapeDtypeStruct((n_ctx, own_rows, dim), jnp.float32),
            jax.ShapeDtypeStruct((own_rows, dim), jnp.bfloat16),
        ]
    else:
        out_shape = [
            jax.ShapeDtypeStruct((len(half), own_rows, dim), jnp.bfloat16) for half in halves
        ]
    scratch = [
        pltpu.VMEM((rows, dim), jnp.bfloat16),
        pltpu.VMEM((rows, dim), jnp.float32),
        pltpu.VMEM((rows, 2 * LANES), jnp.float32),
    ]
    args = (*pieces, gain.reshape(1, -1), *weights)
    kernel = functools.partial(expert_kernel, n_ctx, halves)
    flops = 12 * rows * dim * hidden
    return call(kernel, args, out_shape, scratch, flops, 12 * dim * hidden, 28)


def dense_body(query, keys, values, residual, o_weight, gain, routes, gates, w_gate, w_up, w_down):
    q_list = [query]
    for _ in range(3):
        q_list.append(shift(q_list[-1], 1))
    parts = prepare(keys, values, residual, routes, gates)
    parts = [parts[0]] + [shift(parts[s], s) for s in (1, 2, 3)]

    weights = [w_gate, w_up, w_down]
    weights += [swap(w, 1) for w in weights]

    first = attend((0, 1), q_list[:2], parts, o_weight, ())
    later = attend((2,), q_list[2:3], parts, o_weight, ())
    later = attend((3,), q_list[3:], parts, o_weight, later)
    sums = []
    for group in (first, later):
        sums.append(group[0])
        sums += [swap(group[j], j) for j in (1, 2, 3)]
    piece, shared = combine(sums, parts, (2, 2))
    pieces = [shared] + [shift(piece, m) for m in (1, 2, 3)]
    other_pieces = [swap(x, 2) for x in pieces]

    own_out, mixed = experts(pieces, gain, weights, None)
    halves = ((2, 1), (3, 0))
    other_out = experts(other_pieces, gain, weights, halves)

    result = 0.0
    for half, out in zip(halves, other_out):
        got = swap(out, 2)
        for at, t in enumerate(half):
            total = own_out[t] + got[at].astype(jnp.float32)
            if t:
                total = shift(total.astype(jnp.bfloat16), -t).astype(jnp.float32)
            result = result + total
    return (mixed, result.astype(jnp.bfloat16))


def body(*args):
    residual, routes = args[3], args[6]
    own_rows, dim = residual.shape
    n_ctx, n_head = lax.axis_size("ctx"), lax.axis_size("head")
    dense = slots_per_expert(own_rows, routes.shape[1], n_ctx * n_head) == own_rows
    dense = dense and n_ctx == 4 and n_head == 4 and (dim // n_ctx) % (2 * HEAD_DIMENSION) == 0
    dense = dense and args[1].shape[1] == HEAD_DIMENSION and n_ctx * n_head <= LANES
    if not dense:
        return sparse_body(*args)
    return dense_body(*args)


def solution(mesh):
    return jax.shard_map(
        body,
        mesh=mesh,
        in_specs=(
            P(("group", "ctx"), "head"),
            P(("group", "ctx"), "head"),
            P(("group", "ctx"), "head"),
            P(("group", "ctx", "head"), None),
            P("head", "ctx"),
            P(),
            P(("group", "ctx", "head"), None),
            P(("group", "ctx", "head"), None),
            P(("ctx", "head"), None, None),
            P(("ctx", "head"), None, None),
            P(("ctx", "head"), None, None),
        ),
        out_specs=(P(("group", "ctx", "head"), None), P(("group", "ctx", "head"), None)),
        check_vma=False,
    )
```

time: 256 us -> 114 us (0.45)
  the two profiles are of different devices: /device:TPU:11 before, /device:TPU:0 now
where the time goes in v2:
time: 114 us
  waiting for transfers between devices  54.6 us (48%)
  starting transfers between devices  36.1 us (32%)
  Pallas kernels  12.2 us (11%)
  local copies, waits for them, and re-layouts  9.09 us (8%)
    ppermute x12, waiting for transfers between devices, shift(): return lax.ppermute(x, 'ctx', pairs)  37.6 us
    ppermute x12, starting transfers between devices, shift(): return lax.ppermute(x, 'ctx', pairs)  23.6 us
    ppermute x15, waiting for transfers between devices, swap(): return lax.ppermute(x, 'head', [(i, i ^ mask) for i in range(n)])  16.9 us
    ppermute x15, starting transfers between devices, swap(): return lax.ppermute(x, 'head', [(i, i ^ mask) for i in range(n)])  12.5 us
    pallas_call x7, Pallas kernels, call(): pl.pallas_call(kernel, out_shape=out_shape, in_specs=[vmem] * len(args),...  12.2 us
    unnamed x24, local copies, waits for them, and re-layouts  9.09 us
  transfers between devices with their start and end apart: 27, of which 19 were waited for; matrix products, arithmetic and copies ran while one was open for 0% of the time, Pallas kernels for 8%

profile of v2, /device:TPU:0, one launch (start us, length us, event | category | flops | bytes accessed | tf_op | source)
XLA Modules:
  0.0 113.6 jit_solution(2674624595419205784)
XLA Ops:
  1.7 2.6 %collective-permute-start = (bf16[128,1024]{1,0:T(8,128)(2,1)}, bf16[128,1024]{1,0:T(8,128)(2,1)S(1)}, u32[]{:S(2)}, u32[]{:S(2)}) collective-permute-start(bf16[128,1024]{1,0:T(8,128)(2,1)} %refs_0_.1), channel_id=1, source_target_pairs={{0,4},{4,12},{12,8},{8,0},{1,5},{5,13},{13,9},{9,1},{2,6},{6,14},{... | collective-permute-start | bytes 786440 | tf_op jit(solution)/shard_map/ppermute | solution.py:129
  4.3 8.1 %collective-permute-done.refs_1_ = bf16[128,1024]{1,0:T(8,128)(2,1)S(1)} collective-permute-done((bf16[128,1024]{1,0:T(8,128)(2,1)}, bf16[128,1024]{1,0:T(8,128)(2,1)S(1)}, u32[]{:S(2)}, u32[]{:S(2)}) %collective-permute-start) | collective-permute-done | bytes 262176 | tf_op jit(solution)/shard_map/ppermute | solution.py:129
  17.6 3.3 %collective-permute-start.1 = (bf16[224,256]{1,0:T(8,128)(2,1)S(1)}, bf16[224,256]{1,0:T(8,128)(2,1)S(1)}, u32[]{:S(2)}, u32[]{:S(2)}) collective-permute-start(bf16[224,256]{1,0:T(8,128)(2,1)S(1)} %get-tuple-element.25), channel_id=1, source_target_pairs={{0,4},{4,12},{12,8},{8,0},{1,5},{5,13},{13,9},{9,1},{2,6},{6,14},{... | collective-permute-start | bytes 344072 | tf_op jit(solution)/shard_map/ppermute | solution.py:129
  20.9 3.0 %collective-permute-done.1.refs_3_.refs_2_.refs_9_ = bf16[224,256]{1,0:T(8,128)(2,1)S(1)} collective-permute-done((bf16[224,256]{1,0:T(8,128)(2,1)S(1)}, bf16[224,256]{1,0:T(8,128)(2,1)S(1)}, u32[]{:S(2)}, u32[]{:S(2)}) %collective-permute-start.1) | collective-permute-done | bytes 114720 | tf_op jit(solution)/shard_map/ppermute | solution.py:129
  23.9 3.4 %collective-permute-start.2 = (bf16[224,256]{1,0:T(8,128)(2,1)S(1)}, bf16[224,256]{1,0:T(8,128)(2,1)S(1)}, u32[]{:S(2)}, u32[]{:S(2)}) collective-permute-start(bf16[224,256]{1,0:T(8,128)(2,1)S(1)} %get-tuple-element.26), channel_id=1, source_target_pairs={{0,12},{4,8},{12,0},{8,4},{1,13},{5,9},{13,1},{9,5},{2,14},{6,10},... | collective-permute-start | bytes 344072 | tf_op jit(solution)/shard_map/ppermute | solution.py:129
  27.3 4.4 %collective-permute-done.2.refs_4_.refs_3_.refs_10_ = bf16[224,256]{1,0:T(8,128)(2,1)S(1)} collective-permute-done((bf16[224,256]{1,0:T(8,128)(2,1)S(1)}, bf16[224,256]{1,0:T(8,128)(2,1)S(1)}, u32[]{:S(2)}, u32[]{:S(2)}) %collective-permute-start.2) | collective-permute-done | bytes 114720 | tf_op jit(solution)/shard_map/ppermute | solution.py:129
  32.4 5.4 %collective-permute-done.3.refs_5_.refs_4_.refs_11_ = bf16[224,256]{1,0:T(8,128)(2,1)S(1)} collective-permute-done((bf16[224,256]{1,0:T(8,128)(2,1)S(1)}, bf16[224,256]{1,0:T(8,128)(2,1)S(1)}, u32[]{:S(2)}, u32[]{:S(2)}) %collective-permute-start.3) | collective-permute-done | bytes 114720 | tf_op jit(solution)/shard_map/ppermute | solution.py:129
  40.0 2.7 %shard_map.123 = (f32[2,32,512]{2,1,0:T(8,128)S(1)}, bf16[2,32,512]{2,1,0:T(8,128)(2,1)S(1)}, bf16[2,32,512]{2,1,0:T(8,128)(2,1)S(1)}, bf16[2,32,512]{2,1,0:T(8,128)(2,1)S(1)}) custom-call(bf16[128,1024]{1,0:T(8,128)(2,1)S(1)} %copy-done.11, bf16[128,1024]{1,0:T(8,128)(2,1)S(1)} %collective-permute-done.refs_1_, ...), custom_call_target="tpu_custom_call" | custom-call | flops 805306368 | bytes 1048576 | tf_op jit(solution)/shard_map/pallas_call | solution.py:139
  42.7 1.4 %collective-permute-start.5 = (bf16[2,32,512]{2,1,0:T(8,128)(2,1)S(1)}, bf16[2,32,512]{2,1,0:T(8,128)(2,1)S(1)}, u32[]{:S(2)}, u32[]{:S(2)}) collective-permute-start(bf16[2,32,512]{2,1,0:T(8,128)(2,1)S(1)} %get-tuple-element.30), channel_id=1, source_target_pairs={{0,2},{1,3},{2,0},{3,1},{4,6},{5,7},{6,4},{7,5},{8,10},{9,11},{10,... | collective-permute-start | bytes 196616 | tf_op jit(solution)/shard_map/ppermute | solution.py:134
  45.4 1.4 %shard_map.124 = (f32[1,32,512]{2,1,0:T(8,128)S(1)}, bf16[1,32,512]{2,1,0:T(8,128)(2,1)S(1)}, bf16[1,32,512]{2,1,0:T(8,128)(2,1)S(1)}, bf16[1,32,512]{2,1,0:T(8,128)(2,1)S(1)}) custom-call(bf16[128,1024]{1,0:T(8,128)(2,1)S(1)} %collective-permute-done.7.refs_0_, bf16[224,256]{1,0:T(8,128)(2,1)S(1)} %get-tuple-element.24.refs_2_.refs_1_.refs_8_, ...), custom_call_target="tpu_custom_call" | custom-call | flops 402653184 | bytes 1048576 | tf_op jit(solution)/shard_map/pallas_call | solution.py:139
  46.8 1.4 %shard_map.125 = (f32[2,32,512]{2,1,0:T(8,128)S(1)}, bf16[2,32,512]{2,1,0:T(8,128)(2,1)S(1)}, bf16[2,32,512]{2,1,0:T(8,128)(2,1)S(1)}, bf16[2,32,512]{2,1,0:T(8,128)(2,1)S(1)}) custom-call(bf16[128,1024]{1,0:T(8,128)(2,1)S(1)} %collective-permute-done.8.refs_0_, bf16[224,256]{1,0:T(8,128)(2,1)S(1)} %get-tuple-element.24.refs_2_.refs_1_.refs_8_, ...), custom_call_target="tpu_custom_call" | custom-call | flops 402653184 | bytes 1048576 | tf_op jit(solution)/shard_map/pallas_call | solution.py:139
  50.1 2.3 %collective-permute-done.6.refs_3_ = bf16[2,32,512]{2,1,0:T(8,128)(2,1)S(1)} collective-permute-done((bf16[2,32,512]{2,1,0:T(8,128)(2,1)S(1)}, bf16[2,32,512]{2,1,0:T(8,128)(2,1)S(1)}, u32[]{:S(2)}, u32[]{:S(2)}) %collective-permute-start.6) | collective-permute-done | bytes 65568 | tf_op jit(solution)/shard_map/ppermute | solution.py:134
  54.1 2.0 %collective-permute-done.11.refs_7_ = bf16[2,32,512]{2,1,0:T(8,128)(2,1)S(1)} collective-permute-done((bf16[2,32,512]{2,1,0:T(8,128)(2,1)S(1)}, bf16[2,32,512]{2,1,0:T(8,128)(2,1)S(1)}, u32[]{:S(2)}, u32[]{:S(2)}) %collective-permute-start.11) | collective-permute-done | bytes 65568 | tf_op jit(solution)/shard_map/ppermute | solution.py:134
  57.2 3.0 %collective-permute-start.13 = (bf16[4,32,512]{2,1,0:T(8,128)(2,1)S(1)}, bf16[4,32,512]{2,1,0:T(8,128)(2,1)S(1)}, u32[]{:S(2)}, u32[]{:S(2)}) collective-permute-start(bf16[4,32,512]{2,1,0:T(8,128)(2,1)S(1)} %get-tuple-element.41), channel_id=1, source_target_pairs={{0,12},{4,8},{12,0},{8,4},{1,13},{5,9},{13,1},{9,5},{2,14},{6,10},... | collective-permute-start | bytes 393224 | tf_op jit(solution)/shard_map/ppermute | solution.py:129
  60.2 3.3 %collective-permute-done.12.refs_1_ = bf16[4,32,512]{2,1,0:T(8,128)(2,1)S(1)} collective-permute-done((bf16[4,32,512]{2,1,0:T(8,128)(2,1)S(1)}, bf16[4,32,512]{2,1,0:T(8,128)(2,1)S(1)}, u32[]{:S(2)}, u32[]{:S(2)}) %collective-permute-start.12) | collective-permute-done | bytes 131104 | tf_op jit(solution)/shard_map/ppermute | solution.py:129
  63.6 1.6 %collective-permute-start.14 = (bf16[4,32,512]{2,1,0:T(8,128)(2,1)S(1)}, bf16[4,32,512]{2,1,0:T(8,128)(2,1)S(1)}, u32[]{:S(2)}, u32[]{:S(2)}) collective-permute-start(bf16[4,32,512]{2,1,0:T(8,128)(2,1)S(1)} %get-tuple-element.41), channel_id=1, source_target_pairs={{0,8},{4,0},{12,4},{8,12},{1,9},{5,1},{13,5},{9,13},{2,10},{6,2},{... | collective-permute-start | bytes 393224 | tf_op jit(solution)/shard_map/ppermute | solution.py:129
  65.1 1.9 %collective-permute-done.13.refs_2_ = bf16[4,32,512]{2,1,0:T(8,128)(2,1)S(1)} collective-permute-done((bf16[4,32,512]{2,1,0:T(8,128)(2,1)S(1)}, bf16[4,32,512]{2,1,0:T(8,128)(2,1)S(1)}, u32[]{:S(2)}, u32[]{:S(2)}) %collective-permute-start.13) | collective-permute-done | bytes 131104 | tf_op jit(solution)/shard_map/ppermute | solution.py:129
  68.1 4.5 %collective-permute-done.14.refs_3_ = bf16[4,32,512]{2,1,0:T(8,128)(2,1)S(1)} collective-permute-done((bf16[4,32,512]{2,1,0:T(8,128)(2,1)S(1)}, bf16[4,32,512]{2,1,0:T(8,128)(2,1)S(1)}, u32[]{:S(2)}, u32[]{:S(2)}) %collective-permute-start.14) | collective-permute-done | bytes 131104 | tf_op jit(solution)/shard_map/ppermute | solution.py:129
  72.5 1.4 %collective-permute-start.19 = (bf16[4,32,512]{2,1,0:T(8,128)(2,1)S(1)}, bf16[4,32,512]{2,1,0:T(8,128)(2,1)S(1)}, u32[]{:S(2)}, u32[]{:S(2)}) collective-permute-start(bf16[4,32,512]{2,1,0:T(8,128)(2,1)S(1)} %collective-permute-done.12.refs_1_), channel_id=1, source_target_pairs={{0,2},{1,3},{2,0},{3,1},{4,6},{5,7},{6,4},{7,5},{8,10},{9,11},{10,... | collective-permute-start | bytes 393224 | tf_op jit(solution)/shard_map/ppermute | solution.py:134
  75.0 3.3 %collective-permute-done.19.refs_1_ = bf16[4,32,512]{2,1,0:T(8,128)(2,1)S(1)} collective-permute-done((bf16[4,32,512]{2,1,0:T(8,128)(2,1)S(1)}, bf16[4,32,512]{2,1,0:T(8,128)(2,1)S(1)}, u32[]{:S(2)}, u32[]{:S(2)}) %collective-permute-start.19) | collective-permute-done | bytes 131104 | tf_op jit(solution)/shard_map/ppermute | solution.py:134
  78.2 1.9 %collective-permute-start.21 = (bf16[4,32,512]{2,1,0:T(8,128)(2,1)S(1)}, bf16[4,32,512]{2,1,0:T(8,128)(2,1)S(1)}, u32[]{:S(2)}, u32[]{:S(2)}) collective-permute-start(bf16[4,32,512]{2,1,0:T(8,128)(2,1)S(1)} %collective-permute-done.14.refs_3_), channel_id=1, source_target_pairs={{0,2},{1,3},{2,0},{3,1},{4,6},{5,7},{6,4},{7,5},{8,10},{9,11},{10,... | collective-permute-start | bytes 393224 | tf_op jit(solution)/shard_map/ppermute | solution.py:134
  80.3 2.9 %collective-permute-done.21.refs_3_ = bf16[4,32,512]{2,1,0:T(8,128)(2,1)S(1)} collective-permute-done((bf16[4,32,512]{2,1,0:T(8,128)(2,1)S(1)}, bf16[4,32,512]{2,1,0:T(8,128)(2,1)S(1)}, u32[]{:S(2)}, u32[]{:S(2)}) %collective-permute-start.21) | collective-permute-done | bytes 131104 | tf_op jit(solution)/shard_map/ppermute | solution.py:134
  83.2 1.9 %copy-done.2 = bf16[1,768,2048]{2,1,0:T(8,128)(2,1)S(1)} copy-done((bf16[1,768,2048]{2,1,0:T(8,128)(2,1)S(1)}, bf16[1,768,2048]{2,1,0:T(8,128)(2,1)}, u32[]{:S(2)}) %copy-start.2) | copy-done | bytes 3145752
  85.1 3.1 %shard_map.128 = (bf16[2,32,2048]{2,1,0:T(8,128)(2,1)S(1)}, bf16[2,32,2048]{2,1,0:T(8,128)(2,1)S(1)}) custom-call(bf16[4,32,640]{2,1,0:T(8,128)(2,1)S(1)} %collective-permute-done.18.refs_0_, bf16[4,32,512]{2,1,0:T(8,128)(2,1)S(1)} %collective-permute-done.19.refs_1_, bf16[4,32,512]{2,1,0:T(8,128)(2,1)S(1)} %collective-permute-done.20.refs_2_, ...), custom_call_target="tpu_custom_call" | custom-call | flops 2415919104 | bytes 18874368 | tf_op jit(solution)/shard_map/pallas_call | solution.py:139
  88.3 2.0 %collective-permute-start.22 = (bf16[2,32,2048]{2,1,0:T(8,128)(2,1)S(1)}, bf16[2,32,2048]{2,1,0:T(8,128)(2,1)S(1)}, u32[]{:S(2)}, u32[]{:S(2)}) collective-permute-start(bf16[2,32,2048]{2,1,0:T(8,128)(2,1)S(1)} %get-tuple-element.44), channel_id=1, source_target_pairs={{0,2},{1,3},{2,0},{3,1},{4,6},{5,7},{6,4},{7,5},{8,10},{9,11},{10,... | collective-permute-start | bytes 786440 | tf_op jit(solution)/shard_map/ppermute | solution.py:134
  90.3 3.1 %shard_map.127 = (f32[4,32,2048]{2,1,0:T(8,128)S(1)}, bf16[32,2048]{1,0:T(8,128)(2,1)}) custom-call(bf16[4,32,640]{2,1,0:T(8,128)(2,1)S(1)} %get-tuple-element.40.refs_0_, bf16[4,32,512]{2,1,0:T(8,128)(2,1)S(1)} %collective-permute-done.12.refs_1_, bf16[4,32,512]{2,1,0:T(8,128)(2,1)S(1)} %collective-permute-done.13.refs_2_, ...), custom_call_target="tpu_custom_call" | custom-call | flops 2415919104 | bytes 18874368 | tf_op jit(solution)/shard_map/pallas_call | solution.py:139
  93.5 2.4 %collective-permute-done.22 = bf16[2,32,2048]{2,1,0:T(8,128)(2,1)S(1)} collective-permute-done((bf16[2,32,2048]{2,1,0:T(8,128)(2,1)S(1)}, bf16[2,32,2048]{2,1,0:T(8,128)(2,1)S(1)}, u32[]{:S(2)}, u32[]{:S(2)}) %collective-permute-start.22) | collective-permute-done | bytes 262176 | tf_op jit(solution)/shard_map/ppermute | solution.py:134
  95.8 2.8 %collective-permute-done.25 = bf16[2,32,2048]{2,1,0:T(8,128)(2,1)S(1)} collective-permute-done((bf16[2,32,2048]{2,1,0:T(8,128)(2,1)S(1)}, bf16[2,32,2048]{2,1,0:T(8,128)(2,1)S(1)}, u32[]{:S(2)}, u32[]{:S(2)}) %collective-permute-start.25) | collective-permute-done | bytes 262176 | tf_op jit(solution)/shard_map/ppermute | solution.py:134
  98.7 4.1 %collective-permute-start.23 = (bf16[32,2048]{1,0:T(8,128)(2,1)S(1)}, bf16[32,2048]{1,0:T(8,128)(2,1)S(1)}, u32[]{:S(2)}, u32[]{:S(2)}) collective-permute-start(bf16[32,2048]{1,0:T(8,128)(2,1)S(1)} %get-tuple-element.46), channel_id=1, source_target_pairs={{0,12},{4,8},{12,0},{8,4},{1,13},{5,9},{13,1},{9,5},{2,14},{6,10},... | collective-permute-start | bytes 393224 | tf_op jit(solution)/shard_map/ppermute | solution.py:129
  102.9 2.4 %collective-permute-start.24 = (bf16[32,2048]{1,0:T(8,128)(2,1)S(1)}, bf16[32,2048]{1,0:T(8,128)(2,1)S(1)}, u32[]{:S(2)}, u32[]{:S(2)}) collective-permute-start(bf16[32,2048]{1,0:T(8,128)(2,1)S(1)} %get-tuple-element.47), channel_id=1, source_target_pairs={{0,8},{4,0},{12,4},{8,12},{1,9},{5,1},{13,5},{9,13},{2,10},{6,2},{... | collective-permute-start | bytes 393224 | tf_op jit(solution)/shard_map/ppermute | solution.py:129
  106.8 3.2 %collective-permute-done.24 = bf16[32,2048]{1,0:T(8,128)(2,1)S(1)} collective-permute-done((bf16[32,2048]{1,0:T(8,128)(2,1)S(1)}, bf16[32,2048]{1,0:T(8,128)(2,1)S(1)}, u32[]{:S(2)}, u32[]{:S(2)}) %collective-permute-start.24) | collective-permute-done | bytes 131104 | tf_op jit(solution)/shard_map/ppermute | solution.py:129
  110.0 2.9 %collective-permute-done.26 = bf16[32,2048]{1,0:T(8,128)(2,1)S(1)} collective-permute-done((bf16[32,2048]{1,0:T(8,128)(2,1)S(1)}, bf16[32,2048]{1,0:T(8,128)(2,1)S(1)}, u32[]{:S(2)}, u32[]{:S(2)}) %collective-permute-start.26) | collective-permute-done | bytes 131104 | tf_op jit(solution)/shard_map/ppermute | solution.py:129
  (55 shorter events, 19.7 us)
Async XLA Ops:
  0.6 82.6 %collective-permute-start.15 = (bf16[1,2048,768]{2,1,0:T(8,128)(2,1)}, bf16[1,2048,768]{2,1,0:T(8,128)(2,1)S(1)}, u32[]{:S(2)}, u32[]{:S(2)}) collective-permute-start(bf16[1,2048,768]{2,1,0:T(8,128)(2,1)} %refs_5_.7), channel_id=1, source_target_pairs={{0,1},{1,0},{2,3},{3,2},{4,5},{5,4},{6,7},{7,6},{8,9},{9,8},{10,11... | collective-permute-start | bytes 9437192 | tf_op jit(solution)/shard_map/ppermute | solution.py:134
  1.2 82.0 %collective-permute-start.16 = (bf16[1,2048,768]{2,1,0:T(8,128)(2,1)}, bf16[1,2048,768]{2,1,0:T(8,128)(2,1)S(1)}, u32[]{:S(2)}, u32[]{:S(2)}) collective-permute-start(bf16[1,2048,768]{2,1,0:T(8,128)(2,1)} %refs_6_.5), channel_id=1, source_target_pairs={{0,1},{1,0},{2,3},{3,2},{4,5},{5,4},{6,7},{7,6},{8,9},{9,8},{10,11... | collective-permute-start | bytes 9437192 | tf_op jit(solution)/shard_map/ppermute | solution.py:134
  1.3 81.9 %collective-permute-start.17 = (bf16[1,768,2048]{2,1,0:T(8,128)(2,1)}, bf16[1,768,2048]{2,1,0:T(8,128)(2,1)S(1)}, u32[]{:S(2)}, u32[]{:S(2)}) collective-permute-start(bf16[1,768,2048]{2,1,0:T(8,128)(2,1)} %refs_7_.3), channel_id=1, source_target_pairs={{0,1},{1,0},{2,3},{3,2},{4,5},{5,4},{6,7},{7,6},{8,9},{9,8},{10,11... | collective-permute-start | bytes 9437192 | tf_op jit(solution)/shard_map/ppermute | solution.py:134
  1.7 10.8 %collective-permute-start = (bf16[128,1024]{1,0:T(8,128)(2,1)}, bf16[128,1024]{1,0:T(8,128)(2,1)S(1)}, u32[]{:S(2)}, u32[]{:S(2)}) collective-permute-start(bf16[128,1024]{1,0:T(8,128)(2,1)} %refs_0_.1), channel_id=1, source_target_pairs={{0,4},{4,12},{12,8},{8,0},{1,5},{5,13},{13,9},{9,1},{2,6},{6,14},{... | collective-permute-start | bytes 786440 | tf_op jit(solution)/shard_map/ppermute | solution.py:129
  12.5 14.8 %collective-permute-start.7 = (bf16[128,1024]{1,0:T(8,128)(2,1)S(1)}, bf16[128,1024]{1,0:T(8,128)(2,1)S(1)}, u32[]{:S(2)}, u32[]{:S(2)}) collective-permute-start(bf16[128,1024]{1,0:T(8,128)(2,1)S(1)} %collective-permute-done.refs_1_), channel_id=1, source_target_pairs={{0,4},{4,12},{12,8},{8,0},{1,5},{5,13},{13,9},{9,1},{2,6},{6,14},{... | collective-permute-start | bytes 786440 | tf_op jit(solution)/shard_map/ppermute | solution.py:129
  17.6 6.3 %collective-permute-start.1 = (bf16[224,256]{1,0:T(8,128)(2,1)S(1)}, bf16[224,256]{1,0:T(8,128)(2,1)S(1)}, u32[]{:S(2)}, u32[]{:S(2)}) collective-permute-start(bf16[224,256]{1,0:T(8,128)(2,1)S(1)} %get-tuple-element.25), channel_id=1, source_target_pairs={{0,4},{4,12},{12,8},{8,0},{1,5},{5,13},{13,9},{9,1},{2,6},{6,14},{... | collective-permute-start | bytes 344072 | tf_op jit(solution)/shard_map/ppermute | solution.py:129
  23.9 7.8 %collective-permute-start.2 = (bf16[224,256]{1,0:T(8,128)(2,1)S(1)}, bf16[224,256]{1,0:T(8,128)(2,1)S(1)}, u32[]{:S(2)}, u32[]{:S(2)}) collective-permute-start(bf16[224,256]{1,0:T(8,128)(2,1)S(1)} %get-tuple-element.26), channel_id=1, source_target_pairs={{0,12},{4,8},{12,0},{8,4},{1,13},{5,9},{13,1},{9,5},{2,14},{6,10},... | collective-permute-start | bytes 344072 | tf_op jit(solution)/shard_map/ppermute | solution.py:129
  27.3 15.5 %collective-permute-start.8 = (bf16[128,1024]{1,0:T(8,128)(2,1)S(1)}, bf16[128,1024]{1,0:T(8,128)(2,1)S(1)}, u32[]{:S(2)}, u32[]{:S(2)}) collective-permute-start(bf16[128,1024]{1,0:T(8,128)(2,1)S(1)} %collective-permute-done.7.refs_0_), channel_id=1, source_target_pairs={{0,4},{4,12},{12,8},{8,0},{1,5},{5,13},{13,9},{9,1},{2,6},{6,14},{... | collective-permute-start | bytes 786440 | tf_op jit(solution)/shard_map/ppermute | solution.py:129
  31.7 6.1 %collective-permute-start.3 = (bf16[224,256]{1,0:T(8,128)(2,1)S(1)}, bf16[224,256]{1,0:T(8,128)(2,1)S(1)}, u32[]{:S(2)}, u32[]{:S(2)}) collective-permute-start(bf16[224,256]{1,0:T(8,128)(2,1)S(1)} %get-tuple-element.27), channel_id=1, source_target_pairs={{0,8},{4,0},{12,4},{8,12},{1,9},{5,1},{13,5},{9,13},{2,10},{6,2},{... | collective-permute-start | bytes 344072 | tf_op jit(solution)/shard_map/ppermute | solution.py:129
  37.8 1.2 %copy-start.3 = (bf16[1024,512]{1,0:T(8,128)(2,1)S(1)}, bf16[1024,512]{1,0:T(8,128)(2,1)}, u32[]{:S(2)}) copy-start(bf16[1024,512]{1,0:T(8,128)(2,1)} %refs_5_.5) | copy-start | bytes 3145732
  40.0 43.2 %copy-start.1 = (bf16[1,2048,768]{2,1,0:T(8,128)(2,1)S(1)}, bf16[1,2048,768]{2,1,0:T(8,128)(2,1)}, u32[]{:S(2)}) copy-start(bf16[1,2048,768]{2,1,0:T(8,128)(2,1)} %refs_6_.5) | copy-start | bytes 9437188
  42.6 40.6 %copy-start = (bf16[1,2048,768]{2,1,0:T(8,128)(2,1)S(1)}, bf16[1,2048,768]{2,1,0:T(8,128)(2,1)}, u32[]{:S(2)}) copy-start(bf16[1,2048,768]{2,1,0:T(8,128)(2,1)} %refs_5_.7) | copy-start | bytes 9437188
  42.6 5.6 %collective-permute-start.4 = (bf16[2,32,512]{2,1,0:T(8,128)(2,1)S(1)}, bf16[2,32,512]{2,1,0:T(8,128)(2,1)S(1)}, u32[]{:S(2)}, u32[]{:S(2)}) collective-permute-start(bf16[2,32,512]{2,1,0:T(8,128)(2,1)S(1)} %get-tuple-element.29), channel_id=1, source_target_pairs={{0,1},{1,0},{2,3},{3,2},{4,5},{5,4},{6,7},{7,6},{8,9},{9,8},{10,11... | collective-permute-start | bytes 196616 | tf_op jit(solution)/shard_map/ppermute | solution.py:134
  42.7 6.0 %collective-permute-start.5 = (bf16[2,32,512]{2,1,0:T(8,128)(2,1)S(1)}, bf16[2,32,512]{2,1,0:T(8,128)(2,1)S(1)}, u32[]{:S(2)}, u32[]{:S(2)}) collective-permute-start(bf16[2,32,512]{2,1,0:T(8,128)(2,1)S(1)} %get-tuple-element.30), channel_id=1, source_target_pairs={{0,2},{1,3},{2,0},{3,1},{4,6},{5,7},{6,4},{7,5},{8,10},{9,11},{10,... | collective-permute-start | bytes 196616 | tf_op jit(solution)/shard_map/ppermute | solution.py:134
  45.4 37.8 %copy-start.6 = (f32[2048]{0:T(1024)S(1)}, f32[2048]{0:T(1024)}, u32[]{:S(2)}) copy-start(f32[2048]{0:T(1024)} %param.16) | copy-start | bytes 24580
  48.2 4.1 %collective-permute-start.6 = (bf16[2,32,512]{2,1,0:T(8,128)(2,1)S(1)}, bf16[2,32,512]{2,1,0:T(8,128)(2,1)S(1)}, u32[]{:S(2)}, u32[]{:S(2)}) collective-permute-start(bf16[2,32,512]{2,1,0:T(8,128)(2,1)S(1)} %get-tuple-element.31), channel_id=1, source_target_pairs={{0,3},{1,2},{2,1},{3,0},{4,7},{5,6},{6,5},{7,4},{8,11},{9,10},{10,... | collective-permute-start | bytes 196616 | tf_op jit(solution)/shard_map/ppermute | solution.py:134
  48.7 5.4 %collective-permute-start.10 = (bf16[2,32,512]{2,1,0:T(8,128)(2,1)S(1)}, bf16[2,32,512]{2,1,0:T(8,128)(2,1)S(1)}, u32[]{:S(2)}, u32[]{:S(2)}) collective-permute-start(bf16[2,32,512]{2,1,0:T(8,128)(2,1)S(1)} %get-tuple-element.38), channel_id=1, source_target_pairs={{0,2},{1,3},{2,0},{3,1},{4,6},{5,7},{6,4},{7,5},{8,10},{9,11},{10,... | collective-permute-start | bytes 196616 | tf_op jit(solution)/shard_map/ppermute | solution.py:134
  52.4 3.8 %collective-permute-start.11 = (bf16[2,32,512]{2,1,0:T(8,128)(2,1)S(1)}, bf16[2,32,512]{2,1,0:T(8,128)(2,1)S(1)}, u32[]{:S(2)}, u32[]{:S(2)}) collective-permute-start(bf16[2,32,512]{2,1,0:T(8,128)(2,1)S(1)} %get-tuple-element.39), channel_id=1, source_target_pairs={{0,3},{1,2},{2,1},{3,0},{4,7},{5,6},{6,5},{7,4},{8,11},{9,10},{10,... | collective-permute-start | bytes 196616 | tf_op jit(solution)/shard_map/ppermute | solution.py:134
  54.1 2.0 %collective-permute-start.9 = (bf16[2,32,512]{2,1,0:T(8,128)(2,1)S(1)}, bf16[2,32,512]{2,1,0:T(8,128)(2,1)S(1)}, u32[]{:S(2)}, u32[]{:S(2)}) collective-permute-start(bf16[2,32,512]{2,1,0:T(8,128)(2,1)S(1)} %get-tuple-element.37), channel_id=1, source_target_pairs={{0,1},{1,0},{2,3},{3,2},{4,5},{5,4},{6,7},{7,6},{8,9},{9,8},{10,11... | collective-permute-start | bytes 196616 | tf_op jit(solution)/shard_map/ppermute | solution.py:134
  56.2 7.3 %collective-permute-start.12 = (bf16[4,32,512]{2,1,0:T(8,128)(2,1)S(1)}, bf16[4,32,512]{2,1,0:T(8,128)(2,1)S(1)}, u32[]{:S(2)}, u32[]{:S(2)}) collective-permute-start(bf16[4,32,512]{2,1,0:T(8,128)(2,1)S(1)} %get-tuple-element.41), channel_id=1, source_target_pairs={{0,4},{4,12},{12,8},{8,0},{1,5},{5,13},{13,9},{9,1},{2,6},{6,14},{... | collective-permute-start | bytes 393224 | tf_op jit(solution)/shard_map/ppermute | solution.py:129
  57.2 9.8 %collective-permute-start.13 = (bf16[4,32,512]{2,1,0:T(8,128)(2,1)S(1)}, bf16[4,32,512]{2,1,0:T(8,128)(2,1)S(1)}, u32[]{:S(2)}, u32[]{:S(2)}) collective-permute-start(bf16[4,32,512]{2,1,0:T(8,128)(2,1)S(1)} %get-tuple-element.41), channel_id=1, source_target_pairs={{0,12},{4,8},{12,0},{8,4},{1,13},{5,9},{13,1},{9,5},{2,14},{6,10},... | collective-permute-start | bytes 393224 | tf_op jit(solution)/shard_map/ppermute | solution.py:129
  63.6 9.0 %collective-permute-start.14 = (bf16[4,32,512]{2,1,0:T(8,128)(2,1)S(1)}, bf16[4,32,512]{2,1,0:T(8,128)(2,1)S(1)}, u32[]{:S(2)}, u32[]{:S(2)}) collective-permute-start(bf16[4,32,512]{2,1,0:T(8,128)(2,1)S(1)} %get-tuple-element.41), channel_id=1, source_target_pairs={{0,8},{4,0},{12,4},{8,12},{1,9},{5,1},{13,5},{9,13},{2,10},{6,2},{... | collective-permute-start | bytes 393224 | tf_op jit(solution)/shard_map/ppermute | solution.py:129
  67.0 7.1 %collective-permute-start.18 = (bf16[4,32,640]{2,1,0:T(8,128)(2,1)S(1)}, bf16[4,32,640]{2,1,0:T(8,128)(2,1)S(1)}, u32[]{:S(2)}, u32[]{:S(2)}) collective-permute-start(bf16[4,32,640]{2,1,0:T(8,128)(2,1)S(1)} %get-tuple-element.40.refs_0_), channel_id=1, source_target_pairs={{0,2},{1,3},{2,0},{3,1},{4,6},{5,7},{6,4},{7,5},{8,10},{9,11},{10,... | collective-permute-start | bytes 491528 | tf_op jit(solution)/shard_map/ppermute | solution.py:134
  72.5 5.7 %collective-permute-start.19 = (bf16[4,32,512]{2,1,0:T(8,128)(2,1)S(1)}, bf16[4,32,512]{2,1,0:T(8,128)(2,1)S(1)}, u32[]{:S(2)}, u32[]{:S(2)}) collective-permute-start(bf16[4,32,512]{2,1,0:T(8,128)(2,1)S(1)} %collective-permute-done.12.refs_1_), channel_id=1, source_target_pairs={{0,2},{1,3},{2,0},{3,1},{4,6},{5,7},{6,4},{7,5},{8,10},{9,11},{10,... | collective-permute-start | bytes 393224 | tf_op jit(solution)/shard_map/ppermute | solution.py:134
  74.1 6.2 %collective-permute-start.20 = (bf16[4,32,512]{2,1,0:T(8,128)(2,1)S(1)}, bf16[4,32,512]{2,1,0:T(8,128)(2,1)S(1)}, u32[]{:S(2)}, u32[]{:S(2)}) collective-permute-start(bf16[4,32,512]{2,1,0:T(8,128)(2,1)S(1)} %collective-permute-done.13.refs_2_), channel_id=1, source_target_pairs={{0,2},{1,3},{2,0},{3,1},{4,6},{5,7},{6,4},{7,5},{8,10},{9,11},{10,... | collective-permute-start | bytes 393224 | tf_op jit(solution)/shard_map/ppermute | solution.py:134
  78.2 5.0 %collective-permute-start.21 = (bf16[4,32,512]{2,1,0:T(8,128)(2,1)S(1)}, bf16[4,32,512]{2,1,0:T(8,128)(2,1)S(1)}, u32[]{:S(2)}, u32[]{:S(2)}) collective-permute-start(bf16[4,32,512]{2,1,0:T(8,128)(2,1)S(1)} %collective-permute-done.14.refs_3_), channel_id=1, source_target_pairs={{0,2},{1,3},{2,0},{3,1},{4,6},{5,7},{6,4},{7,5},{8,10},{9,11},{10,... | collective-permute-start | bytes 393224 | tf_op jit(solution)/shard_map/ppermute | solution.py:134
  83.2 1.9 %copy-start.2 = (bf16[1,768,2048]{2,1,0:T(8,128)(2,1)S(1)}, bf16[1,768,2048]{2,1,0:T(8,128)(2,1)}, u32[]{:S(2)}) copy-start(bf16[1,768,2048]{2,1,0:T(8,128)(2,1)} %refs_7_.3) | copy-start | bytes 9437188
  88.3 7.6 %collective-permute-start.22 = (bf16[2,32,2048]{2,1,0:T(8,128)(2,1)S(1)}, bf16[2,32,2048]{2,1,0:T(8,128)(2,1)S(1)}, u32[]{:S(2)}, u32[]{:S(2)}) collective-permute-start(bf16[2,32,2048]{2,1,0:T(8,128)(2,1)S(1)} %get-tuple-element.44), channel_id=1, source_target_pairs={{0,2},{1,3},{2,0},{3,1},{4,6},{5,7},{6,4},{7,5},{8,10},{9,11},{10,... | collective-permute-start | bytes 786440 | tf_op jit(solution)/shard_map/ppermute | solution.py:134
  90.3 8.4 %collective-permute-start.25 = (bf16[2,32,2048]{2,1,0:T(8,128)(2,1)S(1)}, bf16[2,32,2048]{2,1,0:T(8,128)(2,1)S(1)}, u32[]{:S(2)}, u32[]{:S(2)}) collective-permute-start(bf16[2,32,2048]{2,1,0:T(8,128)(2,1)S(1)} %get-tuple-element.45), channel_id=1, source_target_pairs={{0,2},{1,3},{2,0},{3,1},{4,6},{5,7},{6,4},{7,5},{8,10},{9,11},{10,... | collective-permute-start | bytes 786440 | tf_op jit(solution)/shard_map/ppermute | solution.py:134
  98.7 8.1 %collective-permute-start.23 = (bf16[32,2048]{1,0:T(8,128)(2,1)S(1)}, bf16[32,2048]{1,0:T(8,128)(2,1)S(1)}, u32[]{:S(2)}, u32[]{:S(2)}) collective-permute-start(bf16[32,2048]{1,0:T(8,128)(2,1)S(1)} %get-tuple-element.46), channel_id=1, source_target_pairs={{0,12},{4,8},{12,0},{8,4},{1,13},{5,9},{13,1},{9,5},{2,14},{6,10},... | collective-permute-start | bytes 393224 | tf_op jit(solution)/shard_map/ppermute | solution.py:129
  102.9 7.1 %collective-permute-start.24 = (bf16[32,2048]{1,0:T(8,128)(2,1)S(1)}, bf16[32,2048]{1,0:T(8,128)(2,1)S(1)}, u32[]{:S(2)}, u32[]{:S(2)}) collective-permute-start(bf16[32,2048]{1,0:T(8,128)(2,1)S(1)} %get-tuple-element.47), channel_id=1, source_target_pairs={{0,8},{4,0},{12,4},{8,12},{1,9},{5,1},{13,5},{9,13},{2,10},{6,2},{... | collective-permute-start | bytes 393224 | tf_op jit(solution)/shard_map/ppermute | solution.py:129
  105.3 7.5 %collective-permute-start.26 = (bf16[32,2048]{1,0:T(8,128)(2,1)S(1)}, bf16[32,2048]{1,0:T(8,128)(2,1)S(1)}, u32[]{:S(2)}, u32[]{:S(2)}) collective-permute-start(bf16[32,2048]{1,0:T(8,128)(2,1)S(1)} %get-tuple-element.48), channel_id=1, source_target_pairs={{0,4},{4,12},{12,8},{8,0},{1,5},{5,13},{13,9},{9,1},{2,6},{6,14},{... | collective-permute-start | bytes 393224 | tf_op jit(solution)/shard_map/ppermute | solution.py:129
  (7 other events, 6.0 us)

commit v3 on v2

--- a/solution.py
+++ b/solution.py
@@ -134,12 +134,17 @@
     return lax.ppermute(x, "head", [(i, i ^ mask) for i in range(n)])
 
 
-def call(kernel, args, out_shape, scratch, flops, moved, limit):
+def call(kernel, args, out_shape, scratch, flops, moved, limit, fetched=()):
     vmem = pl.BlockSpec(memory_space=pltpu.VMEM)
+    away = pl.BlockSpec(memory_space=pltpu.HBM)
+    args = [
+        pltpu.with_memory_space_constraint(x, pltpu.HBM) if i in fetched else x
+        for i, x in enumerate(args)
+    ]
     return pl.pallas_call(
         kernel,
         out_shape=out_shape,
-        in_specs=[vmem] * len(args),
+        in_specs=[away if i in fetched else vmem for i in range(len(args))],
         out_specs=[vmem] * len(out_shape),
         scratch_shapes=scratch,
         cost_estimate=pl.CostEstimate(flops=flops, bytes_accessed=moved, transcendentals=0),
@@ -147,71 +152,96 @@
     )(*args)
 
 
-def prepare_kernel(n_ctx, k_ref, v_ref, skip_ref, route_ref, gate_ref, *out_refs):
-    hd = HEAD_DIMENSION
+def fetch(pairs, sems):
+    copies = [pltpu.make_async_copy(a, b, sems.at[i]) for i, (a, b) in enumerate(pairs)]
+    for copy in copies:
+        copy.start()
+    return copies
+
+
+def stage_kernel(n, *refs):
+    for copy in fetch(tuple(zip(refs[:n], refs[n : 2 * n])), refs[2 * n]):
+        copy.wait()
+
+
+def stage(*arrays):
+    n = len(arrays)
+    out = [jax.ShapeDtypeStruct(x.shape, x.dtype) for x in arrays]
+    scratch = [pltpu.SemaphoreType.DMA((n,))]
+    kernel = functools.partial(stage_kernel, n)
+    return call(kernel, arrays, out, scratch, 0, 1 << 22, 8, range(n))
+
+
+def pair_kernel(k_ref, v_ref, out_ref, sems):
+    hd = k_ref.shape[1]
+    for copy in fetch(((k_ref, out_ref.at[:, :hd]), (v_ref, out_ref.at[:, hd:])), sems):
+        copy.wait()
+
+
+def pair(keys, values):
+    out = jax.ShapeDtypeStruct((keys.shape[0], 2 * keys.shape[1]), keys.dtype)
+    scratch = [pltpu.SemaphoreType.DMA((2,))]
+    return call(pair_kernel, (keys, values), [out], scratch, 0, 1 << 16, 2, (0, 1))[0]
+
+
+def parts_kernel(n_ctx, skip_in, route_in, gate_in, *refs):
+    out_refs, (skip_ref, route_ref, gate_ref, sems) = refs[:n_ctx], refs[n_ctx:]
+    copies = fetch(((skip_in, skip_ref), (route_in, route_ref), (gate_in, gate_ref)), sems)
+    for copy in copies:
+        copy.wait()
     gates = gate_ref[...].T
     routes = route_ref[...].T
     share = gates / jnp.sum(gates, axis=-1, keepdims=True)
     own_rows, dim = skip_ref.shape
+    cols = dim // n_ctx
     lanes = lax.broadcasted_iota(jnp.int32, (own_rows, 2 * LANES), 1)
     table = jnp.zeros((own_rows, 2 * LANES), jnp.float32)
     for k in range(gates.shape[1]):
         table += jnp.where(lanes % LANES == routes[:, k : k + 1], share[:, k : k + 1], 0.0)
     high = table.astype(jnp.bfloat16).astype(jnp.float32)
     packed = jnp.where(lanes < LANES, high, table - high).astype(jnp.bfloat16)
-    rows = k_ref.shape[0]
-    width = 2 * hd
     for s, out_ref in enumerate(out_refs):
-        out_ref[:rows, :hd] = k_ref[...]
-        out_ref[:rows, hd:] = v_ref[...]
-        first = behind(-s) * (dim // n_ctx)
-        at = rows
-        for i in range(dim // n_ctx // width):
-            cols = pl.ds(pl.multiple_of(first + i * width, width), width)
-            out_ref[at : at + own_rows, :] = skip_ref[:, cols]
-            at += own_rows
-        out_ref[at:, : 2 * LANES] = packed
-        out_ref[at:, 2 * LANES :] = jnp.zeros((own_rows, width - 2 * LANES), jnp.bfloat16)
-
-
-def prepare(keys, values, residual, routes, gates):
+        at = pl.ds(pl.multiple_of(behind(-s) * cols, cols), cols)
+        out_ref[:, :cols] = skip_ref[:, at]
+        out_ref[:, cols:] = packed
+
+
+def make_parts(residual, routes, gates):
     n_ctx = lax.axis_size("ctx")
     own_rows, dim = residual.shape
-    rows = keys.shape[0] + own_rows * (dim // n_ctx // (2 * HEAD_DIMENSION) + 1)
-    part = jax.ShapeDtypeStruct((rows, 2 * HEAD_DIMENSION), jnp.bfloat16)
-    args = (keys, values, residual, routes.T, gates.T)
-    kernel = functools.partial(prepare_kernel, n_ctx)
-    return call(kernel, args, [part] * n_ctx, [], 0, 1 << 18, 4)
-
-
-def attend_kernel(steps, n_before, n_ctx, n_head, *refs):
+    part = jax.ShapeDtypeStruct((own_rows, dim // n_ctx + 2 * LANES), jnp.bfloat16)
+    args = (residual, routes.T, gates.T)
+    scratch = [pltpu.VMEM(x.shape, x.dtype) for x in args] + [pltpu.SemaphoreType.DMA((3,))]
+    kernel = functools.partial(parts_kernel, n_ctx)
+    return call(kernel, args, [part] * n_ctx, scratch, 0, 1 << 18, 4, (0, 1, 2))
+
+
+def attend_kernel(steps, splits, n_ctx, n_head, *refs):
     n = len(steps)
-    q_refs, refs = refs[:n], refs[n:]
-    part_refs, refs = refs[:n_ctx], refs[n_ctx:]
+    q_refs, refs = refs[: n * splits], refs[n * splits :]
+    kv_refs, refs = refs[:n_ctx], refs[n_ctx:]
     w_ref, refs = refs[0], refs[1:]
-    if n_before:
-        before, refs = refs[:n_head], refs[n_head:]
-    out_refs, (k_all, v_all, queries, att, prod) = refs[:n_head], refs[n_head:]
+    keep_ref, send_ref, k_all, v_all, queries, att, prod = refs
     hd = HEAD_DIMENSION
-    rows, q_cols = q_refs[0].shape
+    rows, q_cols = k_all.shape[0] // n_ctx, q_refs[0].shape[1]
     own_rows = rows // n_head
     heads = q_cols // hd
     together = 4
     _, h = place()
     key_pos = []
     for m in range(n_ctx):
-        k_all[m * rows : (m + 1) * rows, :] = part_refs[m][:rows, :hd]
-        v_all[m * rows : (m + 1) * rows, :] = part_refs[m][:rows, hd:]
+        k_all[m * rows : (m + 1) * rows, :] = kv_refs[m][:, :hd]
+        v_all[m * rows : (m + 1) * rows, :] = kv_refs[m][:, hd:]
         key_pos.append(behind(m) * rows + lax.broadcasted_iota(jnp.int32, (rows, rows), 1))
     key_pos = jnp.concatenate(key_pos, axis=1)
     row_pos = lax.broadcasted_iota(jnp.int32, (rows, 1), 0)
     scale = hd**-0.5
-    for j in range(n_head if n_before else 0):
-        out_refs[j][:n_before] = before[j][...]
     for i, step in enumerate(steps):
         visible = key_pos <= behind(step) * rows + row_pos
         for g in range(heads):
-            queries[g * rows : (g + 1) * rows, :] = q_refs[i][:, g * hd : (g + 1) * hd]
+            for k, q_ref in enumerate(q_refs[i * splits : (i + 1) * splits]):
+                at = g * rows + k * (rows // splits)
+                queries[at : at + rows // splits, :] = q_ref[:, g * hd : (g + 1) * hd]
         for g in range(0, heads, together):
             scores = lax.dot_general(
                 queries[g * rows : (g + together) * rows, :],
@@ -235,19 +265,21 @@
         for j in range(n_head):
             start = pl.multiple_of(jnp.bitwise_xor(h, j) * own_rows, own_rows)
             block = prod[pl.ds(start, own_rows), :]
-            out_refs[j][n_before + i] = block.astype(out_refs[j].dtype)
-
-
-def attend(steps, q_list, parts, o_weight, before):
+            if j % 2:
+                send_ref[i, j // 2] = block.astype(jnp.bfloat16)
+            else:
+                keep_ref[i, j // 2] = block
+
+
+def attend(steps, q_list, kv_list, o_weight):
     n_ctx, n_head = lax.axis_size("ctx"), lax.axis_size("head")
-    rows, q_cols = q_list[0].shape
+    rows, q_cols = kv_list[0].shape[0], q_list[0].shape[1]
     out_cols = o_weight.shape[1]
     n = len(steps)
-    n_before = before[0].shape[0] if before else 0
-    piece = (n_before + n, rows // n_head, out_cols)
-    out_shape = [jax.ShapeDtypeStruct(piece, jnp.float32)]
-    out_shape += [jax.ShapeDtypeStruct(piece, jnp.bfloat16)] * (n_head - 1)
-    kernel = functools.partial(attend_kernel, steps, n_before, n_ctx, n_head)
+    splits = len(q_list) // n
+    piece = (n, n_head // 2, rows // n_head, out_cols)
+    out_shape = [jax.ShapeDtypeStruct(piece, t) for t in (jnp.float32, jnp.bfloat16)]
+    kernel = functools.partial(attend_kernel, steps, splits, n_ctx, n_head)
     scratch = [
         pltpu.VMEM((rows * n_ctx, HEAD_DIMENSION), jnp.bfloat16),
         pltpu.VMEM((rows * n_ctx, HEAD_DIMENSION), jnp.bfloat16),
@@ -256,50 +288,60 @@
         pltpu.VMEM((rows, out_cols), jnp.float32),
     ]
     flops = n * (4 * rows * q_cols * rows * n_ctx + 2 * rows * q_cols * out_cols)
-    args = (*q_list, *parts, o_weight, *before)
+    args = (*q_list, *kv_list, o_weight)
     return call(kernel, args, out_shape, scratch, flops, 2 * q_cols * out_cols, 16)
 
 
-def combine_kernel(n_ctx, sizes, n_head, *refs):
-    sums, refs = refs[: n_head * len(sizes)], refs[n_head * len(sizes) :]
+def halve_kernel(n, *refs):
+    keeps, gots, (own_ref, send_ref) = refs[:n], refs[n : 2 * n], refs[2 * n :]
+    at = 0
+    for keep, got in zip(keeps, gots):
+        here = slice(at, at + keep.shape[0])
+        total = keep[...] + got[...].astype(jnp.float32)
+        own_ref[here] = total[:, 0]
+        send_ref[here] = total[:, 1].astype(jnp.bfloat16)
+        at += keep.shape[0]
+
+
+def halve(keeps, gots):
+    n_blocks = sum(x.shape[0] for x in keeps)
+    shape = (n_blocks, *keeps[0].shape[2:])
+    out_shape = [jax.ShapeDtypeStruct(shape, t) for t in (jnp.float32, jnp.bfloat16)]
+    kernel = functools.partial(halve_kernel, len(keeps))
+    return call(kernel, (*keeps, *gots), out_shape, [], 0, 1 << 20, 6)
+
+
+def combine_kernel(n_ctx, own_ref, got_ref, *refs):
     part_refs, (piece_ref, shared_ref) = refs[:n_ctx], refs[n_ctx:]
-    own_rows, cols = piece_ref.shape[1:]
-    width = part_refs[0].shape[1]
-    base = part_refs[0].shape[0] - own_rows * (cols // width + 1)
-    s = 0
-    for k, size in enumerate(sizes):
-        for i in range(size):
-            total = sums[k * n_head][i]
-            for j in range(1, n_head):
-                total += sums[k * n_head + j][i].astype(jnp.float32)
-            for b in range(cols // width):
-                at = slice(b * width, (b + 1) * width)
-                first = base + b * own_rows
-                skip = part_refs[s][first : first + own_rows, :].astype(jnp.float32)
-                block = (total[:, at] + skip).astype(jnp.bfloat16)
-                piece_ref[s, :, at] = block
-                shared_ref[s, :, at] = block
-            shared_ref[s, :, cols:] = part_refs[s][base + cols // width * own_rows :, : 2 * LANES]
-            s += 1
-
-
-def combine(sums, parts, sizes):
-    n_ctx, n_head = lax.axis_size("ctx"), lax.axis_size("head")
-    _, own_rows, cols = sums[0].shape
+    cols = piece_ref.shape[2]
+    for s in range(n_ctx):
+        total = own_ref[s] + got_ref[s].astype(jnp.float32)
+        block = (total + part_refs[s][:, :cols].astype(jnp.float32)).astype(jnp.bfloat16)
+        piece_ref[s] = block
+        shared_ref[s, :, :cols] = block
+        shared_ref[s, :, cols:] = part_refs[s][:, cols:]
+
+
+def combine(own, got, parts):
+    n_ctx, own_rows, cols = own.shape
     out_shape = [
         jax.ShapeDtypeStruct((n_ctx, own_rows, cols), jnp.bfloat16),
         jax.ShapeDtypeStruct((n_ctx, own_rows, cols + 2 * LANES), jnp.bfloat16),
     ]
-    kernel = functools.partial(combine_kernel, n_ctx, sizes, n_head)
-    return call(kernel, (*sums, *parts), out_shape, [], 0, 1 << 20, 4)
-
-
-def expert_kernel(n_ctx, halves, *refs):
-    pieces, refs = refs[:n_ctx], refs[n_ctx:]
+    kernel = functools.partial(combine_kernel, n_ctx)
+    return call(kernel, (own, got, *parts), out_shape, [], 0, 1 << 20, 4)
+
+
+def expert_kernel(n_ctx, own, *refs):
+    if own:
+        pieces, refs = refs[:n_ctx], refs[n_ctx:]
+    else:
+        shared, near, far, *refs = refs
+        pieces = (shared, near.at[0], far, near.at[1])
     gain_ref, refs = refs[0], refs[1:]
     weights, refs = (refs[:3], refs[3:6]), refs[6:]
     outs, (x_ref, acc_ref, share_ref) = refs[:-3], refs[-3:]
-    own_rows, cols = pieces[1].shape[1:]
+    own_rows, cols = pieces[2].shape[1:]
     c, h = place()
 
     for t in range(n_ctx):
@@ -311,8 +353,8 @@
             square += jnp.sum(block_f * block_f, axis=-1, keepdims=True)
             at = pl.ds(pl.multiple_of(behind(m) * cols, cols), cols)
             blocks.append((block_f, at))
-            if halves is None and t == 0:
-                outs[1][:, at] = block
+            if own and t == 0:
+                outs[-1][:, at] = block
         root = lax.rsqrt(square / (cols * n_ctx) + 1e-06)
         here = slice(t * own_rows, (t + 1) * own_rows)
         for block_f, at in blocks:
@@ -329,72 +371,72 @@
         out = jnp.dot(hidden, down_ref[0], preferred_element_type=jnp.float32) * share
         if i == 0:
             acc_ref[...] = out
-        elif halves is None:
-            outs[0][...] = (acc_ref[...] + out).reshape(outs[0].shape)
         else:
-            total = (acc_ref[...] + out).astype(jnp.bfloat16)
-            for out_ref, half in zip(outs, halves):
-                for at, t in enumerate(half):
-                    out_ref[at] = total[t * own_rows : (t + 1) * own_rows, :]
-
-
-def experts(pieces, gain, weights, halves):
+            total = (acc_ref[...] + out).astype(outs[0].dtype)
+            for t in range(n_ctx):
+                outs[t][...] = total[t * own_rows : (t + 1) * own_rows, :]
+
+
+def experts(pieces, gain, weights, own):
     n_ctx, own_rows, _ = pieces[0].shape
     _, dim, hidden = weights[0].shape
     rows = own_rows * n_ctx
-    if halves is None:
-        out_shape = [
-            jax.ShapeDtypeStruct((n_ctx, own_rows, dim), jnp.float32),
-            jax.ShapeDtypeStruct((own_rows, dim), jnp.bfloat16),
-        ]
-    else:
-        out_shape = [
-            jax.ShapeDtypeStruct((len(half), own_rows, dim), jnp.bfloat16) for half in halves
-        ]
+    out = jax.ShapeDtypeStruct((own_rows, dim), jnp.float32 if own else jnp.bfloat16)
+    out_shape = [out] * n_ctx
+    if own:
+        out_shape.append(jax.ShapeDtypeStruct((own_rows, dim), jnp.bfloat16))
     scratch = [
         pltpu.VMEM((rows, dim), jnp.bfloat16),
         pltpu.VMEM((rows, dim), jnp.float32),
         pltpu.VMEM((rows, 2 * LANES), jnp.float32),
     ]
     args = (*pieces, gain.reshape(1, -1), *weights)
-    kernel = functools.partial(expert_kernel, n_ctx, halves)
+    kernel = functools.partial(expert_kernel, n_ctx, own)
     flops = 12 * rows * dim * hidden
     return call(kernel, args, out_shape, scratch, flops, 12 * dim * hidden, 28)
+
+
+def add_kernel(a_ref, b_ref, out_ref):
+    out_ref[...] = (a_ref[...] + b_ref[...].astype(jnp.float32)).astype(out_ref.dtype)
+
+
+def add(a, b):
+    return call(add_kernel, (a, b), [jax.ShapeDtypeStruct(b.shape, b.dtype)], [], 0, 1 << 19, 2)[0]
 
 
 def dense_body(query, keys, values, residual, o_weight, gain, routes, gates, w_gate, w_up, w_down):
     q_list = [query]
     for _ in range(3):
         q_list.append(shift(q_list[-1], 1))
-    parts = prepare(keys, values, residual, routes, gates)
+    kv = pair(keys, values)
+    kv_back = shift(kv, 1)
+    kv_list = [kv, kv_back, shift(kv_back, 1), shift(kv, 3)]
+    parts = make_parts(residual, routes, gates)
     parts = [parts[0]] + [shift(parts[s], s) for s in (1, 2, 3)]
 
     weights = [w_gate, w_up, w_down]
     weights += [swap(w, 1) for w in weights]
-
-    first = attend((0, 1), q_list[:2], parts, o_weight, ())
-    later = attend((2,), q_list[2:3], parts, o_weight, ())
-    later = attend((3,), q_list[3:], parts, o_weight, later)
-    sums = []
-    for group in (first, later):
-        sums.append(group[0])
-        sums += [swap(group[j], j) for j in (1, 2, 3)]
-    piece, shared = combine(sums, parts, (2, 2))
-    pieces = [shared] + [shift(piece, m) for m in (1, 2, 3)]
-    other_pieces = [swap(x, 2) for x in pieces]
-
-    own_out, mixed = experts(pieces, gain, weights, None)
-    halves = ((2, 1), (3, 0))
-    other_out = experts(other_pieces, gain, weights, halves)
-
-    result = 0.0
-    for half, out in zip(halves, other_out):
-        got = swap(out, 2)
-        for at, t in enumerate(half):
-            total = own_out[t] + got[at].astype(jnp.float32)
-            if t:
-                total = shift(total.astype(jnp.bfloat16), -t).astype(jnp.float32)
-            result = result + total
+    o_weight, q_list[0], weights[2] = stage(o_weight, query, w_down)
+
+    first = attend((0, 1, 2), q_list[:3], kv_list, o_weight)
+    last = attend((3,), q_list[3:], kv_list, o_weight)
+    keeps, sends = zip(first, last)
+    gots = [swap(x, 1) for x in sends]
+    own, send = halve(keeps, gots)
+    piece, shared = combine(own, swap(send, 2), parts)
+    back, ahead = shift(piece, 1), shift(piece, 3)
+    pieces = [shared, back, shift(back, 1), ahead]
+    sides = swap(jnp.stack([back, ahead]), 2)
+    other_pieces = [swap(shared, 2), sides, swap(pieces[2], 2)]
+
+    *own_out, mixed = experts(pieces, gain, weights, True)
+    other_out = experts(other_pieces, gain, weights, False)
+
+    got = [swap(x, 2) for x in other_out]
+    result = own_out[0] + got[0].astype(jnp.float32)
+    for t in (1, 2, 3):
+        total = shift(add(own_out[t], got[t]), -t)
+        result = result + total.astype(jnp.float32)
     return (mixed, result.astype(jnp.bfloat16))
 
 

time: 114 us -> 100 us (0.88)
  local copies, waits for them, and re-layouts: 9.09 us -> 0.02 us
  starting transfers between devices: 36.1 us -> 31.6 us
  waiting for transfers between devices: 54.6 us -> 50.5 us
  Pallas kernels: 12.2 us -> 16.2 us
    unnamed x24 -> x6, local copies, waits for them, and re-layouts: 9.09 us -> 0.02 us
    ppermute x15 -> x13, waiting for transfers between devices: 16.9 us -> 10.5 us  [swap(): return lax.ppermute(x, 'head', [(i, i ^ mask) for i in range(n)])]
    pallas_call x7 -> x12, Pallas kernels: 12.2 us -> 16.2 us  [call(): pl.pallas_call(kernel, out_shape=out_shape, in_specs=[away if i in fetche...]
    ppermute x15 -> x13, starting transfers between devices: 12.5 us -> 8.95 us  [swap(): return lax.ppermute(x, 'head', [(i, i ^ mask) for i in range(n)])]
    ppermute x12 -> x15, waiting for transfers between devices: 37.6 us -> 40 us  [shift(): return lax.ppermute(x, 'ctx', pairs)]
    ppermute x12 -> x15, starting transfers between devices: 23.6 us -> 22.7 us  [shift(): return lax.ppermute(x, 'ctx', pairs)]
  transfers between devices with their start and end apart: 27 -> 28, of which waited for: 19 -> 15; matrix products, arithmetic and copies ran while one was open for 0% -> 0% of each run, Pallas kernels for 8% -> 13%
where the time goes in v3:
time: 100 us; the launch traced here: 99.9 us
  waiting for transfers between devices  50.5 us (50%)
  starting transfers between devices  31.6 us (32%)
  Pallas kernels  16.2 us (16%)
    ppermute x15, waiting for transfers between devices, shift(): return lax.ppermute(x, 'ctx', pairs)  40 us
    ppermute x15, starting transfers between devices, shift(): return lax.ppermute(x, 'ctx', pairs)  22.7 us
    pallas_call x12, Pallas kernels, call(): pl.pallas_call(kernel, out_shape=out_shape, in_specs=[away if i in fetche...  16.2 us
    ppermute x13, waiting for transfers between devices, swap(): return lax.ppermute(x, 'head', [(i, i ^ mask) for i in range(n)])  10.5 us
    ppermute x13, starting transfers between devices, swap(): return lax.ppermute(x, 'head', [(i, i ^ mask) for i in range(n)])  8.95 us
  transfers between devices with their start and end apart: 28, of which 15 were waited for; matrix products, arithmetic and copies ran while one was open for 0% of the time, Pallas kernels for 13%

profile of v3, /device:TPU:0, one launch (start us, length us, event | category | flops | bytes accessed | tf_op | source)
XLA Modules:
  0.0 99.9 jit_solution(6324226355537158374)
XLA Ops:
  1.7 2.6 %collective-permute-start = (bf16[128,1024]{1,0:T(8,128)(2,1)}, bf16[128,1024]{1,0:T(8,128)(2,1)S(1)}, u32[]{:S(2)}, u32[]{:S(2)}) collective-permute-start(bf16[128,1024]{1,0:T(8,128)(2,1)} %refs_1_.1), channel_id=1, source_target_pairs={{0,4},{4,12},{12,8},{8,0},{1,5},{5,13},{13,9},{9,1},{2,6},{6,14},{... | collective-permute-start | bytes 786440 | tf_op jit(solution)/shard_map/ppermute | solution.py:129
  4.3 8.1 %collective-permute-done.refs_1_ = bf16[128,1024]{1,0:T(8,128)(2,1)S(1)} collective-permute-done((bf16[128,1024]{1,0:T(8,128)(2,1)}, bf16[128,1024]{1,0:T(8,128)(2,1)S(1)}, u32[]{:S(2)}, u32[]{:S(2)}) %collective-permute-start) | collective-permute-done | bytes 262176 | tf_op jit(solution)/shard_map/ppermute | solution.py:129
  14.2 3.3 %collective-permute-start.2 = (bf16[128,256]{1,0:T(8,128)(2,1)S(1)}, bf16[128,256]{1,0:T(8,128)(2,1)S(1)}, u32[]{:S(2)}, u32[]{:S(2)}) collective-permute-start(bf16[128,256]{1,0:T(8,128)(2,1)S(1)} %shard_map.123.refs_3_.refs_1_), channel_id=1, source_target_pairs={{0,4},{4,12},{12,8},{8,0},{1,5},{5,13},{13,9},{9,1},{2,6},{6,14},{... | collective-permute-start | bytes 196616 | tf_op jit(solution)/shard_map/ppermute | solution.py:129
  17.5 5.3 %collective-permute-done.2.refs_4_.refs_2_ = bf16[128,256]{1,0:T(8,128)(2,1)S(1)} collective-permute-done((bf16[128,256]{1,0:T(8,128)(2,1)S(1)}, bf16[128,256]{1,0:T(8,128)(2,1)S(1)}, u32[]{:S(2)}, u32[]{:S(2)}) %collective-permute-start.2) | collective-permute-done | bytes 65568 | tf_op jit(solution)/shard_map/ppermute | solution.py:129
  22.8 1.3 %collective-permute-start.4 = (bf16[128,256]{1,0:T(8,128)(2,1)S(1)}, bf16[128,256]{1,0:T(8,128)(2,1)S(1)}, u32[]{:S(2)}, u32[]{:S(2)}) collective-permute-start(bf16[128,256]{1,0:T(8,128)(2,1)S(1)} %shard_map.123.refs_3_.refs_1_), channel_id=1, source_target_pairs={{0,8},{4,0},{12,4},{8,12},{1,9},{5,1},{13,5},{9,13},{2,10},{6,2},{... | collective-permute-start | bytes 196616 | tf_op jit(solution)/shard_map/ppermute | solution.py:129
  24.1 3.0 %collective-permute-done.4.refs_6_.refs_4_ = bf16[128,256]{1,0:T(8,128)(2,1)S(1)} collective-permute-done((bf16[128,256]{1,0:T(8,128)(2,1)S(1)}, bf16[128,256]{1,0:T(8,128)(2,1)S(1)}, u32[]{:S(2)}, u32[]{:S(2)}) %collective-permute-start.4) | collective-permute-done | bytes 65568 | tf_op jit(solution)/shard_map/ppermute | solution.py:129
  27.1 1.9 %collective-permute-start.3 = (bf16[128,256]{1,0:T(8,128)(2,1)S(1)}, bf16[128,256]{1,0:T(8,128)(2,1)S(1)}, u32[]{:S(2)}, u32[]{:S(2)}) collective-permute-start(bf16[128,256]{1,0:T(8,128)(2,1)S(1)} %collective-permute-done.2.refs_4_.refs_2_), channel_id=1, source_target_pairs={{0,4},{4,12},{12,8},{8,0},{1,5},{5,13},{13,9},{9,1},{2,6},{6,14},{... | collective-permute-start | bytes 196616 | tf_op jit(solution)/shard_map/ppermute | solution.py:129
  29.0 2.0 %collective-permute-start.5 = (bf16[128,1024]{1,0:T(8,128)(2,1)S(1)}, bf16[128,1024]{1,0:T(8,128)(2,1)S(1)}, u32[]{:S(2)}, u32[]{:S(2)}) collective-permute-start(bf16[128,1024]{1,0:T(8,128)(2,1)S(1)} %collective-permute-done.1.refs_2_), channel_id=1, source_target_pairs={{0,4},{4,12},{12,8},{8,0},{1,5},{5,13},{13,9},{9,1},{2,6},{6,14},{... | collective-permute-start | bytes 786440 | tf_op jit(solution)/shard_map/ppermute | solution.py:129
  31.0 2.3 %shard_map.122 = (bf16[1024,512]{1,0:T(8,128)(2,1)S(1)}, bf16[128,1024]{1,0:T(8,128)(2,1)S(1)}, bf16[1,768,2048]{2,1,0:T(8,128)(2,1)S(1)}) custom-call(bf16[1024,512]{1,0:T(8,128)(2,1)} %refs_0_.1, bf16[128,1024]{1,0:T(8,128)(2,1)} %refs_1_.1, bf16[1,768,2048]{2,1,0:T(8,128)(2,1)} %refs_2_.1), custom_call_target="tpu_custom_call" | custom-call | bytes 4194304 | tf_op jit(solution)/shard_map/pallas_call | solution.py:144
  33.4 3.9 %shard_map.124 = (f32[3,2,32,512]{3,2,1,0:T(8,128)S(1)}, bf16[3,2,32,512]{3,2,1,0:T(8,128)(2,1)S(1)}) custom-call(bf16[128,1024]{1,0:T(8,128)(2,1)S(1)} %get-tuple-element.26.refs_0_, bf16[128,1024]{1,0:T(8,128)(2,1)S(1)} %collective-permute-done.refs_1_, bf16[128,1024]{1,0:T(8,128)(2,1)S(1)} %collective-permute-done.1.refs_2_, ...), custom_call_target="tpu_custom_call" | custom-call | flops 1207959552 | bytes 1048576 | tf_op jit(solution)/shard_map/pallas_call | solution.py:144
  37.4 1.4 %shard_map.125 = (f32[1,2,32,512]{3,2,1,0:T(8,128)S(1)}, bf16[1,2,32,512]{3,2,1,0:T(8,128)(2,1)S(1)}) custom-call(bf16[128,1024]{1,0:T(8,128)(2,1)S(1)} %collective-permute-done.5.refs_0_, bf16[128,256]{1,0:T(8,128)(2,1)S(1)} %shard_map.123.refs_3_.refs_1_, bf16[128,256]{1,0:T(8,128)(2,1)S(1)} %collective-permute-done.2.refs_4_.refs_2_, ...), custom_call_target="tpu_custom_call" | custom-call | flops 402653184 | bytes 1048576 | tf_op jit(solution)/shard_map/pallas_call | solution.py:144
  40.3 1.6 %collective-permute-start.8 = (bf16[4,32,512]{2,1,0:T(8,128)(2,1)S(1)}, bf16[4,32,512]{2,1,0:T(8,128)(2,1)S(1)}, u32[]{:S(2)}, u32[]{:S(2)}) collective-permute-start(bf16[4,32,512]{2,1,0:T(8,128)(2,1)S(1)} %get-tuple-element.33), channel_id=1, source_target_pairs={{0,2},{1,3},{2,0},{3,1},{4,6},{5,7},{6,4},{7,5},{8,10},{9,11},{10,... | collective-permute-start | bytes 393224 | tf_op jit(solution)/shard_map/ppermute | solution.py:134
  41.9 1.3 %shard_map.127 = (bf16[32,640]{1,0:T(8,128)(2,1)S(1)}, bf16[32,640]{1,0:T(8,128)(2,1)S(1)}, bf16[32,640]{1,0:T(8,128)(2,1)S(1)}, bf16[32,640]{1,0:T(8,128)(2,1)S(1)}) custom-call(bf16[32,2048]{1,0:T(8,128)(2,1)} %skip_in.1, s32[8,32]{1,0:T(8,128)} %bitcast.9, f32[8,32]{1,0:T(8,128)} %bitcast.10), custom_call_target="tpu_custom_call" | custom-call | bytes 262144 | tf_op jit(solution)/shard_map/pallas_call | solution.py:144
  43.2 2.4 %collective-permute-start.10 = (bf16[32,640]{1,0:T(8,128)(2,1)S(1)}, bf16[32,640]{1,0:T(8,128)(2,1)S(1)}, u32[]{:S(2)}, u32[]{:S(2)}) collective-permute-start(bf16[32,640]{1,0:T(8,128)(2,1)S(1)} %get-tuple-element.36), channel_id=1, source_target_pairs={{0,12},{4,8},{12,0},{8,4},{1,13},{5,9},{13,1},{9,5},{2,14},{6,10},... | collective-permute-start | bytes 122888 | tf_op jit(solution)/shard_map/ppermute | solution.py:129
  45.6 3.5 %collective-permute-done.10.refs_2_ = bf16[32,640]{1,0:T(8,128)(2,1)S(1)} collective-permute-done((bf16[32,640]{1,0:T(8,128)(2,1)S(1)}, bf16[32,640]{1,0:T(8,128)(2,1)S(1)}, u32[]{:S(2)}, u32[]{:S(2)}) %collective-permute-start.10) | collective-permute-done | bytes 40992 | tf_op jit(solution)/shard_map/ppermute | solution.py:129
  49.1 4.0 %collective-permute-done.11.refs_3_ = bf16[32,640]{1,0:T(8,128)(2,1)S(1)} collective-permute-done((bf16[32,640]{1,0:T(8,128)(2,1)S(1)}, bf16[32,640]{1,0:T(8,128)(2,1)S(1)}, u32[]{:S(2)}, u32[]{:S(2)}) %collective-permute-start.11) | collective-permute-done | bytes 40992 | tf_op jit(solution)/shard_map/ppermute | solution.py:129
  54.0 4.0 %collective-permute-done.9.refs_1_ = bf16[32,640]{1,0:T(8,128)(2,1)S(1)} collective-permute-done((bf16[32,640]{1,0:T(8,128)(2,1)S(1)}, bf16[32,640]{1,0:T(8,128)(2,1)S(1)}, u32[]{:S(2)}, u32[]{:S(2)}) %collective-permute-start.9) | collective-permute-done | bytes 40992 | tf_op jit(solution)/shard_map/ppermute | solution.py:129
  58.4 2.6 %collective-permute-start.14 = (bf16[4,32,512]{2,1,0:T(8,128)(2,1)S(1)}, bf16[4,32,512]{2,1,0:T(8,128)(2,1)S(1)}, u32[]{:S(2)}, u32[]{:S(2)}) collective-permute-start(bf16[4,32,512]{2,1,0:T(8,128)(2,1)S(1)} %get-tuple-element.39), channel_id=1, source_target_pairs={{0,8},{4,0},{12,4},{8,12},{1,9},{5,1},{13,5},{9,13},{2,10},{6,2},{... | collective-permute-start | bytes 393224 | tf_op jit(solution)/shard_map/ppermute | solution.py:129
  61.0 3.0 %collective-permute-done.12.refs_1_ = bf16[4,32,512]{2,1,0:T(8,128)(2,1)S(1)} collective-permute-done((bf16[4,32,512]{2,1,0:T(8,128)(2,1)S(1)}, bf16[4,32,512]{2,1,0:T(8,128)(2,1)S(1)}, u32[]{:S(2)}, u32[]{:S(2)}) %collective-permute-start.12) | collective-permute-done | bytes 131104 | tf_op jit(solution)/shard_map/ppermute | solution.py:129
  64.6 2.2 %collective-permute-done.14.refs_3_ = bf16[4,32,512]{2,1,0:T(8,128)(2,1)S(1)} collective-permute-done((bf16[4,32,512]{2,1,0:T(8,128)(2,1)S(1)}, bf16[4,32,512]{2,1,0:T(8,128)(2,1)S(1)}, u32[]{:S(2)}, u32[]{:S(2)}) %collective-permute-start.14) | collective-permute-done | bytes 131104 | tf_op jit(solution)/shard_map/ppermute | solution.py:129
  67.7 3.4 %collective-permute-done.18.refs_0_ = bf16[4,32,640]{2,1,0:T(8,128)(2,1)S(1)} collective-permute-done((bf16[4,32,640]{2,1,0:T(8,128)(2,1)S(1)}, bf16[4,32,640]{2,1,0:T(8,128)(2,1)S(1)}, u32[]{:S(2)}, u32[]{:S(2)}) %collective-permute-start.18) | collective-permute-done | bytes 163872 | tf_op jit(solution)/shard_map/ppermute | solution.py:134
  71.7 1.0 collective-permute-done.13.refs_2_
  73.2 6.1 %collective-permute-done.20.refs_2_ = bf16[4,32,512]{2,1,0:T(8,128)(2,1)S(1)} collective-permute-done((bf16[4,32,512]{2,1,0:T(8,128)(2,1)S(1)}, bf16[4,32,512]{2,1,0:T(8,128)(2,1)S(1)}, u32[]{:S(2)}, u32[]{:S(2)}) %collective-permute-start.20) | collective-permute-done | bytes 131104 | tf_op jit(solution)/shard_map/ppermute | solution.py:134
  79.3 3.1 %shard_map.130 = (bf16[32,2048]{1,0:T(8,128)(2,1)S(1)}, bf16[32,2048]{1,0:T(8,128)(2,1)S(1)}, bf16[32,2048]{1,0:T(8,128)(2,1)S(1)}, bf16[32,2048]{1,0:T(8,128)(2,1)S(1)}) custom-call(bf16[4,32,640]{2,1,0:T(8,128)(2,1)S(1)} %collective-permute-done.18.refs_0_, bf16[2,4,32,512]{3,2,1,0:T(8,128)(2,1)S(1)} %collective-permute-done.19.refs_1_, ...), custom_call_target="tpu_custom_call" | custom-call | flops 2415919104 | bytes 18874368 | tf_op jit(solution)/shard_map/pallas_call | solution.py:144
  83.1 1.5 %collective-permute-start.24 = (bf16[32,2048]{1,0:T(8,128)(2,1)S(1)}, bf16[32,2048]{1,0:T(8,128)(2,1)S(1)}, u32[]{:S(2)}, u32[]{:S(2)}) collective-permute-start(bf16[32,2048]{1,0:T(8,128)(2,1)S(1)} %get-tuple-element.47), channel_id=1, source_target_pairs={{0,2},{1,3},{2,0},{3,1},{4,6},{5,7},{6,4},{7,5},{8,10},{9,11},{10,... | collective-permute-start | bytes 393224 | tf_op jit(solution)/shard_map/ppermute | solution.py:134
  85.1 1.5 %collective-permute-start.21 = (bf16[32,2048]{1,0:T(8,128)(2,1)S(1)}, bf16[32,2048]{1,0:T(8,128)(2,1)S(1)}, u32[]{:S(2)}, u32[]{:S(2)}) collective-permute-start(bf16[32,2048]{1,0:T(8,128)(2,1)S(1)} %get-tuple-element.43), channel_id=1, source_target_pairs={{0,2},{1,3},{2,0},{3,1},{4,6},{5,7},{6,4},{7,5},{8,10},{9,11},{10,... | collective-permute-start | bytes 393224 | tf_op jit(solution)/shard_map/ppermute | solution.py:134
  86.6 3.1 %shard_map.129 = (f32[32,2048]{1,0:T(8,128)S(1)}, f32[32,2048]{1,0:T(8,128)S(1)}, f32[32,2048]{1,0:T(8,128)S(1)}, f32[32,2048]{1,0:T(8,128)S(1)}, bf16[32,2048]{1,0:T(8,128)(2,1)}) custom-call(bf16[4,32,640]{2,1,0:T(8,128)(2,1)S(1)} %get-tuple-element.38.refs_0_, bf16[4,32,512]{2,1,0:T(8,128)(2,1)S(1)} %collective-permute-done.12.refs_1_, ...), custom_call_target="tpu_custom_call" | custom-call | flops 2415919104 | bytes 18874368 | tf_op jit(solution)/shard_map/pallas_call | solution.py:144
  89.9 2.1 %collective-permute-start.25 = (bf16[32,2048]{1,0:T(8,128)(2,1)S(1)}, bf16[32,2048]{1,0:T(8,128)(2,1)S(1)}, u32[]{:S(2)}, u32[]{:S(2)}) collective-permute-start(bf16[32,2048]{1,0:T(8,128)(2,1)S(1)} %shard_map.132), channel_id=1, source_target_pairs={{0,12},{4,8},{12,0},{8,4},{1,13},{5,9},{13,1},{9,5},{2,14},{6,10},... | collective-permute-start | bytes 393224 | tf_op jit(solution)/shard_map/ppermute | solution.py:129
  92.1 1.2 %collective-permute-start.27 = (bf16[32,2048]{1,0:T(8,128)(2,1)S(1)}, bf16[32,2048]{1,0:T(8,128)(2,1)S(1)}, u32[]{:S(2)}, u32[]{:S(2)}) collective-permute-start(bf16[32,2048]{1,0:T(8,128)(2,1)S(1)} %shard_map.133), channel_id=1, source_target_pairs={{0,4},{4,12},{12,8},{8,0},{1,5},{5,13},{13,9},{9,1},{2,6},{6,14},{... | collective-permute-start | bytes 393224 | tf_op jit(solution)/shard_map/ppermute | solution.py:129
  93.2 1.6 %collective-permute-done.23 = bf16[32,2048]{1,0:T(8,128)(2,1)S(1)} collective-permute-done((bf16[32,2048]{1,0:T(8,128)(2,1)S(1)}, bf16[32,2048]{1,0:T(8,128)(2,1)S(1)}, u32[]{:S(2)}, u32[]{:S(2)}) %collective-permute-start.23) | collective-permute-done | bytes 131104 | tf_op jit(solution)/shard_map/ppermute | solution.py:129
  94.8 2.0 %collective-permute-done.25 = bf16[32,2048]{1,0:T(8,128)(2,1)S(1)} collective-permute-done((bf16[32,2048]{1,0:T(8,128)(2,1)S(1)}, bf16[32,2048]{1,0:T(8,128)(2,1)S(1)}, u32[]{:S(2)}, u32[]{:S(2)}) %collective-permute-start.25) | collective-permute-done | bytes 131104 | tf_op jit(solution)/shard_map/ppermute | solution.py:129
  96.8 2.3 %collective-permute-done.27 = bf16[32,2048]{1,0:T(8,128)(2,1)S(1)} collective-permute-done((bf16[32,2048]{1,0:T(8,128)(2,1)S(1)}, bf16[32,2048]{1,0:T(8,128)(2,1)S(1)}, u32[]{:S(2)}, u32[]{:S(2)}) %collective-permute-start.27) | collective-permute-done | bytes 131104 | tf_op jit(solution)/shard_map/ppermute | solution.py:129
  (44 shorter events, 10.3 us)
Async XLA Ops:
  0.6 78.7 %collective-permute-start.15 = (bf16[1,2048,768]{2,1,0:T(8,128)(2,1)}, bf16[1,2048,768]{2,1,0:T(8,128)(2,1)S(1)}, u32[]{:S(2)}, u32[]{:S(2)}) collective-permute-start(bf16[1,2048,768]{2,1,0:T(8,128)(2,1)} %refs_4_.1), channel_id=1, source_target_pairs={{0,1},{1,0},{2,3},{3,2},{4,5},{5,4},{6,7},{7,6},{8,9},{9,8},{10,11... | collective-permute-start | bytes 9437192 | tf_op jit(solution)/shard_map/ppermute | solution.py:134
  1.2 78.1 %collective-permute-start.16 = (bf16[1,2048,768]{2,1,0:T(8,128)(2,1)}, bf16[1,2048,768]{2,1,0:T(8,128)(2,1)S(1)}, u32[]{:S(2)}, u32[]{:S(2)}) collective-permute-start(bf16[1,2048,768]{2,1,0:T(8,128)(2,1)} %refs_5_.3), channel_id=1, source_target_pairs={{0,1},{1,0},{2,3},{3,2},{4,5},{5,4},{6,7},{7,6},{8,9},{9,8},{10,11... | collective-permute-start | bytes 9437192 | tf_op jit(solution)/shard_map/ppermute | solution.py:134
  1.3 78.0 %collective-permute-start.17 = (bf16[1,768,2048]{2,1,0:T(8,128)(2,1)}, bf16[1,768,2048]{2,1,0:T(8,128)(2,1)S(1)}, u32[]{:S(2)}, u32[]{:S(2)}) collective-permute-start(bf16[1,768,2048]{2,1,0:T(8,128)(2,1)} %refs_2_.1), channel_id=1, source_target_pairs={{0,1},{1,0},{2,3},{3,2},{4,5},{5,4},{6,7},{7,6},{8,9},{9,8},{10,11... | collective-permute-start | bytes 9437192 | tf_op jit(solution)/shard_map/ppermute | solution.py:134
  1.7 10.8 %collective-permute-start = (bf16[128,1024]{1,0:T(8,128)(2,1)}, bf16[128,1024]{1,0:T(8,128)(2,1)S(1)}, u32[]{:S(2)}, u32[]{:S(2)}) collective-permute-start(bf16[128,1024]{1,0:T(8,128)(2,1)} %refs_1_.1), channel_id=1, source_target_pairs={{0,4},{4,12},{12,8},{8,0},{1,5},{5,13},{13,9},{9,1},{2,6},{6,14},{... | collective-permute-start | bytes 786440 | tf_op jit(solution)/shard_map/ppermute | solution.py:129
  12.5 16.6 %collective-permute-start.1 = (bf16[128,1024]{1,0:T(8,128)(2,1)S(1)}, bf16[128,1024]{1,0:T(8,128)(2,1)S(1)}, u32[]{:S(2)}, u32[]{:S(2)}) collective-permute-start(bf16[128,1024]{1,0:T(8,128)(2,1)S(1)} %collective-permute-done.refs_1_), channel_id=1, source_target_pairs={{0,4},{4,12},{12,8},{8,0},{1,5},{5,13},{13,9},{9,1},{2,6},{6,14},{... | collective-permute-start | bytes 786440 | tf_op jit(solution)/shard_map/ppermute | solution.py:129
  14.2 8.6 %collective-permute-start.2 = (bf16[128,256]{1,0:T(8,128)(2,1)S(1)}, bf16[128,256]{1,0:T(8,128)(2,1)S(1)}, u32[]{:S(2)}, u32[]{:S(2)}) collective-permute-start(bf16[128,256]{1,0:T(8,128)(2,1)S(1)} %shard_map.123.refs_3_.refs_1_), channel_id=1, source_target_pairs={{0,4},{4,12},{12,8},{8,0},{1,5},{5,13},{13,9},{9,1},{2,6},{6,14},{... | collective-permute-start | bytes 196616 | tf_op jit(solution)/shard_map/ppermute | solution.py:129
  22.8 4.3 %collective-permute-start.4 = (bf16[128,256]{1,0:T(8,128)(2,1)S(1)}, bf16[128,256]{1,0:T(8,128)(2,1)S(1)}, u32[]{:S(2)}, u32[]{:S(2)}) collective-permute-start(bf16[128,256]{1,0:T(8,128)(2,1)S(1)} %shard_map.123.refs_3_.refs_1_), channel_id=1, source_target_pairs={{0,8},{4,0},{12,4},{8,12},{1,9},{5,1},{13,5},{9,13},{2,10},{6,2},{... | collective-permute-start | bytes 196616 | tf_op jit(solution)/shard_map/ppermute | solution.py:129
  27.1 6.3 %collective-permute-start.3 = (bf16[128,256]{1,0:T(8,128)(2,1)S(1)}, bf16[128,256]{1,0:T(8,128)(2,1)S(1)}, u32[]{:S(2)}, u32[]{:S(2)}) collective-permute-start(bf16[128,256]{1,0:T(8,128)(2,1)S(1)} %collective-permute-done.2.refs_4_.refs_2_), channel_id=1, source_target_pairs={{0,4},{4,12},{12,8},{8,0},{1,5},{5,13},{13,9},{9,1},{2,6},{6,14},{... | collective-permute-start | bytes 196616 | tf_op jit(solution)/shard_map/ppermute | solution.py:129
  29.0 8.4 %collective-permute-start.5 = (bf16[128,1024]{1,0:T(8,128)(2,1)S(1)}, bf16[128,1024]{1,0:T(8,128)(2,1)S(1)}, u32[]{:S(2)}, u32[]{:S(2)}) collective-permute-start(bf16[128,1024]{1,0:T(8,128)(2,1)S(1)} %collective-permute-done.1.refs_2_), channel_id=1, source_target_pairs={{0,4},{4,12},{12,8},{8,0},{1,5},{5,13},{13,9},{9,1},{2,6},{6,14},{... | collective-permute-start | bytes 786440 | tf_op jit(solution)/shard_map/ppermute | solution.py:129
  33.4 45.9 %copy-start = (bf16[1,2048,768]{2,1,0:T(8,128)(2,1)S(1)}, bf16[1,2048,768]{2,1,0:T(8,128)(2,1)}, u32[]{:S(2)}) copy-start(bf16[1,2048,768]{2,1,0:T(8,128)(2,1)} %refs_4_.1) | copy-start | bytes 9437188
  33.4 45.9 %copy-start.1 = (bf16[1,2048,768]{2,1,0:T(8,128)(2,1)S(1)}, bf16[1,2048,768]{2,1,0:T(8,128)(2,1)}, u32[]{:S(2)}) copy-start(bf16[1,2048,768]{2,1,0:T(8,128)(2,1)} %refs_5_.3) | copy-start | bytes 9437188
  33.4 45.9 %copy-start.2 = (f32[2048]{0:T(1024)S(1)}, f32[2048]{0:T(1024)}, u32[]{:S(2)}) copy-start(f32[2048]{0:T(1024)} %param.16) | copy-start | bytes 24580
  37.3 2.1 %collective-permute-start.6 = (bf16[3,2,32,512]{3,2,1,0:T(8,128)(2,1)S(1)}, bf16[3,2,32,512]{3,2,1,0:T(8,128)(2,1)S(1)}, u32[]{:S(2)}, u32[]{:S(2)}) collective-permute-start(bf16[3,2,32,512]{3,2,1,0:T(8,128)(2,1)S(1)} %get-tuple-element.30), channel_id=1, source_target_pairs={{0,1},{1,0},{2,3},{3,2},{4,5},{5,4},{6,7},{7,6},{8,9},{9,8},{10,11... | collective-permute-start | bytes 589832 | tf_op jit(solution)/shard_map/ppermute | solution.py:134
  38.8 1.5 %collective-permute-start.7 = (bf16[1,2,32,512]{3,2,1,0:T(8,128)(2,1)S(1)}, bf16[1,2,32,512]{3,2,1,0:T(8,128)(2,1)S(1)}, u32[]{:S(2)}, u32[]{:S(2)}) collective-permute-start(bf16[1,2,32,512]{3,2,1,0:T(8,128)(2,1)S(1)} %get-tuple-element.31), channel_id=1, source_target_pairs={{0,1},{1,0},{2,3},{3,2},{4,5},{5,4},{6,7},{7,6},{8,9},{9,8},{10,11... | collective-permute-start | bytes 196616 | tf_op jit(solution)/shard_map/ppermute | solution.py:134
  40.3 17.7 %collective-permute-start.8 = (bf16[4,32,512]{2,1,0:T(8,128)(2,1)S(1)}, bf16[4,32,512]{2,1,0:T(8,128)(2,1)S(1)}, u32[]{:S(2)}, u32[]{:S(2)}) collective-permute-start(bf16[4,32,512]{2,1,0:T(8,128)(2,1)S(1)} %get-tuple-element.33), channel_id=1, source_target_pairs={{0,2},{1,3},{2,0},{3,1},{4,6},{5,7},{6,4},{7,5},{8,10},{9,11},{10,... | collective-permute-start | bytes 393224 | tf_op jit(solution)/shard_map/ppermute | solution.py:134
  43.2 5.9 %collective-permute-start.10 = (bf16[32,640]{1,0:T(8,128)(2,1)S(1)}, bf16[32,640]{1,0:T(8,128)(2,1)S(1)}, u32[]{:S(2)}, u32[]{:S(2)}) collective-permute-start(bf16[32,640]{1,0:T(8,128)(2,1)S(1)} %get-tuple-element.36), channel_id=1, source_target_pairs={{0,12},{4,8},{12,0},{8,4},{1,13},{5,9},{13,1},{9,5},{2,14},{6,10},... | collective-permute-start | bytes 122888 | tf_op jit(solution)/shard_map/ppermute | solution.py:129
  49.1 4.0 %collective-permute-start.11 = (bf16[32,640]{1,0:T(8,128)(2,1)S(1)}, bf16[32,640]{1,0:T(8,128)(2,1)S(1)}, u32[]{:S(2)}, u32[]{:S(2)}) collective-permute-start(bf16[32,640]{1,0:T(8,128)(2,1)S(1)} %get-tuple-element.37), channel_id=1, source_target_pairs={{0,8},{4,0},{12,4},{8,12},{1,9},{5,1},{13,5},{9,13},{2,10},{6,2},{... | collective-permute-start | bytes 122888 | tf_op jit(solution)/shard_map/ppermute | solution.py:129
  53.1 4.9 %collective-permute-start.9 = (bf16[32,640]{1,0:T(8,128)(2,1)S(1)}, bf16[32,640]{1,0:T(8,128)(2,1)S(1)}, u32[]{:S(2)}, u32[]{:S(2)}) collective-permute-start(bf16[32,640]{1,0:T(8,128)(2,1)S(1)} %get-tuple-element.35), channel_id=1, source_target_pairs={{0,4},{4,12},{12,8},{8,0},{1,5},{5,13},{13,9},{9,1},{2,6},{6,14},{... | collective-permute-start | bytes 122888 | tf_op jit(solution)/shard_map/ppermute | solution.py:129
  58.1 6.0 %collective-permute-start.12 = (bf16[4,32,512]{2,1,0:T(8,128)(2,1)S(1)}, bf16[4,32,512]{2,1,0:T(8,128)(2,1)S(1)}, u32[]{:S(2)}, u32[]{:S(2)}) collective-permute-start(bf16[4,32,512]{2,1,0:T(8,128)(2,1)S(1)} %get-tuple-element.39), channel_id=1, source_target_pairs={{0,4},{4,12},{12,8},{8,0},{1,5},{5,13},{13,9},{9,1},{2,6},{6,14},{... | collective-permute-start | bytes 393224 | tf_op jit(solution)/shard_map/ppermute | solution.py:129
  58.4 8.3 %collective-permute-start.14 = (bf16[4,32,512]{2,1,0:T(8,128)(2,1)S(1)}, bf16[4,32,512]{2,1,0:T(8,128)(2,1)S(1)}, u32[]{:S(2)}, u32[]{:S(2)}) collective-permute-start(bf16[4,32,512]{2,1,0:T(8,128)(2,1)S(1)} %get-tuple-element.39), channel_id=1, source_target_pairs={{0,8},{4,0},{12,4},{8,12},{1,9},{5,1},{13,5},{9,13},{2,10},{6,2},{... | collective-permute-start | bytes 393224 | tf_op jit(solution)/shard_map/ppermute | solution.py:129
  64.1 7.1 %collective-permute-start.18 = (bf16[4,32,640]{2,1,0:T(8,128)(2,1)S(1)}, bf16[4,32,640]{2,1,0:T(8,128)(2,1)S(1)}, u32[]{:S(2)}, u32[]{:S(2)}) collective-permute-start(bf16[4,32,640]{2,1,0:T(8,128)(2,1)S(1)} %get-tuple-element.38.refs_0_), channel_id=1, source_target_pairs={{0,2},{1,3},{2,0},{3,1},{4,6},{5,7},{6,4},{7,5},{8,10},{9,11},{10,... | collective-permute-start | bytes 491528 | tf_op jit(solution)/shard_map/ppermute | solution.py:134
  66.8 5.9 %collective-permute-start.13 = (bf16[4,32,512]{2,1,0:T(8,128)(2,1)S(1)}, bf16[4,32,512]{2,1,0:T(8,128)(2,1)S(1)}, u32[]{:S(2)}, u32[]{:S(2)}) collective-permute-start(bf16[4,32,512]{2,1,0:T(8,128)(2,1)S(1)} %collective-permute-done.12.refs_1_), channel_id=1, source_target_pairs={{0,4},{4,12},{12,8},{8,0},{1,5},{5,13},{13,9},{9,1},{2,6},{6,14},{... | collective-permute-start | bytes 393224 | tf_op jit(solution)/shard_map/ppermute | solution.py:129
  71.1 8.2 %collective-permute-start.19 = (bf16[2,4,32,512]{3,2,1,0:T(8,128)(2,1)S(1)}, bf16[2,4,32,512]{3,2,1,0:T(8,128)(2,1)S(1)}, u32[]{:S(2)}, u32[]{:S(2)}) collective-permute-start(bf16[2,4,32,512]{3,2,1,0:T(8,128)(2,1)S(1)} %pad_maximum_fusion), channel_id=1, source_target_pairs={{0,2},{1,3},{2,0},{3,1},{4,6},{5,7},{6,4},{7,5},{8,10},{9,11},{10,... | collective-permute-start | bytes 786440 | tf_op jit(solution)/shard_map/ppermute | solution.py:134
  72.6 6.6 %collective-permute-start.20 = (bf16[4,32,512]{2,1,0:T(8,128)(2,1)S(1)}, bf16[4,32,512]{2,1,0:T(8,128)(2,1)S(1)}, u32[]{:S(2)}, u32[]{:S(2)}) collective-permute-start(bf16[4,32,512]{2,1,0:T(8,128)(2,1)S(1)} %collective-permute-done.13.refs_2_), channel_id=1, source_target_pairs={{0,2},{1,3},{2,0},{3,1},{4,6},{5,7},{6,4},{7,5},{8,10},{9,11},{10,... | collective-permute-start | bytes 393224 | tf_op jit(solution)/shard_map/ppermute | solution.py:134
  82.5 7.3 %collective-permute-start.22 = (bf16[32,2048]{1,0:T(8,128)(2,1)S(1)}, bf16[32,2048]{1,0:T(8,128)(2,1)S(1)}, u32[]{:S(2)}, u32[]{:S(2)}) collective-permute-start(bf16[32,2048]{1,0:T(8,128)(2,1)S(1)} %get-tuple-element.45), channel_id=1, source_target_pairs={{0,2},{1,3},{2,0},{3,1},{4,6},{5,7},{6,4},{7,5},{8,10},{9,11},{10,... | collective-permute-start | bytes 393224 | tf_op jit(solution)/shard_map/ppermute | solution.py:134
  83.1 6.8 %collective-permute-start.24 = (bf16[32,2048]{1,0:T(8,128)(2,1)S(1)}, bf16[32,2048]{1,0:T(8,128)(2,1)S(1)}, u32[]{:S(2)}, u32[]{:S(2)}) collective-permute-start(bf16[32,2048]{1,0:T(8,128)(2,1)S(1)} %get-tuple-element.47), channel_id=1, source_target_pairs={{0,2},{1,3},{2,0},{3,1},{4,6},{5,7},{6,4},{7,5},{8,10},{9,11},{10,... | collective-permute-start | bytes 393224 | tf_op jit(solution)/shard_map/ppermute | solution.py:134
  84.6 7.5 %collective-permute-start.26 = (bf16[32,2048]{1,0:T(8,128)(2,1)S(1)}, bf16[32,2048]{1,0:T(8,128)(2,1)S(1)}, u32[]{:S(2)}, u32[]{:S(2)}) collective-permute-start(bf16[32,2048]{1,0:T(8,128)(2,1)S(1)} %get-tuple-element.49), channel_id=1, source_target_pairs={{0,2},{1,3},{2,0},{3,1},{4,6},{5,7},{6,4},{7,5},{8,10},{9,11},{10,... | collective-permute-start | bytes 393224 | tf_op jit(solution)/shard_map/ppermute | solution.py:134
  85.1 8.1 %collective-permute-start.21 = (bf16[32,2048]{1,0:T(8,128)(2,1)S(1)}, bf16[32,2048]{1,0:T(8,128)(2,1)S(1)}, u32[]{:S(2)}, u32[]{:S(2)}) collective-permute-start(bf16[32,2048]{1,0:T(8,128)(2,1)S(1)} %get-tuple-element.43), channel_id=1, source_target_pairs={{0,2},{1,3},{2,0},{3,1},{4,6},{5,7},{6,4},{7,5},{8,10},{9,11},{10,... | collective-permute-start | bytes 393224 | tf_op jit(solution)/shard_map/ppermute | solution.py:134
  89.8 5.0 %collective-permute-start.23 = (bf16[32,2048]{1,0:T(8,128)(2,1)S(1)}, bf16[32,2048]{1,0:T(8,128)(2,1)S(1)}, u32[]{:S(2)}, u32[]{:S(2)}) collective-permute-start(bf16[32,2048]{1,0:T(8,128)(2,1)S(1)} %shard_map.131), channel_id=1, source_target_pairs={{0,8},{4,0},{12,4},{8,12},{1,9},{5,1},{13,5},{9,13},{2,10},{6,2},{... | collective-permute-start | bytes 393224 | tf_op jit(solution)/shard_map/ppermute | solution.py:129
  89.9 6.9 %collective-permute-start.25 = (bf16[32,2048]{1,0:T(8,128)(2,1)S(1)}, bf16[32,2048]{1,0:T(8,128)(2,1)S(1)}, u32[]{:S(2)}, u32[]{:S(2)}) collective-permute-start(bf16[32,2048]{1,0:T(8,128)(2,1)S(1)} %shard_map.132), channel_id=1, source_target_pairs={{0,12},{4,8},{12,0},{8,4},{1,13},{5,9},{13,1},{9,5},{2,14},{6,10},... | collective-permute-start | bytes 393224 | tf_op jit(solution)/shard_map/ppermute | solution.py:129
  92.1 7.1 %collective-permute-start.27 = (bf16[32,2048]{1,0:T(8,128)(2,1)S(1)}, bf16[32,2048]{1,0:T(8,128)(2,1)S(1)}, u32[]{:S(2)}, u32[]{:S(2)}) collective-permute-start(bf16[32,2048]{1,0:T(8,128)(2,1)S(1)} %shard_map.133), channel_id=1, source_target_pairs={{0,4},{4,12},{12,8},{8,0},{1,5},{5,13},{13,9},{9,1},{2,6},{6,14},{... | collective-permute-start | bytes 393224 | tf_op jit(solution)/shard_map/ppermute | solution.py:129

commit v4 on v3

--- a/solution.py
+++ b/solution.py
@@ -123,6 +123,17 @@
     return ring_at(jnp.bitwise_and(ring_at(c) - steps + n, n - 1))
 
 
+def across(x, mask):
+    n = lax.axis_size("ctx")
+    return lax.ppermute(x, "ctx", [(i, i ^ mask) for i in range(n)])
+
+
+def source(m, t):
+    n, c = lax.axis_size("ctx"), lax.axis_index("ctx")
+    other = jnp.bitwise_xor(c, m)
+    return other, jnp.bitwise_and(t - ring_at(c) + ring_at(other) + n, n - 1)
+
+
 def shift(x, by):
     n = lax.axis_size("ctx")
     pairs = [(ring_at(i), ring_at((i + by) % n)) for i in range(n)]
@@ -172,48 +183,57 @@
     return call(kernel, arrays, out, scratch, 0, 1 << 22, 8, range(n))
 
 
-def pair_kernel(k_ref, v_ref, out_ref, sems):
-    hd = k_ref.shape[1]
-    for copy in fetch(((k_ref, out_ref.at[:, :hd]), (v_ref, out_ref.at[:, hd:])), sems):
-        copy.wait()
-
-
-def pair(keys, values):
-    out = jax.ShapeDtypeStruct((keys.shape[0], 2 * keys.shape[1]), keys.dtype)
-    scratch = [pltpu.SemaphoreType.DMA((2,))]
-    return call(pair_kernel, (keys, values), [out], scratch, 0, 1 << 16, 2, (0, 1))[0]
-
-
-def parts_kernel(n_ctx, skip_in, route_in, gate_in, *refs):
-    out_refs, (skip_ref, route_ref, gate_ref, sems) = refs[:n_ctx], refs[n_ctx:]
-    copies = fetch(((skip_in, skip_ref), (route_in, route_ref), (gate_in, gate_ref)), sems)
+def pack_kernel(n_ctx, k_in, v_in, skip_in, route_in, gate_in, *refs):
+    out_refs, (k_ref, v_ref, skip_ref, route_ref, gate_ref, sems) = refs[:-6], refs[-6:]
+    kv_ref, part_refs = out_refs[0], out_refs[1:]
+    inputs = (k_in, v_in, skip_in, route_in, gate_in)
+    copies = fetch(tuple(zip(inputs, (k_ref, v_ref, skip_ref, route_ref, gate_ref))), sems)
     for copy in copies:
         copy.wait()
     gates = gate_ref[...].T
     routes = route_ref[...].T
     share = gates / jnp.sum(gates, axis=-1, keepdims=True)
     own_rows, dim = skip_ref.shape
-    cols = dim // n_ctx
     lanes = lax.broadcasted_iota(jnp.int32, (own_rows, 2 * LANES), 1)
     table = jnp.zeros((own_rows, 2 * LANES), jnp.float32)
     for k in range(gates.shape[1]):
         table += jnp.where(lanes % LANES == routes[:, k : k + 1], share[:, k : k + 1], 0.0)
     high = table.astype(jnp.bfloat16).astype(jnp.float32)
     packed = jnp.where(lanes < LANES, high, table - high).astype(jnp.bfloat16)
-    for s, out_ref in enumerate(out_refs):
-        at = pl.ds(pl.multiple_of(behind(-s) * cols, cols), cols)
-        out_ref[:, :cols] = skip_ref[:, at]
-        out_ref[:, cols:] = packed
-
-
-def make_parts(residual, routes, gates):
+    hd = HEAD_DIMENSION
+    kv_ref[:, :hd] = k_ref[...]
+    kv_ref[:, hd:] = v_ref[...]
+    rows = k_ref.shape[0]
+    for s, out_ref in enumerate(part_refs):
+        at = 0
+        if s % 2:
+            out_ref[:rows, :hd] = k_ref[...]
+            out_ref[:rows, hd:] = v_ref[...]
+            at = rows
+        first = behind(-s) * (dim // n_ctx)
+        for i in range(dim // n_ctx // (2 * hd)):
+            cols = pl.ds(pl.multiple_of(first + i * 2 * hd, 2 * hd), 2 * hd)
+            out_ref[at : at + own_rows, :] = skip_ref[:, cols]
+            at += own_rows
+        out_ref[at:, : 2 * LANES] = packed[: own_rows // 2]
+        out_ref[at:, 2 * LANES :] = packed[own_rows // 2 :]
+
+
+def part_rows(own_rows, cols):
+    return own_rows * cols // (2 * HEAD_DIMENSION) + own_rows // 2
+
+
+def pack(keys, values, residual, routes, gates):
     n_ctx = lax.axis_size("ctx")
     own_rows, dim = residual.shape
-    part = jax.ShapeDtypeStruct((own_rows, dim // n_ctx + 2 * LANES), jnp.bfloat16)
-    args = (residual, routes.T, gates.T)
-    scratch = [pltpu.VMEM(x.shape, x.dtype) for x in args] + [pltpu.SemaphoreType.DMA((3,))]
-    kernel = functools.partial(parts_kernel, n_ctx)
-    return call(kernel, args, [part] * n_ctx, scratch, 0, 1 << 18, 4, (0, 1, 2))
+    rows, width = keys.shape[0], 2 * HEAD_DIMENSION
+    extra = part_rows(own_rows, dim // n_ctx)
+    heights = [rows] + [extra + rows * (s % 2) for s in range(n_ctx)]
+    out = [jax.ShapeDtypeStruct((height, width), jnp.bfloat16) for height in heights]
+    args = (keys, values, residual, routes.T, gates.T)
+    scratch = [pltpu.VMEM(x.shape, x.dtype) for x in args] + [pltpu.SemaphoreType.DMA((5,))]
+    kernel = functools.partial(pack_kernel, n_ctx)
+    return call(kernel, args, out, scratch, 0, 1 << 18, 4, range(5))
 
 
 def attend_kernel(steps, splits, n_ctx, n_head, *refs):
@@ -230,8 +250,8 @@
     _, h = place()
     key_pos = []
     for m in range(n_ctx):
-        k_all[m * rows : (m + 1) * rows, :] = kv_refs[m][:, :hd]
-        v_all[m * rows : (m + 1) * rows, :] = kv_refs[m][:, hd:]
+        k_all[m * rows : (m + 1) * rows, :] = kv_refs[m][:rows, :hd]
+        v_all[m * rows : (m + 1) * rows, :] = kv_refs[m][:rows, hd:]
         key_pos.append(behind(m) * rows + lax.broadcasted_iota(jnp.int32, (rows, rows), 1))
     key_pos = jnp.concatenate(key_pos, axis=1)
     row_pos = lax.broadcasted_iota(jnp.int32, (rows, 1), 0)
@@ -313,13 +333,20 @@
 
 def combine_kernel(n_ctx, own_ref, got_ref, *refs):
     part_refs, (piece_ref, shared_ref) = refs[:n_ctx], refs[n_ctx:]
-    cols = piece_ref.shape[2]
-    for s in range(n_ctx):
+    own_rows, cols = piece_ref.shape[1:]
+    width = part_refs[0].shape[1]
+    for s, part_ref in enumerate(part_refs):
         total = own_ref[s] + got_ref[s].astype(jnp.float32)
-        block = (total + part_refs[s][:, :cols].astype(jnp.float32)).astype(jnp.bfloat16)
-        piece_ref[s] = block
-        shared_ref[s, :, :cols] = block
-        shared_ref[s, :, cols:] = part_refs[s][:, cols:]
+        at = part_ref.shape[0] - part_rows(own_rows, cols)
+        for first in range(0, cols, width):
+            here = slice(first, first + width)
+            skip = part_ref[at : at + own_rows, :].astype(jnp.float32)
+            block = (total[:, here] + skip).astype(jnp.bfloat16)
+            piece_ref[s, :, here] = block
+            shared_ref[s, :, here] = block
+            at += own_rows
+        shared_ref[s, : own_rows // 2, cols:] = part_ref[at:, : 2 * LANES]
+        shared_ref[s, own_rows // 2 :, cols:] = part_ref[at:, 2 * LANES :]
 
 
 def combine(own, got, parts):
@@ -332,53 +359,92 @@
     return call(kernel, (own, got, *parts), out_shape, [], 0, 1 << 20, 4)
 
 
-def expert_kernel(n_ctx, own, *refs):
+def scaled_piece(piece, m, gain_ref, x_ref):
+    n_ctx = piece.shape[0]
+    own_rows, cols = x_ref.shape[0] // n_ctx, x_ref.shape[1]
+    at = pl.ds(pl.multiple_of(source(m, 0)[0] * cols, cols), cols)
+    squares = []
+    for t in range(n_ctx):
+        block = piece[source(m, t)[1], :, :cols].astype(jnp.float32)
+        squares.append(jnp.sum(block * block, axis=-1, keepdims=True))
+        x_ref[t * own_rows : (t + 1) * own_rows, :] = (block * gain_ref[:, at]).astype(jnp.bfloat16)
+    return jnp.concatenate(squares, axis=0), at
+
+
+def begin_kernel(early, *refs):
+    pieces, (gain_ref, *weights) = refs[:-8], refs[-8:-3]
+    acc_ref, square_ref, x_ref = refs[-3:]
+    total = 0.0
+    rows_of = []
+    for k, (m, piece) in enumerate(zip(early, pieces)):
+        square, at = scaled_piece(piece, m, gain_ref, x_ref.at[k])
+        total += square
+        rows_of.append(at)
+    square_ref[...] = jnp.broadcast_to(total, square_ref.shape)
+    for i, weight in enumerate(weights):
+        acc = 0.0
+        for k, at in enumerate(rows_of):
+            acc += jnp.dot(x_ref[k], weight[0, at, :], preferred_element_type=jnp.float32)
+        acc_ref[i] = acc
+
+
+def begin(pieces, early, gain, weights):
+    n_ctx, own_rows, cols = pieces[1].shape
+    rows = n_ctx * own_rows
+    _, dim, hidden = weights[0].shape
+    args = (*pieces, gain, weights[0], weights[1], weights[3], weights[4])
+    out_shape = [
+        jax.ShapeDtypeStruct((4, rows, hidden), jnp.float32),
+        jax.ShapeDtypeStruct((rows, 2 * LANES), jnp.float32),
+    ]
+    scratch = [pltpu.VMEM((len(early), rows, cols), jnp.bfloat16)]
+    kernel = functools.partial(begin_kernel, early)
+    flops = 8 * rows * len(early) * cols * hidden
+    return call(kernel, args, out_shape, scratch, flops, 8 * dim * hidden, 24)
+
+
+def finish_kernel(late, n_ctx, own, *refs):
+    pieces, refs = refs[:n_ctx], refs[n_ctx:]
+    acc_ref, square_ref, gain_ref, *refs = refs
+    weights, refs = (refs[:3], refs[3:6]), refs[6:]
+    outs, (x_ref, out_ref, share_ref) = refs[:-3], refs[-3:]
+    cols = x_ref.shape[1]
+    own_rows = x_ref.shape[0] // n_ctx
+    c, h = place()
+    square, at = scaled_piece(pieces[late], late, gain_ref, x_ref)
+    root = lax.rsqrt((square + square_ref[:, :1]) / (cols * n_ctx) + 1e-06)
     if own:
-        pieces, refs = refs[:n_ctx], refs[n_ctx:]
-    else:
-        shared, near, far, *refs = refs
-        pieces = (shared, near.at[0], far, near.at[1])
-    gain_ref, refs = refs[0], refs[1:]
-    weights, refs = (refs[:3], refs[3:6]), refs[6:]
-    outs, (x_ref, acc_ref, share_ref) = refs[:-3], refs[-3:]
-    own_rows, cols = pieces[2].shape[1:]
-    c, h = place()
-
+        for m in range(n_ctx):
+            column, place_0 = source(m, 0)
+            here = pl.ds(pl.multiple_of(column * cols, cols), cols)
+            outs[-1][:, here] = pieces[m][place_0, :, :cols]
     for t in range(n_ctx):
-        blocks = []
-        square = jnp.zeros((own_rows, 1), jnp.float32)
-        for m in range(n_ctx):
-            block = pieces[m][(t - m) % n_ctx, :, :cols]
-            block_f = block.astype(jnp.float32)
-            square += jnp.sum(block_f * block_f, axis=-1, keepdims=True)
-            at = pl.ds(pl.multiple_of(behind(m) * cols, cols), cols)
-            blocks.append((block_f, at))
-            if own and t == 0:
-                outs[-1][:, at] = block
-        root = lax.rsqrt(square / (cols * n_ctx) + 1e-06)
         here = slice(t * own_rows, (t + 1) * own_rows)
-        for block_f, at in blocks:
-            x_ref[here, at] = (block_f * root * gain_ref[:, at]).astype(jnp.bfloat16)
         share_ref[here, :] = pieces[0][t, :, cols:].astype(jnp.float32)
-
     lanes = lax.broadcasted_iota(jnp.int32, share_ref.shape, 1) % LANES
     for i, (gate_ref, up_ref, down_ref) in enumerate(weights):
         expert = c * lax.axis_size("head") + jnp.bitwise_xor(h, i)
         share = jnp.sum(jnp.where(lanes == expert, share_ref[...], 0.0), axis=-1, keepdims=True)
-        gate = jnp.dot(x_ref[...], gate_ref[0], preferred_element_type=jnp.float32)
-        up = jnp.dot(x_ref[...], up_ref[0], preferred_element_type=jnp.float32)
+        gate, up = (
+            (
+                acc_ref[2 * i + k]
+                + jnp.dot(x_ref[...], ref[0, at, :], preferred_element_type=jnp.float32)
+            )
+            * root
+            for k, ref in enumerate((gate_ref, up_ref))
+        )
         hidden = (gate * jax.nn.sigmoid(gate) * up).astype(jnp.bfloat16)
         out = jnp.dot(hidden, down_ref[0], preferred_element_type=jnp.float32) * share
         if i == 0:
-            acc_ref[...] = out
+            out_ref[...] = out
         else:
-            total = (acc_ref[...] + out).astype(outs[0].dtype)
+            total = (out_ref[...] + out).astype(outs[0].dtype)
             for t in range(n_ctx):
                 outs[t][...] = total[t * own_rows : (t + 1) * own_rows, :]
 
 
-def experts(pieces, gain, weights, own):
-    n_ctx, own_rows, _ = pieces[0].shape
+def finish(pieces, late, begun, gain, weights, own):
+    n_ctx, own_rows, cols = pieces[1].shape
     _, dim, hidden = weights[0].shape
     rows = own_rows * n_ctx
     out = jax.ShapeDtypeStruct((own_rows, dim), jnp.float32 if own else jnp.bfloat16)
@@ -386,13 +452,13 @@
     if own:
         out_shape.append(jax.ShapeDtypeStruct((own_rows, dim), jnp.bfloat16))
     scratch = [
-        pltpu.VMEM((rows, dim), jnp.bfloat16),
+        pltpu.VMEM((rows, cols), jnp.bfloat16),
         pltpu.VMEM((rows, dim), jnp.float32),
         pltpu.VMEM((rows, 2 * LANES), jnp.float32),
     ]
-    args = (*pieces, gain.reshape(1, -1), *weights)
-    kernel = functools.partial(expert_kernel, n_ctx, own)
-    flops = 12 * rows * dim * hidden
+    args = (*pieces, *begun, gain, *weights)
+    kernel = functools.partial(finish_kernel, late, n_ctx, own)
+    flops = 4 * rows * hidden * (2 * cols + dim)
     return call(kernel, args, out_shape, scratch, flops, 12 * dim * hidden, 28)
 
 
@@ -408,11 +474,9 @@
     q_list = [query]
     for _ in range(3):
         q_list.append(shift(q_list[-1], 1))
-    kv = pair(keys, values)
-    kv_back = shift(kv, 1)
-    kv_list = [kv, kv_back, shift(kv_back, 1), shift(kv, 3)]
-    parts = make_parts(residual, routes, gates)
+    kv, *parts = pack(keys, values, residual, routes, gates)
     parts = [parts[0]] + [shift(parts[s], s) for s in (1, 2, 3)]
+    kv_list = [kv, parts[1], shift(parts[1][: kv.shape[0]], 1), parts[3]]
 
     weights = [w_gate, w_up, w_down]
     weights += [swap(w, 1) for w in weights]
@@ -424,13 +488,16 @@
     gots = [swap(x, 1) for x in sends]
     own, send = halve(keeps, gots)
     piece, shared = combine(own, swap(send, 2), parts)
-    back, ahead = shift(piece, 1), shift(piece, 3)
-    pieces = [shared, back, shift(back, 1), ahead]
-    sides = swap(jnp.stack([back, ahead]), 2)
-    other_pieces = [swap(shared, 2), sides, swap(pieces[2], 2)]
-
-    *own_out, mixed = experts(pieces, gain, weights, True)
-    other_out = experts(other_pieces, gain, weights, False)
+    pieces = [shared, across(piece, 1), across(piece, 2)]
+    pieces.append(across(pieces[2], 1))
+    other_pieces = [swap(x, 2) for x in pieces]
+
+    gain = gain.reshape(1, -1)
+    early, late = (0, 1, 2), 3
+    own_begun = begin(pieces[:late], early, gain, weights)
+    *own_out, mixed = finish(pieces, late, own_begun, gain, weights, True)
+    other_begun = begin(other_pieces[:late], early, gain, weights)
+    other_out = finish(other_pieces, late, other_begun, gain, weights, False)
 
     got = [swap(x, 2) for x in other_out]
     result = own_out[0] + got[0].astype(jnp.float32)
@@ -446,6 +513,7 @@
     n_ctx, n_head = lax.axis_size("ctx"), lax.axis_size("head")
     dense = slots_per_expert(own_rows, routes.shape[1], n_ctx * n_head) == own_rows
     dense = dense and n_ctx == 4 and n_head == 4 and (dim // n_ctx) % (2 * HEAD_DIMENSION) == 0
+    dense = dense and 4 * LANES == 2 * HEAD_DIMENSION and own_rows % 32 == 0
     dense = dense and args[1].shape[1] == HEAD_DIMENSION and n_ctx * n_head <= LANES
     if not dense:
         return sparse_body(*args)

time: 100 us -> 93.8 us (0.938)
  waiting for transfers between devices: 50.5 us -> 45.2 us
    ppermute x15 -> x10, waiting for transfers between devices: 40 us -> 27.5 us  [shift(): return lax.ppermute(x, 'ctx', pairs)]
    ppermute x0 -> x3, waiting for transfers between devices: none -> 7.29 us  [across(): return lax.ppermute(x, 'ctx', [(i, i ^ mask) for i in range(n)])]
    ppermute x15 -> x10, starting transfers between devices: 22.7 us -> 16.7 us  [shift(): return lax.ppermute(x, 'ctx', pairs)]
    ppermute x0 -> x3, starting transfers between devices: none -> 2.96 us  [across(): return lax.ppermute(x, 'ctx', [(i, i ^ mask) for i in range(n)])]
    ppermute x13 -> x14, starting transfers between devices: 8.95 us -> 11.5 us  [swap(): return lax.ppermute(x, 'head', [(i, i ^ mask) for i in range(n)])]
    pallas_call x12 -> x13, Pallas kernels: 16.2 us -> 15.6 us  [call(): pl.pallas_call(kernel, out_shape=out_shape, in_specs=[away if i in fetche...]
    ppermute x13 -> x14, waiting for transfers between devices: 10.5 us -> 10.4 us  [swap(): return lax.ppermute(x, 'head', [(i, i ^ mask) for i in range(n)])]
  transfers between devices with their start and end apart: 28 -> 27, of which waited for: 15 -> 15; matrix products, arithmetic and copies ran while one was open for 0% -> 0% of each run, Pallas kernels for 13% -> 15%
where the time goes in v4:
time: 93.8 us; the launch traced here: 93.7 us
  waiting for transfers between devices  45.2 us (48%)
  starting transfers between devices  31.2 us (33%)
  Pallas kernels  15.6 us (17%)
    ppermute x10, waiting for transfers between devices, shift(): return lax.ppermute(x, 'ctx', pairs)  27.5 us
    ppermute x10, starting transfers between devices, shift(): return lax.ppermute(x, 'ctx', pairs)  16.7 us
    pallas_call x13, Pallas kernels, call(): pl.pallas_call(kernel, out_shape=out_shape, in_specs=[away if i in fetche...  15.6 us
    ppermute x14, starting transfers between devices, swap(): return lax.ppermute(x, 'head', [(i, i ^ mask) for i in range(n)])  11.5 us
    ppermute x14, waiting for transfers between devices, swap(): return lax.ppermute(x, 'head', [(i, i ^ mask) for i in range(n)])  10.4 us
    ppermute x3, waiting for transfers between devices, across(): return lax.ppermute(x, 'ctx', [(i, i ^ mask) for i in range(n)])  7.29 us
    ppermute x3, starting transfers between devices, across(): return lax.ppermute(x, 'ctx', [(i, i ^ mask) for i in range(n)])  2.96 us
  transfers between devices with their start and end apart: 27, of which 15 were waited for; matrix products, arithmetic and copies ran while one was open for 0% of the time, Pallas kernels for 15%

profile of v4, /device:TPU:0, one launch (start us, length us, event | category | flops | bytes accessed | tf_op | source)
XLA Modules:
  0.0 93.7 jit_solution(17041521683804838302)
XLA Ops:
  1.7 2.6 %collective-permute-start = (bf16[128,1024]{1,0:T(8,128)(2,1)}, bf16[128,1024]{1,0:T(8,128)(2,1)S(1)}, u32[]{:S(2)}, u32[]{:S(2)}) collective-permute-start(bf16[128,1024]{1,0:T(8,128)(2,1)} %refs_1_.1), channel_id=1, source_target_pairs={{0,4},{4,12},{12,8},{8,0},{1,5},{5,13},{13,9},{9,1},{2,6},{6,14},{... | collective-permute-start | bytes 786440 | tf_op jit(solution)/shard_map/ppermute | solution.py:140
  4.3 8.1 %collective-permute-done.refs_1_ = bf16[128,1024]{1,0:T(8,128)(2,1)S(1)} collective-permute-done((bf16[128,1024]{1,0:T(8,128)(2,1)}, bf16[128,1024]{1,0:T(8,128)(2,1)S(1)}, u32[]{:S(2)}, u32[]{:S(2)}) %collective-permute-start) | collective-permute-done | bytes 262176 | tf_op jit(solution)/shard_map/ppermute | solution.py:140
  13.4 1.4 %shard_map.123 = (bf16[128,256]{1,0:T(8,128)(2,1)S(1)}, bf16[80,256]{1,0:T(8,128)(2,1)S(1)}, bf16[208,256]{1,0:T(8,128)(2,1)S(1)}, bf16[80,256]{1,0:T(8,128)(2,1)S(1)}, bf16[208,256]{1,0:T(8,128)(2,1)S(1)}) custom-call(bf16[128,128]{1,0:T(8,128)(2,1)} %k_in.1, bf16[128,128]{1,0:T(8,128)(2,1)} %v_in.1, bf16[32,2048]{1,0:T(8,128)(2,1)} %skip_in.1, ...), custom_call_target="tpu_custom_call" | custom-call | bytes 262144 | tf_op jit(solution)/shard_map/pallas_call | solution.py:155
  14.8 3.3 %collective-permute-start.2 = (bf16[208,256]{1,0:T(8,128)(2,1)S(1)}, bf16[208,256]{1,0:T(8,128)(2,1)S(1)}, u32[]{:S(2)}, u32[]{:S(2)}) collective-permute-start(bf16[208,256]{1,0:T(8,128)(2,1)S(1)} %get-tuple-element.33), channel_id=1, source_target_pairs={{0,4},{4,12},{12,8},{8,0},{1,5},{5,13},{13,9},{9,1},{2,6},{6,14},{... | collective-permute-start | bytes 319496 | tf_op jit(solution)/shard_map/ppermute | solution.py:140
  18.1 5.6 %collective-permute-done.2.refs_4_.refs_2_.refs_1_ = bf16[208,256]{1,0:T(8,128)(2,1)S(1)} collective-permute-done((bf16[208,256]{1,0:T(8,128)(2,1)S(1)}, bf16[208,256]{1,0:T(8,128)(2,1)S(1)}, u32[]{:S(2)}, u32[]{:S(2)}) %collective-permute-start.2) | collective-permute-done | bytes 106528 | tf_op jit(solution)/shard_map/ppermute | solution.py:140
  23.7 1.3 %collective-permute-start.4 = (bf16[208,256]{1,0:T(8,128)(2,1)S(1)}, bf16[208,256]{1,0:T(8,128)(2,1)S(1)}, u32[]{:S(2)}, u32[]{:S(2)}) collective-permute-start(bf16[208,256]{1,0:T(8,128)(2,1)S(1)} %get-tuple-element.34), channel_id=1, source_target_pairs={{0,8},{4,0},{12,4},{8,12},{1,9},{5,1},{13,5},{9,13},{2,10},{6,2},{... | collective-permute-start | bytes 319496 | tf_op jit(solution)/shard_map/ppermute | solution.py:140
  25.0 3.4 %collective-permute-done.4.refs_6_.refs_4_.refs_3_ = bf16[208,256]{1,0:T(8,128)(2,1)S(1)} collective-permute-done((bf16[208,256]{1,0:T(8,128)(2,1)S(1)}, bf16[208,256]{1,0:T(8,128)(2,1)S(1)}, u32[]{:S(2)}, u32[]{:S(2)}) %collective-permute-start.4) | collective-permute-done | bytes 106528 | tf_op jit(solution)/shard_map/ppermute | solution.py:140
  28.4 1.9 %collective-permute-start.3 = (bf16[128,256]{1,0:T(8,128)(2,1)S(1)}, bf16[128,256]{1,0:T(8,128)(2,1)S(1)}, u32[]{:S(2)}, u32[]{:S(2)}) collective-permute-start(bf16[128,256]{1,0:T(8,128)(2,1)S(1)} %slice.4), channel_id=1, source_target_pairs={{0,4},{4,12},{12,8},{8,0},{1,5},{5,13},{13,9},{9,1},{2,6},{6,14},{... | collective-permute-start | bytes 196616 | tf_op jit(solution)/shard_map/ppermute | solution.py:140
  30.3 2.0 %collective-permute-start.5 = (bf16[128,1024]{1,0:T(8,128)(2,1)S(1)}, bf16[128,1024]{1,0:T(8,128)(2,1)S(1)}, u32[]{:S(2)}, u32[]{:S(2)}) collective-permute-start(bf16[128,1024]{1,0:T(8,128)(2,1)S(1)} %collective-permute-done.1.refs_2_), channel_id=1, source_target_pairs={{0,4},{4,12},{12,8},{8,0},{1,5},{5,13},{13,9},{9,1},{2,6},{6,14},{... | collective-permute-start | bytes 786440 | tf_op jit(solution)/shard_map/ppermute | solution.py:140
  32.4 2.3 %shard_map.122 = (bf16[1024,512]{1,0:T(8,128)(2,1)S(1)}, bf16[128,1024]{1,0:T(8,128)(2,1)S(1)}, bf16[1,768,2048]{2,1,0:T(8,128)(2,1)S(1)}) custom-call(bf16[1024,512]{1,0:T(8,128)(2,1)} %refs_0_.1, bf16[128,1024]{1,0:T(8,128)(2,1)} %refs_1_.1, bf16[1,768,2048]{2,1,0:T(8,128)(2,1)} %refs_2_.1), custom_call_target="tpu_custom_call" | custom-call | bytes 4194304 | tf_op jit(solution)/shard_map/pallas_call | solution.py:155
  34.7 3.9 %shard_map.124 = (f32[3,2,32,512]{3,2,1,0:T(8,128)S(1)}, bf16[3,2,32,512]{3,2,1,0:T(8,128)(2,1)S(1)}) custom-call(bf16[128,1024]{1,0:T(8,128)(2,1)S(1)} %get-tuple-element.31.refs_0_, bf16[128,1024]{1,0:T(8,128)(2,1)S(1)} %collective-permute-done.refs_1_, bf16[128,1024]{1,0:T(8,128)(2,1)S(1)} %collective-permute-done.1.refs_2_, ...), custom_call_target="tpu_custom_call" | custom-call | flops 1207959552 | bytes 1048576 | tf_op jit(solution)/shard_map/pallas_call | solution.py:155
  38.7 1.4 %shard_map.125 = (f32[1,2,32,512]{3,2,1,0:T(8,128)S(1)}, bf16[1,2,32,512]{3,2,1,0:T(8,128)(2,1)S(1)}) custom-call(bf16[128,1024]{1,0:T(8,128)(2,1)S(1)} %collective-permute-done.5.refs_0_, bf16[128,256]{1,0:T(8,128)(2,1)S(1)} %get-tuple-element.32.refs_3_.refs_1_, bf16[208,256]{1,0:T(8,128)(2,1)S(1)} %collective-permute-done.2.refs_4_.refs_2_.refs_1_, ...), custom_call_target="tpu_custom_call" | custom-call | flops 402653184 | bytes 1048576 | tf_op jit(solution)/shard_map/pallas_call | solution.py:155
  41.7 1.6 %collective-permute-start.8 = (bf16[4,32,512]{2,1,0:T(8,128)(2,1)S(1)}, bf16[4,32,512]{2,1,0:T(8,128)(2,1)S(1)}, u32[]{:S(2)}, u32[]{:S(2)}) collective-permute-start(bf16[4,32,512]{2,1,0:T(8,128)(2,1)S(1)} %get-tuple-element.41), channel_id=1, source_target_pairs={{0,2},{1,3},{2,0},{3,1},{4,6},{5,7},{6,4},{7,5},{8,10},{9,11},{10,... | collective-permute-start | bytes 393224 | tf_op jit(solution)/shard_map/ppermute | solution.py:145
  43.2 2.3 %collective-permute-start.9 = (bf16[80,256]{1,0:T(8,128)(2,1)S(1)}, bf16[80,256]{1,0:T(8,128)(2,1)S(1)}, u32[]{:S(2)}, u32[]{:S(2)}) collective-permute-start(bf16[80,256]{1,0:T(8,128)(2,1)S(1)} %get-tuple-element.43), channel_id=1, source_target_pairs={{0,12},{4,8},{12,0},{8,4},{1,13},{5,9},{13,1},{9,5},{2,14},{6,10},... | collective-permute-start | bytes 122888 | tf_op jit(solution)/shard_map/ppermute | solution.py:140
  45.6 3.5 %collective-permute-done.9.refs_2_ = bf16[80,256]{1,0:T(8,128)(2,1)S(1)} collective-permute-done((bf16[80,256]{1,0:T(8,128)(2,1)S(1)}, bf16[80,256]{1,0:T(8,128)(2,1)S(1)}, u32[]{:S(2)}, u32[]{:S(2)}) %collective-permute-start.9) | collective-permute-done | bytes 40992 | tf_op jit(solution)/shard_map/ppermute | solution.py:140
  49.2 2.9 %collective-permute-start.10 = (bf16[4,32,512]{2,1,0:T(8,128)(2,1)S(1)}, bf16[4,32,512]{2,1,0:T(8,128)(2,1)S(1)}, u32[]{:S(2)}, u32[]{:S(2)}) collective-permute-start(bf16[4,32,512]{2,1,0:T(8,128)(2,1)S(1)} %get-tuple-element.45), channel_id=1, source_target_pairs={{0,4},{4,0},{8,12},{12,8},{1,5},{5,1},{9,13},{13,9},{2,6},{6,2},{1... | collective-permute-start | bytes 393224 | tf_op jit(solution)/shard_map/ppermute | solution.py:128
  52.0 4.8 %collective-permute-done.11.refs_2_ = bf16[4,32,512]{2,1,0:T(8,128)(2,1)S(1)} collective-permute-done((bf16[4,32,512]{2,1,0:T(8,128)(2,1)S(1)}, bf16[4,32,512]{2,1,0:T(8,128)(2,1)S(1)}, u32[]{:S(2)}, u32[]{:S(2)}) %collective-permute-start.11) | collective-permute-done | bytes 131104 | tf_op jit(solution)/shard_map/ppermute | solution.py:128
  57.8 1.1 %collective-permute-start.18 = (bf16[4,32,512]{2,1,0:T(8,128)(2,1)S(1)}, bf16[4,32,512]{2,1,0:T(8,128)(2,1)S(1)}, u32[]{:S(2)}, u32[]{:S(2)}) collective-permute-start(bf16[4,32,512]{2,1,0:T(8,128)(2,1)S(1)} %collective-permute-done.11.refs_2_), channel_id=1, source_target_pairs={{0,2},{1,3},{2,0},{3,1},{4,6},{5,7},{6,4},{7,5},{8,10},{9,11},{10,... | collective-permute-start | bytes 393224 | tf_op jit(solution)/shard_map/ppermute | solution.py:145
  58.9 4.9 %collective-permute-done.16.refs_0_ = bf16[4,32,640]{2,1,0:T(8,128)(2,1)S(1)} collective-permute-done((bf16[4,32,640]{2,1,0:T(8,128)(2,1)S(1)}, bf16[4,32,640]{2,1,0:T(8,128)(2,1)S(1)}, u32[]{:S(2)}, u32[]{:S(2)}) %collective-permute-start.16) | collective-permute-done | bytes 163872 | tf_op jit(solution)/shard_map/ppermute | solution.py:145
  63.8 1.4 %collective-permute-done.18.refs_2_ = bf16[4,32,512]{2,1,0:T(8,128)(2,1)S(1)} collective-permute-done((bf16[4,32,512]{2,1,0:T(8,128)(2,1)S(1)}, bf16[4,32,512]{2,1,0:T(8,128)(2,1)S(1)}, u32[]{:S(2)}, u32[]{:S(2)}) %collective-permute-start.18) | collective-permute-done | bytes 131104 | tf_op jit(solution)/shard_map/ppermute | solution.py:145
  65.2 1.1 %collective-permute-start.17 = (bf16[4,32,512]{2,1,0:T(8,128)(2,1)S(1)}, bf16[4,32,512]{2,1,0:T(8,128)(2,1)S(1)}, u32[]{:S(2)}, u32[]{:S(2)}) collective-permute-start(bf16[4,32,512]{2,1,0:T(8,128)(2,1)S(1)} %collective-permute-done.10.refs_1_), channel_id=1, source_target_pairs={{0,2},{1,3},{2,0},{3,1},{4,6},{5,7},{6,4},{7,5},{8,10},{9,11},{10,... | collective-permute-start | bytes 393224 | tf_op jit(solution)/shard_map/ppermute | solution.py:145
  66.4 2.5 %collective-permute-done.12.refs_3_ = bf16[4,32,512]{2,1,0:T(8,128)(2,1)S(1)} collective-permute-done((bf16[4,32,512]{2,1,0:T(8,128)(2,1)S(1)}, bf16[4,32,512]{2,1,0:T(8,128)(2,1)S(1)}, u32[]{:S(2)}, u32[]{:S(2)}) %collective-permute-start.12) | collective-permute-done | bytes 131104 | tf_op jit(solution)/shard_map/ppermute | solution.py:128
  70.7 1.5 %shard_map.130 = (f32[4,128,768]{2,1,0:T(8,128)S(1)}, f32[128,128]{1,0:T(8,128)S(1)}) custom-call(bf16[4,32,640]{2,1,0:T(8,128)(2,1)S(1)} %collective-permute-done.16.refs_0_, bf16[4,32,512]{2,1,0:T(8,128)(2,1)S(1)} %collective-permute-done.17.refs_1_, bf16[4,32,512]{2,1,0:T(8,128)(2,1)S(1)} %collective-permute-done.18.refs_2_, f32[1,2048]{1,0:T(1,128)S(1)} %bitcast.3, ...), custom_call_target="tpu_custom_call" | custom-call | flops 1207959552 | bytes 12582912 | tf_op jit(solution)/shard_map/pallas_call | solution.py:155
  72.1 1.6 %collective-permute-done.19.refs_3_ = bf16[4,32,512]{2,1,0:T(8,128)(2,1)S(1)} collective-permute-done((bf16[4,32,512]{2,1,0:T(8,128)(2,1)S(1)}, bf16[4,32,512]{2,1,0:T(8,128)(2,1)S(1)}, u32[]{:S(2)}, u32[]{:S(2)}) %collective-permute-start.19) | collective-permute-done | bytes 131104 | tf_op jit(solution)/shard_map/ppermute | solution.py:145
  73.8 1.7 %shard_map.131 = (bf16[32,2048]{1,0:T(8,128)(2,1)S(1)}, bf16[32,2048]{1,0:T(8,128)(2,1)S(1)}, bf16[32,2048]{1,0:T(8,128)(2,1)S(1)}, bf16[32,2048]{1,0:T(8,128)(2,1)S(1)}) custom-call(bf16[4,32,640]{2,1,0:T(8,128)(2,1)S(1)} %collective-permute-done.16.refs_0_, bf16[4,32,512]{2,1,0:T(8,128)(2,1)S(1)} %collective-permute-done.17.refs_1_, ...), custom_call_target="tpu_custom_call" | custom-call | flops 1207959552 | bytes 18874368 | tf_op jit(solution)/shard_map/pallas_call | solution.py:155
  75.5 1.1 %collective-permute-start.20 = (bf16[32,2048]{1,0:T(8,128)(2,1)S(1)}, bf16[32,2048]{1,0:T(8,128)(2,1)S(1)}, u32[]{:S(2)}, u32[]{:S(2)}) collective-permute-start(bf16[32,2048]{1,0:T(8,128)(2,1)S(1)} %get-tuple-element.53), channel_id=1, source_target_pairs={{0,2},{1,3},{2,0},{3,1},{4,6},{5,7},{6,4},{7,5},{8,10},{9,11},{10,... | collective-permute-start | bytes 393224 | tf_op jit(solution)/shard_map/ppermute | solution.py:145
  79.7 1.4 %shard_map.128 = (f32[4,128,768]{2,1,0:T(8,128)S(1)}, f32[128,128]{1,0:T(8,128)S(1)}) custom-call(bf16[4,32,640]{2,1,0:T(8,128)(2,1)S(1)} %get-tuple-element.44.refs_0_, bf16[4,32,512]{2,1,0:T(8,128)(2,1)S(1)} %collective-permute-done.10.refs_1_, bf16[4,32,512]{2,1,0:T(8,128)(2,1)S(1)} %collective-permute-done.11.refs_2_, f32[1,2048]{1,0:T(1,128)S(1)} %bitcast.5, ...), custom_call_target="tpu_custom_call" | custom-call | flops 1207959552 | bytes 12582912 | tf_op jit(solution)/shard_map/pallas_call | solution.py:155
  81.1 1.8 %shard_map.129 = (f32[32,2048]{1,0:T(8,128)S(1)}, f32[32,2048]{1,0:T(8,128)S(1)}, f32[32,2048]{1,0:T(8,128)S(1)}, f32[32,2048]{1,0:T(8,128)S(1)}, bf16[32,2048]{1,0:T(8,128)(2,1)}) custom-call(bf16[4,32,640]{2,1,0:T(8,128)(2,1)S(1)} %get-tuple-element.44.refs_0_, bf16[4,32,512]{2,1,0:T(8,128)(2,1)S(1)} %collective-permute-done.10.refs_1_, ...), custom_call_target="tpu_custom_call" | custom-call | flops 1207959552 | bytes 18874368 | tf_op jit(solution)/shard_map/pallas_call | solution.py:155
  84.1 1.8 %collective-permute-start.24 = (bf16[32,2048]{1,0:T(8,128)(2,1)S(1)}, bf16[32,2048]{1,0:T(8,128)(2,1)S(1)}, u32[]{:S(2)}, u32[]{:S(2)}) collective-permute-start(bf16[32,2048]{1,0:T(8,128)(2,1)S(1)} %shard_map.133), channel_id=1, source_target_pairs={{0,12},{4,8},{12,0},{8,4},{1,13},{5,9},{13,1},{9,5},{2,14},{6,10},... | collective-permute-start | bytes 393224 | tf_op jit(solution)/shard_map/ppermute | solution.py:140
  86.0 2.0 %collective-permute-done.22 = bf16[32,2048]{1,0:T(8,128)(2,1)S(1)} collective-permute-done((bf16[32,2048]{1,0:T(8,128)(2,1)S(1)}, bf16[32,2048]{1,0:T(8,128)(2,1)S(1)}, u32[]{:S(2)}, u32[]{:S(2)}) %collective-permute-start.22) | collective-permute-done | bytes 131104 | tf_op jit(solution)/shard_map/ppermute | solution.py:140
  88.0 3.1 %collective-permute-done.24 = bf16[32,2048]{1,0:T(8,128)(2,1)S(1)} collective-permute-done((bf16[32,2048]{1,0:T(8,128)(2,1)S(1)}, bf16[32,2048]{1,0:T(8,128)(2,1)S(1)}, u32[]{:S(2)}, u32[]{:S(2)}) %collective-permute-start.24) | collective-permute-done | bytes 131104 | tf_op jit(solution)/shard_map/ppermute | solution.py:140
  91.0 1.9 %collective-permute-done.26 = bf16[32,2048]{1,0:T(8,128)(2,1)S(1)} collective-permute-done((bf16[32,2048]{1,0:T(8,128)(2,1)S(1)}, bf16[32,2048]{1,0:T(8,128)(2,1)S(1)}, u32[]{:S(2)}, u32[]{:S(2)}) %collective-permute-start.26) | collective-permute-done | bytes 131104 | tf_op jit(solution)/shard_map/ppermute | solution.py:140
  (43 shorter events, 11.5 us)
Async XLA Ops:
  0.6 70.0 %collective-permute-start.13 = (bf16[1,2048,768]{2,1,0:T(8,128)(2,1)}, bf16[1,2048,768]{2,1,0:T(8,128)(2,1)S(1)}, u32[]{:S(2)}, u32[]{:S(2)}) collective-permute-start(bf16[1,2048,768]{2,1,0:T(8,128)(2,1)} %refs_7_.3), channel_id=1, source_target_pairs={{0,1},{1,0},{2,3},{3,2},{4,5},{5,4},{6,7},{7,6},{8,9},{9,8},{10,11... | collective-permute-start | bytes 9437192 | tf_op jit(solution)/shard_map/ppermute | solution.py:145
  1.2 69.5 %collective-permute-start.14 = (bf16[1,2048,768]{2,1,0:T(8,128)(2,1)}, bf16[1,2048,768]{2,1,0:T(8,128)(2,1)S(1)}, u32[]{:S(2)}, u32[]{:S(2)}) collective-permute-start(bf16[1,2048,768]{2,1,0:T(8,128)(2,1)} %refs_8_.3), channel_id=1, source_target_pairs={{0,1},{1,0},{2,3},{3,2},{4,5},{5,4},{6,7},{7,6},{8,9},{9,8},{10,11... | collective-permute-start | bytes 9437192 | tf_op jit(solution)/shard_map/ppermute | solution.py:145
  1.3 72.5 %collective-permute-start.15 = (bf16[1,768,2048]{2,1,0:T(8,128)(2,1)}, bf16[1,768,2048]{2,1,0:T(8,128)(2,1)S(1)}, u32[]{:S(2)}, u32[]{:S(2)}) collective-permute-start(bf16[1,768,2048]{2,1,0:T(8,128)(2,1)} %refs_2_.1), channel_id=1, source_target_pairs={{0,1},{1,0},{2,3},{3,2},{4,5},{5,4},{6,7},{7,6},{8,9},{9,8},{10,11... | collective-permute-start | bytes 9437192 | tf_op jit(solution)/shard_map/ppermute | solution.py:145
  1.7 10.8 %collective-permute-start = (bf16[128,1024]{1,0:T(8,128)(2,1)}, bf16[128,1024]{1,0:T(8,128)(2,1)S(1)}, u32[]{:S(2)}, u32[]{:S(2)}) collective-permute-start(bf16[128,1024]{1,0:T(8,128)(2,1)} %refs_1_.1), channel_id=1, source_target_pairs={{0,4},{4,12},{12,8},{8,0},{1,5},{5,13},{13,9},{9,1},{2,6},{6,14},{... | collective-permute-start | bytes 786440 | tf_op jit(solution)/shard_map/ppermute | solution.py:140
  12.5 17.9 %collective-permute-start.1 = (bf16[128,1024]{1,0:T(8,128)(2,1)S(1)}, bf16[128,1024]{1,0:T(8,128)(2,1)S(1)}, u32[]{:S(2)}, u32[]{:S(2)}) collective-permute-start(bf16[128,1024]{1,0:T(8,128)(2,1)S(1)} %collective-permute-done.refs_1_), channel_id=1, source_target_pairs={{0,4},{4,12},{12,8},{8,0},{1,5},{5,13},{13,9},{9,1},{2,6},{6,14},{... | collective-permute-start | bytes 786440 | tf_op jit(solution)/shard_map/ppermute | solution.py:140
  14.8 8.9 %collective-permute-start.2 = (bf16[208,256]{1,0:T(8,128)(2,1)S(1)}, bf16[208,256]{1,0:T(8,128)(2,1)S(1)}, u32[]{:S(2)}, u32[]{:S(2)}) collective-permute-start(bf16[208,256]{1,0:T(8,128)(2,1)S(1)} %get-tuple-element.33), channel_id=1, source_target_pairs={{0,4},{4,12},{12,8},{8,0},{1,5},{5,13},{13,9},{9,1},{2,6},{6,14},{... | collective-permute-start | bytes 319496 | tf_op jit(solution)/shard_map/ppermute | solution.py:140
  23.7 4.7 %collective-permute-start.4 = (bf16[208,256]{1,0:T(8,128)(2,1)S(1)}, bf16[208,256]{1,0:T(8,128)(2,1)S(1)}, u32[]{:S(2)}, u32[]{:S(2)}) collective-permute-start(bf16[208,256]{1,0:T(8,128)(2,1)S(1)} %get-tuple-element.34), channel_id=1, source_target_pairs={{0,8},{4,0},{12,4},{8,12},{1,9},{5,1},{13,5},{9,13},{2,10},{6,2},{... | collective-permute-start | bytes 319496 | tf_op jit(solution)/shard_map/ppermute | solution.py:140
  28.4 6.3 %collective-permute-start.3 = (bf16[128,256]{1,0:T(8,128)(2,1)S(1)}, bf16[128,256]{1,0:T(8,128)(2,1)S(1)}, u32[]{:S(2)}, u32[]{:S(2)}) collective-permute-start(bf16[128,256]{1,0:T(8,128)(2,1)S(1)} %slice.4), channel_id=1, source_target_pairs={{0,4},{4,12},{12,8},{8,0},{1,5},{5,13},{13,9},{9,1},{2,6},{6,14},{... | collective-permute-start | bytes 196616 | tf_op jit(solution)/shard_map/ppermute | solution.py:140
  30.3 8.4 %collective-permute-start.5 = (bf16[128,1024]{1,0:T(8,128)(2,1)S(1)}, bf16[128,1024]{1,0:T(8,128)(2,1)S(1)}, u32[]{:S(2)}, u32[]{:S(2)}) collective-permute-start(bf16[128,1024]{1,0:T(8,128)(2,1)S(1)} %collective-permute-done.1.refs_2_), channel_id=1, source_target_pairs={{0,4},{4,12},{12,8},{8,0},{1,5},{5,13},{13,9},{9,1},{2,6},{6,14},{... | collective-permute-start | bytes 786440 | tf_op jit(solution)/shard_map/ppermute | solution.py:140
  34.7 36.0 %copy-start = (bf16[1,2048,768]{2,1,0:T(8,128)(2,1)S(1)}, bf16[1,2048,768]{2,1,0:T(8,128)(2,1)}, u32[]{:S(2)}) copy-start(bf16[1,2048,768]{2,1,0:T(8,128)(2,1)} %refs_7_.3) | copy-start | bytes 9437188
  34.7 36.0 %copy-start.1 = (bf16[1,2048,768]{2,1,0:T(8,128)(2,1)S(1)}, bf16[1,2048,768]{2,1,0:T(8,128)(2,1)}, u32[]{:S(2)}) copy-start(bf16[1,2048,768]{2,1,0:T(8,128)(2,1)} %refs_8_.3) | copy-start | bytes 9437188
  34.7 36.0 %copy-start.2 = (f32[2048]{0:T(1024)S(1)}, f32[2048]{0:T(1024)}, u32[]{:S(2)}) copy-start(f32[2048]{0:T(1024)} %param.16) | copy-start | bytes 24580
  38.6 2.1 %collective-permute-start.6 = (bf16[3,2,32,512]{3,2,1,0:T(8,128)(2,1)S(1)}, bf16[3,2,32,512]{3,2,1,0:T(8,128)(2,1)S(1)}, u32[]{:S(2)}, u32[]{:S(2)}) collective-permute-start(bf16[3,2,32,512]{3,2,1,0:T(8,128)(2,1)S(1)} %get-tuple-element.38), channel_id=1, source_target_pairs={{0,1},{1,0},{2,3},{3,2},{4,5},{5,4},{6,7},{7,6},{8,9},{9,8},{10,11... | collective-permute-start | bytes 589832 | tf_op jit(solution)/shard_map/ppermute | solution.py:145
  40.2 1.5 %collective-permute-start.7 = (bf16[1,2,32,512]{3,2,1,0:T(8,128)(2,1)S(1)}, bf16[1,2,32,512]{3,2,1,0:T(8,128)(2,1)S(1)}, u32[]{:S(2)}, u32[]{:S(2)}) collective-permute-start(bf16[1,2,32,512]{3,2,1,0:T(8,128)(2,1)S(1)} %get-tuple-element.39), channel_id=1, source_target_pairs={{0,1},{1,0},{2,3},{3,2},{4,5},{5,4},{6,7},{7,6},{8,9},{9,8},{10,11... | collective-permute-start | bytes 196616 | tf_op jit(solution)/shard_map/ppermute | solution.py:145
  41.7 7.4 %collective-permute-start.8 = (bf16[4,32,512]{2,1,0:T(8,128)(2,1)S(1)}, bf16[4,32,512]{2,1,0:T(8,128)(2,1)S(1)}, u32[]{:S(2)}, u32[]{:S(2)}) collective-permute-start(bf16[4,32,512]{2,1,0:T(8,128)(2,1)S(1)} %get-tuple-element.41), channel_id=1, source_target_pairs={{0,2},{1,3},{2,0},{3,1},{4,6},{5,7},{6,4},{7,5},{8,10},{9,11},{10,... | collective-permute-start | bytes 393224 | tf_op jit(solution)/shard_map/ppermute | solution.py:145
  43.2 5.8 %collective-permute-start.9 = (bf16[80,256]{1,0:T(8,128)(2,1)S(1)}, bf16[80,256]{1,0:T(8,128)(2,1)S(1)}, u32[]{:S(2)}, u32[]{:S(2)}) collective-permute-start(bf16[80,256]{1,0:T(8,128)(2,1)S(1)} %get-tuple-element.43), channel_id=1, source_target_pairs={{0,12},{4,8},{12,0},{8,4},{1,13},{5,9},{13,1},{9,5},{2,14},{6,10},... | collective-permute-start | bytes 122888 | tf_op jit(solution)/shard_map/ppermute | solution.py:140
  49.1 7.8 %collective-permute-start.11 = (bf16[4,32,512]{2,1,0:T(8,128)(2,1)S(1)}, bf16[4,32,512]{2,1,0:T(8,128)(2,1)S(1)}, u32[]{:S(2)}, u32[]{:S(2)}) collective-permute-start(bf16[4,32,512]{2,1,0:T(8,128)(2,1)S(1)} %get-tuple-element.45), channel_id=1, source_target_pairs={{0,8},{4,12},{8,0},{12,4},{1,9},{5,13},{9,1},{13,5},{2,10},{6,14},... | collective-permute-start | bytes 393224 | tf_op jit(solution)/shard_map/ppermute | solution.py:128
  49.2 8.7 %collective-permute-start.10 = (bf16[4,32,512]{2,1,0:T(8,128)(2,1)S(1)}, bf16[4,32,512]{2,1,0:T(8,128)(2,1)S(1)}, u32[]{:S(2)}, u32[]{:S(2)}) collective-permute-start(bf16[4,32,512]{2,1,0:T(8,128)(2,1)S(1)} %get-tuple-element.45), channel_id=1, source_target_pairs={{0,4},{4,0},{8,12},{12,8},{1,5},{5,1},{9,13},{13,9},{2,6},{6,2},{1... | collective-permute-start | bytes 393224 | tf_op jit(solution)/shard_map/ppermute | solution.py:128
  56.9 7.0 %collective-permute-start.16 = (bf16[4,32,640]{2,1,0:T(8,128)(2,1)S(1)}, bf16[4,32,640]{2,1,0:T(8,128)(2,1)S(1)}, u32[]{:S(2)}, u32[]{:S(2)}) collective-permute-start(bf16[4,32,640]{2,1,0:T(8,128)(2,1)S(1)} %get-tuple-element.44.refs_0_), channel_id=1, source_target_pairs={{0,2},{1,3},{2,0},{3,1},{4,6},{5,7},{6,4},{7,5},{8,10},{9,11},{10,... | collective-permute-start | bytes 491528 | tf_op jit(solution)/shard_map/ppermute | solution.py:145
  57.8 7.4 %collective-permute-start.18 = (bf16[4,32,512]{2,1,0:T(8,128)(2,1)S(1)}, bf16[4,32,512]{2,1,0:T(8,128)(2,1)S(1)}, u32[]{:S(2)}, u32[]{:S(2)}) collective-permute-start(bf16[4,32,512]{2,1,0:T(8,128)(2,1)S(1)} %collective-permute-done.11.refs_2_), channel_id=1, source_target_pairs={{0,2},{1,3},{2,0},{3,1},{4,6},{5,7},{6,4},{7,5},{8,10},{9,11},{10,... | collective-permute-start | bytes 393224 | tf_op jit(solution)/shard_map/ppermute | solution.py:145
  63.8 5.0 %collective-permute-start.12 = (bf16[4,32,512]{2,1,0:T(8,128)(2,1)S(1)}, bf16[4,32,512]{2,1,0:T(8,128)(2,1)S(1)}, u32[]{:S(2)}, u32[]{:S(2)}) collective-permute-start(bf16[4,32,512]{2,1,0:T(8,128)(2,1)S(1)} %collective-permute-done.11.refs_2_), channel_id=1, source_target_pairs={{0,4},{4,0},{8,12},{12,8},{1,5},{5,1},{9,13},{13,9},{2,6},{6,2},{1... | collective-permute-start | bytes 393224 | tf_op jit(solution)/shard_map/ppermute | solution.py:128
  65.2 5.4 %collective-permute-start.17 = (bf16[4,32,512]{2,1,0:T(8,128)(2,1)S(1)}, bf16[4,32,512]{2,1,0:T(8,128)(2,1)S(1)}, u32[]{:S(2)}, u32[]{:S(2)}) collective-permute-start(bf16[4,32,512]{2,1,0:T(8,128)(2,1)S(1)} %collective-permute-done.10.refs_1_), channel_id=1, source_target_pairs={{0,2},{1,3},{2,0},{3,1},{4,6},{5,7},{6,4},{7,5},{8,10},{9,11},{10,... | collective-permute-start | bytes 393224 | tf_op jit(solution)/shard_map/ppermute | solution.py:145
  68.8 5.0 %collective-permute-start.19 = (bf16[4,32,512]{2,1,0:T(8,128)(2,1)S(1)}, bf16[4,32,512]{2,1,0:T(8,128)(2,1)S(1)}, u32[]{:S(2)}, u32[]{:S(2)}) collective-permute-start(bf16[4,32,512]{2,1,0:T(8,128)(2,1)S(1)} %collective-permute-done.12.refs_3_), channel_id=1, source_target_pairs={{0,2},{1,3},{2,0},{3,1},{4,6},{5,7},{6,4},{7,5},{8,10},{9,11},{10,... | collective-permute-start | bytes 393224 | tf_op jit(solution)/shard_map/ppermute | solution.py:145
  75.5 10.4 %collective-permute-start.20 = (bf16[32,2048]{1,0:T(8,128)(2,1)S(1)}, bf16[32,2048]{1,0:T(8,128)(2,1)S(1)}, u32[]{:S(2)}, u32[]{:S(2)}) collective-permute-start(bf16[32,2048]{1,0:T(8,128)(2,1)S(1)} %get-tuple-element.53), channel_id=1, source_target_pairs={{0,2},{1,3},{2,0},{3,1},{4,6},{5,7},{6,4},{7,5},{8,10},{9,11},{10,... | collective-permute-start | bytes 393224 | tf_op jit(solution)/shard_map/ppermute | solution.py:145
  76.6 6.3 %collective-permute-start.21 = (bf16[32,2048]{1,0:T(8,128)(2,1)S(1)}, bf16[32,2048]{1,0:T(8,128)(2,1)S(1)}, u32[]{:S(2)}, u32[]{:S(2)}) collective-permute-start(bf16[32,2048]{1,0:T(8,128)(2,1)S(1)} %get-tuple-element.55), channel_id=1, source_target_pairs={{0,2},{1,3},{2,0},{3,1},{4,6},{5,7},{6,4},{7,5},{8,10},{9,11},{10,... | collective-permute-start | bytes 393224 | tf_op jit(solution)/shard_map/ppermute | solution.py:145
  77.6 6.4 %collective-permute-start.23 = (bf16[32,2048]{1,0:T(8,128)(2,1)S(1)}, bf16[32,2048]{1,0:T(8,128)(2,1)S(1)}, u32[]{:S(2)}, u32[]{:S(2)}) collective-permute-start(bf16[32,2048]{1,0:T(8,128)(2,1)S(1)} %get-tuple-element.57), channel_id=1, source_target_pairs={{0,2},{1,3},{2,0},{3,1},{4,6},{5,7},{6,4},{7,5},{8,10},{9,11},{10,... | collective-permute-start | bytes 393224 | tf_op jit(solution)/shard_map/ppermute | solution.py:145
  78.7 7.2 %collective-permute-start.25 = (bf16[32,2048]{1,0:T(8,128)(2,1)S(1)}, bf16[32,2048]{1,0:T(8,128)(2,1)S(1)}, u32[]{:S(2)}, u32[]{:S(2)}) collective-permute-start(bf16[32,2048]{1,0:T(8,128)(2,1)S(1)} %get-tuple-element.59), channel_id=1, source_target_pairs={{0,2},{1,3},{2,0},{3,1},{4,6},{5,7},{6,4},{7,5},{8,10},{9,11},{10,... | collective-permute-start | bytes 393224 | tf_op jit(solution)/shard_map/ppermute | solution.py:145
  82.9 5.0 %collective-permute-start.22 = (bf16[32,2048]{1,0:T(8,128)(2,1)S(1)}, bf16[32,2048]{1,0:T(8,128)(2,1)S(1)}, u32[]{:S(2)}, u32[]{:S(2)}) collective-permute-start(bf16[32,2048]{1,0:T(8,128)(2,1)S(1)} %shard_map.132), channel_id=1, source_target_pairs={{0,8},{4,0},{12,4},{8,12},{1,9},{5,1},{13,5},{9,13},{2,10},{6,2},{... | collective-permute-start | bytes 393224 | tf_op jit(solution)/shard_map/ppermute | solution.py:140
  84.1 6.9 %collective-permute-start.24 = (bf16[32,2048]{1,0:T(8,128)(2,1)S(1)}, bf16[32,2048]{1,0:T(8,128)(2,1)S(1)}, u32[]{:S(2)}, u32[]{:S(2)}) collective-permute-start(bf16[32,2048]{1,0:T(8,128)(2,1)S(1)} %shard_map.133), channel_id=1, source_target_pairs={{0,12},{4,8},{12,0},{8,4},{1,13},{5,9},{13,1},{9,5},{2,14},{6,10},... | collective-permute-start | bytes 393224 | tf_op jit(solution)/shard_map/ppermute | solution.py:140
  85.9 7.0 %collective-permute-start.26 = (bf16[32,2048]{1,0:T(8,128)(2,1)S(1)}, bf16[32,2048]{1,0:T(8,128)(2,1)S(1)}, u32[]{:S(2)}, u32[]{:S(2)}) collective-permute-start(bf16[32,2048]{1,0:T(8,128)(2,1)S(1)} %shard_map.134), channel_id=1, source_target_pairs={{0,4},{4,12},{12,8},{8,0},{1,5},{5,13},{13,9},{9,1},{2,6},{6,14},{... | collective-permute-start | bytes 393224 | tf_op jit(solution)/shard_map/ppermute | solution.py:140

commit v5 on v4

--- a/solution.py
+++ b/solution.py
@@ -1,4 +1,5 @@
 import functools
+import math
 
 import jax
 import jax.numpy as jnp
@@ -130,8 +131,8 @@
 
 def source(m, t):
     n, c = lax.axis_size("ctx"), lax.axis_index("ctx")
-    other = jnp.bitwise_xor(c, m)
-    return other, jnp.bitwise_and(t - ring_at(c) + ring_at(other) + n, n - 1)
+    other, owner = jnp.bitwise_xor(c, m), jnp.bitwise_xor(c, t)
+    return other, jnp.bitwise_and(ring_at(other) - ring_at(owner) + n, n - 1)
 
 
 def shift(x, by):
@@ -271,7 +272,7 @@
             ).reshape(together, rows, -1)
             scores = jnp.where(visible[None], scores, -1e30)
             top = jnp.max(scores, axis=-1, keepdims=True)
-            weights = jnp.exp((scores - top) * scale)
+            weights = jnp.exp2((scores - top) * (scale * math.log2(math.e)))
             total = jnp.sum(weights, axis=-1, keepdims=True)
             summed = jnp.dot(
                 weights.astype(jnp.bfloat16).reshape(together * rows, -1),
@@ -312,31 +313,26 @@
     return call(kernel, args, out_shape, scratch, flops, 2 * q_cols * out_cols, 16)
 
 
-def halve_kernel(n, *refs):
-    keeps, gots, (own_ref, send_ref) = refs[:n], refs[n : 2 * n], refs[2 * n :]
-    at = 0
-    for keep, got in zip(keeps, gots):
-        here = slice(at, at + keep.shape[0])
-        total = keep[...] + got[...].astype(jnp.float32)
-        own_ref[here] = total[:, 0]
-        send_ref[here] = total[:, 1].astype(jnp.bfloat16)
-        at += keep.shape[0]
-
-
-def halve(keeps, gots):
-    n_blocks = sum(x.shape[0] for x in keeps)
-    shape = (n_blocks, *keeps[0].shape[2:])
+def halve_kernel(keep_ref, got_ref, own_ref, send_ref):
+    total = keep_ref[...] + got_ref[...].astype(jnp.float32)
+    own_ref[...] = total[:, 0]
+    send_ref[...] = total[:, 1].astype(jnp.bfloat16)
+
+
+def halve(keep, got):
+    shape = (keep.shape[0], *keep.shape[2:])
     out_shape = [jax.ShapeDtypeStruct(shape, t) for t in (jnp.float32, jnp.bfloat16)]
-    kernel = functools.partial(halve_kernel, len(keeps))
-    return call(kernel, (*keeps, *gots), out_shape, [], 0, 1 << 20, 6)
-
-
-def combine_kernel(n_ctx, own_ref, got_ref, *refs):
+    return call(halve_kernel, (keep, got), out_shape, [], 0, 1 << 20, 6)
+
+
+def combine_kernel(n_ctx, n, *refs):
+    owns, gots, refs = refs[:n], refs[n : 2 * n], refs[2 * n :]
     part_refs, (piece_ref, shared_ref) = refs[:n_ctx], refs[n_ctx:]
     own_rows, cols = piece_ref.shape[1:]
     width = part_refs[0].shape[1]
-    for s, part_ref in enumerate(part_refs):
-        total = own_ref[s] + got_ref[s].astype(jnp.float32)
+    blocks = [(own, got, i) for own, got in zip(owns, gots) for i in range(own.shape[0])]
+    for s, ((own, got, i), part_ref) in enumerate(zip(blocks, part_refs)):
+        total = own[i] + got[i].astype(jnp.float32)
         at = part_ref.shape[0] - part_rows(own_rows, cols)
         for first in range(0, cols, width):
             here = slice(first, first + width)
@@ -349,14 +345,15 @@
         shared_ref[s, own_rows // 2 :, cols:] = part_ref[at:, 2 * LANES :]
 
 
-def combine(own, got, parts):
-    n_ctx, own_rows, cols = own.shape
+def combine(owns, gots, parts):
+    n_ctx = len(parts)
+    _, own_rows, cols = owns[0].shape
     out_shape = [
         jax.ShapeDtypeStruct((n_ctx, own_rows, cols), jnp.bfloat16),
         jax.ShapeDtypeStruct((n_ctx, own_rows, cols + 2 * LANES), jnp.bfloat16),
     ]
-    kernel = functools.partial(combine_kernel, n_ctx)
-    return call(kernel, (own, got, *parts), out_shape, [], 0, 1 << 20, 4)
+    kernel = functools.partial(combine_kernel, n_ctx, len(owns))
+    return call(kernel, (*owns, *gots, *parts), out_shape, [], 0, 1 << 20, 4)
 
 
 def scaled_piece(piece, m, gain_ref, x_ref):
@@ -420,7 +417,7 @@
             outs[-1][:, here] = pieces[m][place_0, :, :cols]
     for t in range(n_ctx):
         here = slice(t * own_rows, (t + 1) * own_rows)
-        share_ref[here, :] = pieces[0][t, :, cols:].astype(jnp.float32)
+        share_ref[here, :] = pieces[0][source(0, t)[1], :, cols:].astype(jnp.float32)
     lanes = lax.broadcasted_iota(jnp.int32, share_ref.shape, 1) % LANES
     for i, (gate_ref, up_ref, down_ref) in enumerate(weights):
         expert = c * lax.axis_size("head") + jnp.bitwise_xor(h, i)
@@ -485,9 +482,12 @@
     first = attend((0, 1, 2), q_list[:3], kv_list, o_weight)
     last = attend((3,), q_list[3:], kv_list, o_weight)
     keeps, sends = zip(first, last)
-    gots = [swap(x, 1) for x in sends]
-    own, send = halve(keeps, gots)
-    piece, shared = combine(own, swap(send, 2), parts)
+    owns, gots = [], []
+    for keep, send in zip(keeps, sends):
+        own, send = halve(keep, swap(send, 1))
+        owns.append(own)
+        gots.append(swap(send, 2))
+    piece, shared = combine(owns, gots, parts)
     pieces = [shared, across(piece, 1), across(piece, 2)]
     pieces.append(across(pieces[2], 1))
     other_pieces = [swap(x, 2) for x in pieces]
@@ -502,7 +502,7 @@
     got = [swap(x, 2) for x in other_out]
     result = own_out[0] + got[0].astype(jnp.float32)
     for t in (1, 2, 3):
-        total = shift(add(own_out[t], got[t]), -t)
+        total = across(add(own_out[t], got[t]), t)
         result = result + total.astype(jnp.float32)
     return (mixed, result.astype(jnp.bfloat16))
 

time: 93.8 us -> 96.3 us (1.027)
  starting transfers between devices: 31.2 us -> 32.6 us
  waiting for transfers between devices: 45.2 us -> 46.4 us
    ppermute x10 -> x7, waiting for transfers between devices: 27.5 us -> 20.5 us  [shift(): return lax.ppermute(x, 'ctx', pairs)]
    ppermute x3 -> x6, starting transfers between devices: 2.96 us -> 7.21 us  [across(): return lax.ppermute(x, 'ctx', [(i, i ^ mask) for i in range(n)])]
    ppermute x14 -> x15, waiting for transfers between devices: 10.4 us -> 14.6 us  [swap(): return lax.ppermute(x, 'head', [(i, i ^ mask) for i in range(n)])]
    ppermute x3 -> x6, waiting for transfers between devices: 7.29 us -> 11.2 us  [across(): return lax.ppermute(x, 'ctx', [(i, i ^ mask) for i in range(n)])]
    ppermute x10 -> x7, starting transfers between devices: 16.7 us -> 14.5 us  [shift(): return lax.ppermute(x, 'ctx', pairs)]
    ppermute x14 -> x15, starting transfers between devices: 11.5 us -> 10.9 us  [swap(): return lax.ppermute(x, 'head', [(i, i ^ mask) for i in range(n)])]
    pallas_call x13 -> x14, Pallas kernels: 15.6 us -> 15.5 us  [call(): pl.pallas_call(kernel, out_shape=out_shape, in_specs=[away if i in fetche...]
  transfers between devices with their start and end apart: 27 -> 28, of which waited for: 15 -> 15; matrix products, arithmetic and copies ran while one was open for 0% -> 0% of each run, Pallas kernels for 15% -> 14%
where the time goes in v5:
time: 96.3 us; the launch traced here: 96.1 us
  waiting for transfers between devices  46.4 us (48%)
  starting transfers between devices  32.6 us (34%)
  Pallas kernels  15.5 us (16%)
    ppermute x7, waiting for transfers between devices, shift(): return lax.ppermute(x, 'ctx', pairs)  20.5 us
    pallas_call x14, Pallas kernels, call(): pl.pallas_call(kernel, out_shape=out_shape, in_specs=[away if i in fetche...  15.5 us
    ppermute x15, waiting for transfers between devices, swap(): return lax.ppermute(x, 'head', [(i, i ^ mask) for i in range(n)])  14.6 us
    ppermute x7, starting transfers between devices, shift(): return lax.ppermute(x, 'ctx', pairs)  14.5 us
    ppermute x6, waiting for transfers between devices, across(): return lax.ppermute(x, 'ctx', [(i, i ^ mask) for i in range(n)])  11.2 us
    ppermute x15, starting transfers between devices, swap(): return lax.ppermute(x, 'head', [(i, i ^ mask) for i in range(n)])  10.9 us
    ppermute x6, starting transfers between devices, across(): return lax.ppermute(x, 'ctx', [(i, i ^ mask) for i in range(n)])  7.21 us
  transfers between devices with their start and end apart: 28, of which 15 were waited for; matrix products, arithmetic and copies ran while one was open for 0% of the time, Pallas kernels for 14%

profile of v5, /device:TPU:0, one launch (start us, length us, event | category | flops | bytes accessed | tf_op | source)
XLA Modules:
  0.0 96.1 jit_solution(860162482707264991)
XLA Ops:
  1.7 2.6 %collective-permute-start = (bf16[128,1024]{1,0:T(8,128)(2,1)}, bf16[128,1024]{1,0:T(8,128)(2,1)S(1)}, u32[]{:S(2)}, u32[]{:S(2)}) collective-permute-start(bf16[128,1024]{1,0:T(8,128)(2,1)} %refs_1_.1), channel_id=1, source_target_pairs={{0,4},{4,12},{12,8},{8,0},{1,5},{5,13},{13,9},{9,1},{2,6},{6,14},{... | collective-permute-start | bytes 786440 | tf_op jit(solution)/shard_map/ppermute | solution.py:141
  4.3 8.1 %collective-permute-done.refs_1_ = bf16[128,1024]{1,0:T(8,128)(2,1)S(1)} collective-permute-done((bf16[128,1024]{1,0:T(8,128)(2,1)}, bf16[128,1024]{1,0:T(8,128)(2,1)S(1)}, u32[]{:S(2)}, u32[]{:S(2)}) %collective-permute-start) | collective-permute-done | bytes 262176 | tf_op jit(solution)/shard_map/ppermute | solution.py:141
  13.4 1.4 %shard_map.123 = (bf16[128,256]{1,0:T(8,128)(2,1)S(1)}, bf16[80,256]{1,0:T(8,128)(2,1)S(1)}, bf16[208,256]{1,0:T(8,128)(2,1)S(1)}, bf16[80,256]{1,0:T(8,128)(2,1)S(1)}, bf16[208,256]{1,0:T(8,128)(2,1)S(1)}) custom-call(bf16[128,128]{1,0:T(8,128)(2,1)} %k_in.1, bf16[128,128]{1,0:T(8,128)(2,1)} %v_in.1, bf16[32,2048]{1,0:T(8,128)(2,1)} %skip_in.1, ...), custom_call_target="tpu_custom_call" | custom-call | bytes 262144 | tf_op jit(solution)/shard_map/pallas_call | solution.py:156
  14.8 3.3 %collective-permute-start.2 = (bf16[208,256]{1,0:T(8,128)(2,1)S(1)}, bf16[208,256]{1,0:T(8,128)(2,1)S(1)}, u32[]{:S(2)}, u32[]{:S(2)}) collective-permute-start(bf16[208,256]{1,0:T(8,128)(2,1)S(1)} %get-tuple-element.35), channel_id=1, source_target_pairs={{0,4},{4,12},{12,8},{8,0},{1,5},{5,13},{13,9},{9,1},{2,6},{6,14},{... | collective-permute-start | bytes 319496 | tf_op jit(solution)/shard_map/ppermute | solution.py:141
  18.1 5.6 %collective-permute-done.2.refs_4_.refs_2_.refs_5_ = bf16[208,256]{1,0:T(8,128)(2,1)S(1)} collective-permute-done((bf16[208,256]{1,0:T(8,128)(2,1)S(1)}, bf16[208,256]{1,0:T(8,128)(2,1)S(1)}, u32[]{:S(2)}, u32[]{:S(2)}) %collective-permute-start.2) | collective-permute-done | bytes 106528 | tf_op jit(solution)/shard_map/ppermute | solution.py:141
  25.0 3.4 %collective-permute-done.4.refs_6_.refs_4_.refs_7_ = bf16[208,256]{1,0:T(8,128)(2,1)S(1)} collective-permute-done((bf16[208,256]{1,0:T(8,128)(2,1)S(1)}, bf16[208,256]{1,0:T(8,128)(2,1)S(1)}, u32[]{:S(2)}, u32[]{:S(2)}) %collective-permute-start.4) | collective-permute-done | bytes 106528 | tf_op jit(solution)/shard_map/ppermute | solution.py:141
  28.4 1.9 %collective-permute-start.3 = (bf16[128,256]{1,0:T(8,128)(2,1)S(1)}, bf16[128,256]{1,0:T(8,128)(2,1)S(1)}, u32[]{:S(2)}, u32[]{:S(2)}) collective-permute-start(bf16[128,256]{1,0:T(8,128)(2,1)S(1)} %slice.4), channel_id=1, source_target_pairs={{0,4},{4,12},{12,8},{8,0},{1,5},{5,13},{13,9},{9,1},{2,6},{6,14},{... | collective-permute-start | bytes 196616 | tf_op jit(solution)/shard_map/ppermute | solution.py:141
  30.3 2.0 %collective-permute-start.6 = (bf16[128,1024]{1,0:T(8,128)(2,1)S(1)}, bf16[128,1024]{1,0:T(8,128)(2,1)S(1)}, u32[]{:S(2)}, u32[]{:S(2)}) collective-permute-start(bf16[128,1024]{1,0:T(8,128)(2,1)S(1)} %collective-permute-done.1.refs_2_), channel_id=1, source_target_pairs={{0,4},{4,12},{12,8},{8,0},{1,5},{5,13},{13,9},{9,1},{2,6},{6,14},{... | collective-permute-start | bytes 786440 | tf_op jit(solution)/shard_map/ppermute | solution.py:141
  32.4 2.3 %shard_map.122 = (bf16[1024,512]{1,0:T(8,128)(2,1)S(1)}, bf16[128,1024]{1,0:T(8,128)(2,1)S(1)}, bf16[1,768,2048]{2,1,0:T(8,128)(2,1)S(1)}) custom-call(bf16[1024,512]{1,0:T(8,128)(2,1)} %refs_0_.1, bf16[128,1024]{1,0:T(8,128)(2,1)} %refs_1_.1, bf16[1,768,2048]{2,1,0:T(8,128)(2,1)} %refs_2_.1), custom_call_target="tpu_custom_call" | custom-call | bytes 4194304 | tf_op jit(solution)/shard_map/pallas_call | solution.py:156
  34.7 3.8 %shard_map.124 = (f32[3,2,32,512]{3,2,1,0:T(8,128)S(1)}, bf16[3,2,32,512]{3,2,1,0:T(8,128)(2,1)S(1)}) custom-call(bf16[128,1024]{1,0:T(8,128)(2,1)S(1)} %get-tuple-element.33.refs_0_, bf16[128,1024]{1,0:T(8,128)(2,1)S(1)} %collective-permute-done.refs_1_, bf16[128,1024]{1,0:T(8,128)(2,1)S(1)} %collective-permute-done.1.refs_2_, ...), custom_call_target="tpu_custom_call" | custom-call | flops 1207959552 | bytes 1048576 | tf_op jit(solution)/shard_map/pallas_call | solution.py:156
  38.6 1.4 %shard_map.126 = (f32[1,2,32,512]{3,2,1,0:T(8,128)S(1)}, bf16[1,2,32,512]{3,2,1,0:T(8,128)(2,1)S(1)}) custom-call(bf16[128,1024]{1,0:T(8,128)(2,1)S(1)} %collective-permute-done.6.refs_0_, bf16[128,256]{1,0:T(8,128)(2,1)S(1)} %get-tuple-element.34.refs_3_.refs_1_, bf16[208,256]{1,0:T(8,128)(2,1)S(1)} %collective-permute-done.2.refs_4_.refs_2_.refs_5_, ...), custom_call_target="tpu_custom_call" | custom-call | flops 402653184 | bytes 1048576 | tf_op jit(solution)/shard_map/pallas_call | solution.py:156
  40.6 1.6 %collective-permute-start.8 = (bf16[3,32,512]{2,1,0:T(8,128)(2,1)S(1)}, bf16[3,32,512]{2,1,0:T(8,128)(2,1)S(1)}, u32[]{:S(2)}, u32[]{:S(2)}) collective-permute-start(bf16[3,32,512]{2,1,0:T(8,128)(2,1)S(1)} %get-tuple-element.44), channel_id=1, source_target_pairs={{0,2},{1,3},{2,0},{3,1},{4,6},{5,7},{6,4},{7,5},{8,10},{9,11},{10,... | collective-permute-start | bytes 294920 | tf_op jit(solution)/shard_map/ppermute | solution.py:146
  42.1 2.3 %collective-permute-start.10 = (bf16[80,256]{1,0:T(8,128)(2,1)S(1)}, bf16[80,256]{1,0:T(8,128)(2,1)S(1)}, u32[]{:S(2)}, u32[]{:S(2)}) collective-permute-start(bf16[80,256]{1,0:T(8,128)(2,1)S(1)} %get-tuple-element.47), channel_id=1, source_target_pairs={{0,12},{4,8},{12,0},{8,4},{1,13},{5,9},{13,1},{9,5},{2,14},{6,10},... | collective-permute-start | bytes 122888 | tf_op jit(solution)/shard_map/ppermute | solution.py:141
  44.5 3.4 %collective-permute-done.10.refs_6_ = bf16[80,256]{1,0:T(8,128)(2,1)S(1)} collective-permute-done((bf16[80,256]{1,0:T(8,128)(2,1)S(1)}, bf16[80,256]{1,0:T(8,128)(2,1)S(1)}, u32[]{:S(2)}, u32[]{:S(2)}) %collective-permute-start.10) | collective-permute-done | bytes 40992 | tf_op jit(solution)/shard_map/ppermute | solution.py:141
  48.7 3.1 %collective-permute-done.9.refs_3_ = bf16[1,32,512]{2,1,0:T(8,128)(2,1)S(1)} collective-permute-done((bf16[1,32,512]{2,1,0:T(8,128)(2,1)S(1)}, bf16[1,32,512]{2,1,0:T(8,128)(2,1)S(1)}, u32[]{:S(2)}, u32[]{:S(2)}) %collective-permute-start.9) | collective-permute-done | bytes 32800 | tf_op jit(solution)/shard_map/ppermute | solution.py:146
  52.0 2.9 %collective-permute-start.11 = (bf16[4,32,512]{2,1,0:T(8,128)(2,1)S(1)}, bf16[4,32,512]{2,1,0:T(8,128)(2,1)S(1)}, u32[]{:S(2)}, u32[]{:S(2)}) collective-permute-start(bf16[4,32,512]{2,1,0:T(8,128)(2,1)S(1)} %get-tuple-element.49), channel_id=1, source_target_pairs={{0,4},{4,0},{8,12},{12,8},{1,5},{5,1},{9,13},{13,9},{2,6},{6,2},{1... | collective-permute-start | bytes 393224 | tf_op jit(solution)/shard_map/ppermute | solution.py:129
  54.9 3.9 %collective-permute-done.12.refs_2_ = bf16[4,32,512]{2,1,0:T(8,128)(2,1)S(1)} collective-permute-done((bf16[4,32,512]{2,1,0:T(8,128)(2,1)S(1)}, bf16[4,32,512]{2,1,0:T(8,128)(2,1)S(1)}, u32[]{:S(2)}, u32[]{:S(2)}) %collective-permute-start.12) | collective-permute-done | bytes 131104 | tf_op jit(solution)/shard_map/ppermute | solution.py:129
  60.8 3.9 %collective-permute-done.17.refs_0_ = bf16[4,32,640]{2,1,0:T(8,128)(2,1)S(1)} collective-permute-done((bf16[4,32,640]{2,1,0:T(8,128)(2,1)S(1)}, bf16[4,32,640]{2,1,0:T(8,128)(2,1)S(1)}, u32[]{:S(2)}, u32[]{:S(2)}) %collective-permute-start.17) | collective-permute-done | bytes 163872 | tf_op jit(solution)/shard_map/ppermute | solution.py:146
  64.7 2.8 %collective-permute-done.19.refs_2_ = bf16[4,32,512]{2,1,0:T(8,128)(2,1)S(1)} collective-permute-done((bf16[4,32,512]{2,1,0:T(8,128)(2,1)S(1)}, bf16[4,32,512]{2,1,0:T(8,128)(2,1)S(1)}, u32[]{:S(2)}, u32[]{:S(2)}) %collective-permute-start.19) | collective-permute-done | bytes 131104 | tf_op jit(solution)/shard_map/ppermute | solution.py:146
  67.8 1.8 %collective-permute-done.13.refs_3_ = bf16[4,32,512]{2,1,0:T(8,128)(2,1)S(1)} collective-permute-done((bf16[4,32,512]{2,1,0:T(8,128)(2,1)S(1)}, bf16[4,32,512]{2,1,0:T(8,128)(2,1)S(1)}, u32[]{:S(2)}, u32[]{:S(2)}) %collective-permute-start.13) | collective-permute-done | bytes 131104 | tf_op jit(solution)/shard_map/ppermute | solution.py:129
  70.0 2.4 %collective-permute-done.18.refs_1_ = bf16[4,32,512]{2,1,0:T(8,128)(2,1)S(1)} collective-permute-done((bf16[4,32,512]{2,1,0:T(8,128)(2,1)S(1)}, bf16[4,32,512]{2,1,0:T(8,128)(2,1)S(1)}, u32[]{:S(2)}, u32[]{:S(2)}) %collective-permute-start.18) | collective-permute-done | bytes 131104 | tf_op jit(solution)/shard_map/ppermute | solution.py:146
  72.5 1.5 %shard_map.131 = (f32[4,128,768]{2,1,0:T(8,128)S(1)}, f32[128,128]{1,0:T(8,128)S(1)}) custom-call(bf16[4,32,640]{2,1,0:T(8,128)(2,1)S(1)} %collective-permute-done.17.refs_0_, bf16[4,32,512]{2,1,0:T(8,128)(2,1)S(1)} %collective-permute-done.18.refs_1_, bf16[4,32,512]{2,1,0:T(8,128)(2,1)S(1)} %collective-permute-done.19.refs_2_, f32[1,2048]{1,0:T(1,128)S(1)} %bitcast.3, ...), custom_call_target="tpu_custom_call" | custom-call | flops 1207959552 | bytes 12582912 | tf_op jit(solution)/shard_map/pallas_call | solution.py:156
  73.9 2.1 %collective-permute-done.20.refs_3_ = bf16[4,32,512]{2,1,0:T(8,128)(2,1)S(1)} collective-permute-done((bf16[4,32,512]{2,1,0:T(8,128)(2,1)S(1)}, bf16[4,32,512]{2,1,0:T(8,128)(2,1)S(1)}, u32[]{:S(2)}, u32[]{:S(2)}) %collective-permute-start.20) | collective-permute-done | bytes 131104 | tf_op jit(solution)/shard_map/ppermute | solution.py:146
  76.0 1.8 %shard_map.132 = (bf16[32,2048]{1,0:T(8,128)(2,1)S(1)}, bf16[32,2048]{1,0:T(8,128)(2,1)S(1)}, bf16[32,2048]{1,0:T(8,128)(2,1)S(1)}, bf16[32,2048]{1,0:T(8,128)(2,1)S(1)}) custom-call(bf16[4,32,640]{2,1,0:T(8,128)(2,1)S(1)} %collective-permute-done.17.refs_0_, bf16[4,32,512]{2,1,0:T(8,128)(2,1)S(1)} %collective-permute-done.18.refs_1_, ...), custom_call_target="tpu_custom_call" | custom-call | flops 1207959552 | bytes 18874368 | tf_op jit(solution)/shard_map/pallas_call | solution.py:156
  77.9 2.0 %collective-permute-start.22 = (bf16[32,2048]{1,0:T(8,128)(2,1)S(1)}, bf16[32,2048]{1,0:T(8,128)(2,1)S(1)}, u32[]{:S(2)}, u32[]{:S(2)}) collective-permute-start(bf16[32,2048]{1,0:T(8,128)(2,1)S(1)} %get-tuple-element.59), channel_id=1, source_target_pairs={{0,2},{1,3},{2,0},{3,1},{4,6},{5,7},{6,4},{7,5},{8,10},{9,11},{10,... | collective-permute-start | bytes 393224 | tf_op jit(solution)/shard_map/ppermute | solution.py:146
  79.9 1.9 %collective-permute-start.26 = (bf16[32,2048]{1,0:T(8,128)(2,1)S(1)}, bf16[32,2048]{1,0:T(8,128)(2,1)S(1)}, u32[]{:S(2)}, u32[]{:S(2)}) collective-permute-start(bf16[32,2048]{1,0:T(8,128)(2,1)S(1)} %get-tuple-element.63), channel_id=1, source_target_pairs={{0,2},{1,3},{2,0},{3,1},{4,6},{5,7},{6,4},{7,5},{8,10},{9,11},{10,... | collective-permute-start | bytes 393224 | tf_op jit(solution)/shard_map/ppermute | solution.py:146
  81.9 1.4 %shard_map.129 = (f32[4,128,768]{2,1,0:T(8,128)S(1)}, f32[128,128]{1,0:T(8,128)S(1)}) custom-call(bf16[4,32,640]{2,1,0:T(8,128)(2,1)S(1)} %get-tuple-element.48.refs_0_, bf16[4,32,512]{2,1,0:T(8,128)(2,1)S(1)} %collective-permute-done.11.refs_1_, bf16[4,32,512]{2,1,0:T(8,128)(2,1)S(1)} %collective-permute-done.12.refs_2_, f32[1,2048]{1,0:T(1,128)S(1)} %bitcast.5, ...), custom_call_target="tpu_custom_call" | custom-call | flops 1207959552 | bytes 12582912 | tf_op jit(solution)/shard_map/pallas_call | solution.py:156
  83.3 1.8 %shard_map.130 = (f32[32,2048]{1,0:T(8,128)S(1)}, f32[32,2048]{1,0:T(8,128)S(1)}, f32[32,2048]{1,0:T(8,128)S(1)}, f32[32,2048]{1,0:T(8,128)S(1)}, bf16[32,2048]{1,0:T(8,128)(2,1)}) custom-call(bf16[4,32,640]{2,1,0:T(8,128)(2,1)S(1)} %get-tuple-element.48.refs_0_, bf16[4,32,512]{2,1,0:T(8,128)(2,1)S(1)} %collective-permute-done.11.refs_1_, ...), custom_call_target="tpu_custom_call" | custom-call | flops 1207959552 | bytes 18874368 | tf_op jit(solution)/shard_map/pallas_call | solution.py:156
  85.7 2.8 %collective-permute-start.25 = (bf16[32,2048]{1,0:T(8,128)(2,1)S(1)}, bf16[32,2048]{1,0:T(8,128)(2,1)S(1)}, u32[]{:S(2)}, u32[]{:S(2)}) collective-permute-start(bf16[32,2048]{1,0:T(8,128)(2,1)S(1)} %shard_map.134), channel_id=1, source_target_pairs={{0,8},{4,12},{8,0},{12,4},{1,9},{5,13},{9,1},{13,5},{2,10},{6,14},... | collective-permute-start | bytes 393224 | tf_op jit(solution)/shard_map/ppermute | solution.py:129
  88.5 1.4 %collective-permute-start.27 = (bf16[32,2048]{1,0:T(8,128)(2,1)S(1)}, bf16[32,2048]{1,0:T(8,128)(2,1)S(1)}, u32[]{:S(2)}, u32[]{:S(2)}) collective-permute-start(bf16[32,2048]{1,0:T(8,128)(2,1)S(1)} %shard_map.135), channel_id=1, source_target_pairs={{0,12},{4,8},{8,4},{12,0},{1,13},{5,9},{9,5},{13,1},{2,14},{6,10},... | collective-permute-start | bytes 393224 | tf_op jit(solution)/shard_map/ppermute | solution.py:129
  90.3 2.7 %collective-permute-done.25 = bf16[32,2048]{1,0:T(8,128)(2,1)S(1)} collective-permute-done((bf16[32,2048]{1,0:T(8,128)(2,1)S(1)}, bf16[32,2048]{1,0:T(8,128)(2,1)S(1)}, u32[]{:S(2)}, u32[]{:S(2)}) %collective-permute-start.25) | collective-permute-done | bytes 131104 | tf_op jit(solution)/shard_map/ppermute | solution.py:129
  93.0 2.4 %collective-permute-done.27 = bf16[32,2048]{1,0:T(8,128)(2,1)S(1)} collective-permute-done((bf16[32,2048]{1,0:T(8,128)(2,1)S(1)}, bf16[32,2048]{1,0:T(8,128)(2,1)S(1)}, u32[]{:S(2)}, u32[]{:S(2)}) %collective-permute-start.27) | collective-permute-done | bytes 131104 | tf_op jit(solution)/shard_map/ppermute | solution.py:129
  (46 shorter events, 9.5 us)
Async XLA Ops:
  0.6 71.8 %collective-permute-start.14 = (bf16[1,2048,768]{2,1,0:T(8,128)(2,1)}, bf16[1,2048,768]{2,1,0:T(8,128)(2,1)S(1)}, u32[]{:S(2)}, u32[]{:S(2)}) collective-permute-start(bf16[1,2048,768]{2,1,0:T(8,128)(2,1)} %refs_7_.3), channel_id=1, source_target_pairs={{0,1},{1,0},{2,3},{3,2},{4,5},{5,4},{6,7},{7,6},{8,9},{9,8},{10,11... | collective-permute-start | bytes 9437192 | tf_op jit(solution)/shard_map/ppermute | solution.py:146
  1.2 71.2 %collective-permute-start.15 = (bf16[1,2048,768]{2,1,0:T(8,128)(2,1)}, bf16[1,2048,768]{2,1,0:T(8,128)(2,1)S(1)}, u32[]{:S(2)}, u32[]{:S(2)}) collective-permute-start(bf16[1,2048,768]{2,1,0:T(8,128)(2,1)} %refs_8_.3), channel_id=1, source_target_pairs={{0,1},{1,0},{2,3},{3,2},{4,5},{5,4},{6,7},{7,6},{8,9},{9,8},{10,11... | collective-permute-start | bytes 9437192 | tf_op jit(solution)/shard_map/ppermute | solution.py:146
  1.3 74.7 %collective-permute-start.16 = (bf16[1,768,2048]{2,1,0:T(8,128)(2,1)}, bf16[1,768,2048]{2,1,0:T(8,128)(2,1)S(1)}, u32[]{:S(2)}, u32[]{:S(2)}) collective-permute-start(bf16[1,768,2048]{2,1,0:T(8,128)(2,1)} %refs_2_.1), channel_id=1, source_target_pairs={{0,1},{1,0},{2,3},{3,2},{4,5},{5,4},{6,7},{7,6},{8,9},{9,8},{10,11... | collective-permute-start | bytes 9437192 | tf_op jit(solution)/shard_map/ppermute | solution.py:146
  1.7 10.8 %collective-permute-start = (bf16[128,1024]{1,0:T(8,128)(2,1)}, bf16[128,1024]{1,0:T(8,128)(2,1)S(1)}, u32[]{:S(2)}, u32[]{:S(2)}) collective-permute-start(bf16[128,1024]{1,0:T(8,128)(2,1)} %refs_1_.1), channel_id=1, source_target_pairs={{0,4},{4,12},{12,8},{8,0},{1,5},{5,13},{13,9},{9,1},{2,6},{6,14},{... | collective-permute-start | bytes 786440 | tf_op jit(solution)/shard_map/ppermute | solution.py:141
  12.5 17.9 %collective-permute-start.1 = (bf16[128,1024]{1,0:T(8,128)(2,1)S(1)}, bf16[128,1024]{1,0:T(8,128)(2,1)S(1)}, u32[]{:S(2)}, u32[]{:S(2)}) collective-permute-start(bf16[128,1024]{1,0:T(8,128)(2,1)S(1)} %collective-permute-done.refs_1_), channel_id=1, source_target_pairs={{0,4},{4,12},{12,8},{8,0},{1,5},{5,13},{13,9},{9,1},{2,6},{6,14},{... | collective-permute-start | bytes 786440 | tf_op jit(solution)/shard_map/ppermute | solution.py:141
  14.8 8.9 %collective-permute-start.2 = (bf16[208,256]{1,0:T(8,128)(2,1)S(1)}, bf16[208,256]{1,0:T(8,128)(2,1)S(1)}, u32[]{:S(2)}, u32[]{:S(2)}) collective-permute-start(bf16[208,256]{1,0:T(8,128)(2,1)S(1)} %get-tuple-element.35), channel_id=1, source_target_pairs={{0,4},{4,12},{12,8},{8,0},{1,5},{5,13},{13,9},{9,1},{2,6},{6,14},{... | collective-permute-start | bytes 319496 | tf_op jit(solution)/shard_map/ppermute | solution.py:141
  23.7 4.7 %collective-permute-start.4 = (bf16[208,256]{1,0:T(8,128)(2,1)S(1)}, bf16[208,256]{1,0:T(8,128)(2,1)S(1)}, u32[]{:S(2)}, u32[]{:S(2)}) collective-permute-start(bf16[208,256]{1,0:T(8,128)(2,1)S(1)} %get-tuple-element.36), channel_id=1, source_target_pairs={{0,8},{4,0},{12,4},{8,12},{1,9},{5,1},{13,5},{9,13},{2,10},{6,2},{... | collective-permute-start | bytes 319496 | tf_op jit(solution)/shard_map/ppermute | solution.py:141
  28.4 6.3 %collective-permute-start.3 = (bf16[128,256]{1,0:T(8,128)(2,1)S(1)}, bf16[128,256]{1,0:T(8,128)(2,1)S(1)}, u32[]{:S(2)}, u32[]{:S(2)}) collective-permute-start(bf16[128,256]{1,0:T(8,128)(2,1)S(1)} %slice.4), channel_id=1, source_target_pairs={{0,4},{4,12},{12,8},{8,0},{1,5},{5,13},{13,9},{9,1},{2,6},{6,14},{... | collective-permute-start | bytes 196616 | tf_op jit(solution)/shard_map/ppermute | solution.py:141
  30.3 8.3 %collective-permute-start.6 = (bf16[128,1024]{1,0:T(8,128)(2,1)S(1)}, bf16[128,1024]{1,0:T(8,128)(2,1)S(1)}, u32[]{:S(2)}, u32[]{:S(2)}) collective-permute-start(bf16[128,1024]{1,0:T(8,128)(2,1)S(1)} %collective-permute-done.1.refs_2_), channel_id=1, source_target_pairs={{0,4},{4,12},{12,8},{8,0},{1,5},{5,13},{13,9},{9,1},{2,6},{6,14},{... | collective-permute-start | bytes 786440 | tf_op jit(solution)/shard_map/ppermute | solution.py:141
  34.7 37.8 %copy-start = (bf16[1,2048,768]{2,1,0:T(8,128)(2,1)S(1)}, bf16[1,2048,768]{2,1,0:T(8,128)(2,1)}, u32[]{:S(2)}) copy-start(bf16[1,2048,768]{2,1,0:T(8,128)(2,1)} %refs_7_.3) | copy-start | bytes 9437188
  34.7 37.7 %copy-start.1 = (bf16[1,2048,768]{2,1,0:T(8,128)(2,1)S(1)}, bf16[1,2048,768]{2,1,0:T(8,128)(2,1)}, u32[]{:S(2)}) copy-start(bf16[1,2048,768]{2,1,0:T(8,128)(2,1)} %refs_8_.3) | copy-start | bytes 9437188
  34.7 37.7 %copy-start.2 = (f32[2048]{0:T(1024)S(1)}, f32[2048]{0:T(1024)}, u32[]{:S(2)}) copy-start(f32[2048]{0:T(1024)} %param.16) | copy-start | bytes 24580
  38.5 2.0 %collective-permute-start.5 = (bf16[3,2,32,512]{3,2,1,0:T(8,128)(2,1)S(1)}, bf16[3,2,32,512]{3,2,1,0:T(8,128)(2,1)S(1)}, u32[]{:S(2)}, u32[]{:S(2)}) collective-permute-start(bf16[3,2,32,512]{3,2,1,0:T(8,128)(2,1)S(1)} %get-tuple-element.39), channel_id=1, source_target_pairs={{0,1},{1,0},{2,3},{3,2},{4,5},{5,4},{6,7},{7,6},{8,9},{9,8},{10,11... | collective-permute-start | bytes 589832 | tf_op jit(solution)/shard_map/ppermute | solution.py:146
  40.0 2.2 %collective-permute-start.7 = (bf16[1,2,32,512]{3,2,1,0:T(8,128)(2,1)S(1)}, bf16[1,2,32,512]{3,2,1,0:T(8,128)(2,1)S(1)}, u32[]{:S(2)}, u32[]{:S(2)}) collective-permute-start(bf16[1,2,32,512]{3,2,1,0:T(8,128)(2,1)S(1)} %get-tuple-element.42), channel_id=1, source_target_pairs={{0,1},{1,0},{2,3},{3,2},{4,5},{5,4},{6,7},{7,6},{8,9},{9,8},{10,11... | collective-permute-start | bytes 196616 | tf_op jit(solution)/shard_map/ppermute | solution.py:146
  40.6 8.2 %collective-permute-start.8 = (bf16[3,32,512]{2,1,0:T(8,128)(2,1)S(1)}, bf16[3,32,512]{2,1,0:T(8,128)(2,1)S(1)}, u32[]{:S(2)}, u32[]{:S(2)}) collective-permute-start(bf16[3,32,512]{2,1,0:T(8,128)(2,1)S(1)} %get-tuple-element.44), channel_id=1, source_target_pairs={{0,2},{1,3},{2,0},{3,1},{4,6},{5,7},{6,4},{7,5},{8,10},{9,11},{10,... | collective-permute-start | bytes 294920 | tf_op jit(solution)/shard_map/ppermute | solution.py:146
  42.1 5.8 %collective-permute-start.10 = (bf16[80,256]{1,0:T(8,128)(2,1)S(1)}, bf16[80,256]{1,0:T(8,128)(2,1)S(1)}, u32[]{:S(2)}, u32[]{:S(2)}) collective-permute-start(bf16[80,256]{1,0:T(8,128)(2,1)S(1)} %get-tuple-element.47), channel_id=1, source_target_pairs={{0,12},{4,8},{12,0},{8,4},{1,13},{5,9},{13,1},{9,5},{2,14},{6,10},... | collective-permute-start | bytes 122888 | tf_op jit(solution)/shard_map/ppermute | solution.py:141
  47.9 3.9 %collective-permute-start.9 = (bf16[1,32,512]{2,1,0:T(8,128)(2,1)S(1)}, bf16[1,32,512]{2,1,0:T(8,128)(2,1)S(1)}, u32[]{:S(2)}, u32[]{:S(2)}) collective-permute-start(bf16[1,32,512]{2,1,0:T(8,128)(2,1)S(1)} %get-tuple-element.45), channel_id=1, source_target_pairs={{0,2},{1,3},{2,0},{3,1},{4,6},{5,7},{6,4},{7,5},{8,10},{9,11},{10,... | collective-permute-start | bytes 98312 | tf_op jit(solution)/shard_map/ppermute | solution.py:146
  51.9 6.9 %collective-permute-start.12 = (bf16[4,32,512]{2,1,0:T(8,128)(2,1)S(1)}, bf16[4,32,512]{2,1,0:T(8,128)(2,1)S(1)}, u32[]{:S(2)}, u32[]{:S(2)}) collective-permute-start(bf16[4,32,512]{2,1,0:T(8,128)(2,1)S(1)} %get-tuple-element.49), channel_id=1, source_target_pairs={{0,8},{4,12},{8,0},{12,4},{1,9},{5,13},{9,1},{13,5},{2,10},{6,14},... | collective-permute-start | bytes 393224 | tf_op jit(solution)/shard_map/ppermute | solution.py:129
  52.0 7.7 %collective-permute-start.11 = (bf16[4,32,512]{2,1,0:T(8,128)(2,1)S(1)}, bf16[4,32,512]{2,1,0:T(8,128)(2,1)S(1)}, u32[]{:S(2)}, u32[]{:S(2)}) collective-permute-start(bf16[4,32,512]{2,1,0:T(8,128)(2,1)S(1)} %get-tuple-element.49), channel_id=1, source_target_pairs={{0,4},{4,0},{8,12},{12,8},{1,5},{5,1},{9,13},{13,9},{2,6},{6,2},{1... | collective-permute-start | bytes 393224 | tf_op jit(solution)/shard_map/ppermute | solution.py:129
  58.8 5.9 %collective-permute-start.17 = (bf16[4,32,640]{2,1,0:T(8,128)(2,1)S(1)}, bf16[4,32,640]{2,1,0:T(8,128)(2,1)S(1)}, u32[]{:S(2)}, u32[]{:S(2)}) collective-permute-start(bf16[4,32,640]{2,1,0:T(8,128)(2,1)S(1)} %get-tuple-element.48.refs_0_), channel_id=1, source_target_pairs={{0,2},{1,3},{2,0},{3,1},{4,6},{5,7},{6,4},{7,5},{8,10},{9,11},{10,... | collective-permute-start | bytes 491528 | tf_op jit(solution)/shard_map/ppermute | solution.py:146
  59.7 7.8 %collective-permute-start.19 = (bf16[4,32,512]{2,1,0:T(8,128)(2,1)S(1)}, bf16[4,32,512]{2,1,0:T(8,128)(2,1)S(1)}, u32[]{:S(2)}, u32[]{:S(2)}) collective-permute-start(bf16[4,32,512]{2,1,0:T(8,128)(2,1)S(1)} %collective-permute-done.12.refs_2_), channel_id=1, source_target_pairs={{0,2},{1,3},{2,0},{3,1},{4,6},{5,7},{6,4},{7,5},{8,10},{9,11},{10,... | collective-permute-start | bytes 393224 | tf_op jit(solution)/shard_map/ppermute | solution.py:146
  64.7 5.0 %collective-permute-start.13 = (bf16[4,32,512]{2,1,0:T(8,128)(2,1)S(1)}, bf16[4,32,512]{2,1,0:T(8,128)(2,1)S(1)}, u32[]{:S(2)}, u32[]{:S(2)}) collective-permute-start(bf16[4,32,512]{2,1,0:T(8,128)(2,1)S(1)} %collective-permute-done.12.refs_2_), channel_id=1, source_target_pairs={{0,4},{4,0},{8,12},{12,8},{1,5},{5,1},{9,13},{13,9},{2,6},{6,2},{1... | collective-permute-start | bytes 393224 | tf_op jit(solution)/shard_map/ppermute | solution.py:129
  67.5 5.0 %collective-permute-start.18 = (bf16[4,32,512]{2,1,0:T(8,128)(2,1)S(1)}, bf16[4,32,512]{2,1,0:T(8,128)(2,1)S(1)}, u32[]{:S(2)}, u32[]{:S(2)}) collective-permute-start(bf16[4,32,512]{2,1,0:T(8,128)(2,1)S(1)} %collective-permute-done.11.refs_1_), channel_id=1, source_target_pairs={{0,2},{1,3},{2,0},{3,1},{4,6},{5,7},{6,4},{7,5},{8,10},{9,11},{10,... | collective-permute-start | bytes 393224 | tf_op jit(solution)/shard_map/ppermute | solution.py:146
  69.6 6.4 %collective-permute-start.20 = (bf16[4,32,512]{2,1,0:T(8,128)(2,1)S(1)}, bf16[4,32,512]{2,1,0:T(8,128)(2,1)S(1)}, u32[]{:S(2)}, u32[]{:S(2)}) collective-permute-start(bf16[4,32,512]{2,1,0:T(8,128)(2,1)S(1)} %collective-permute-done.13.refs_3_), channel_id=1, source_target_pairs={{0,2},{1,3},{2,0},{3,1},{4,6},{5,7},{6,4},{7,5},{8,10},{9,11},{10,... | collective-permute-start | bytes 393224 | tf_op jit(solution)/shard_map/ppermute | solution.py:146
  77.8 12.1 %collective-permute-start.21 = (bf16[32,2048]{1,0:T(8,128)(2,1)S(1)}, bf16[32,2048]{1,0:T(8,128)(2,1)S(1)}, u32[]{:S(2)}, u32[]{:S(2)}) collective-permute-start(bf16[32,2048]{1,0:T(8,128)(2,1)S(1)} %get-tuple-element.57), channel_id=1, source_target_pairs={{0,2},{1,3},{2,0},{3,1},{4,6},{5,7},{6,4},{7,5},{8,10},{9,11},{10,... | collective-permute-start | bytes 393224 | tf_op jit(solution)/shard_map/ppermute | solution.py:146
  77.9 7.3 %collective-permute-start.22 = (bf16[32,2048]{1,0:T(8,128)(2,1)S(1)}, bf16[32,2048]{1,0:T(8,128)(2,1)S(1)}, u32[]{:S(2)}, u32[]{:S(2)}) collective-permute-start(bf16[32,2048]{1,0:T(8,128)(2,1)S(1)} %get-tuple-element.59), channel_id=1, source_target_pairs={{0,2},{1,3},{2,0},{3,1},{4,6},{5,7},{6,4},{7,5},{8,10},{9,11},{10,... | collective-permute-start | bytes 393224 | tf_op jit(solution)/shard_map/ppermute | solution.py:146
  79.9 5.8 %collective-permute-start.24 = (bf16[32,2048]{1,0:T(8,128)(2,1)S(1)}, bf16[32,2048]{1,0:T(8,128)(2,1)S(1)}, u32[]{:S(2)}, u32[]{:S(2)}) collective-permute-start(bf16[32,2048]{1,0:T(8,128)(2,1)S(1)} %get-tuple-element.61), channel_id=1, source_target_pairs={{0,2},{1,3},{2,0},{3,1},{4,6},{5,7},{6,4},{7,5},{8,10},{9,11},{10,... | collective-permute-start | bytes 393224 | tf_op jit(solution)/shard_map/ppermute | solution.py:146
  79.9 8.5 %collective-permute-start.26 = (bf16[32,2048]{1,0:T(8,128)(2,1)S(1)}, bf16[32,2048]{1,0:T(8,128)(2,1)S(1)}, u32[]{:S(2)}, u32[]{:S(2)}) collective-permute-start(bf16[32,2048]{1,0:T(8,128)(2,1)S(1)} %get-tuple-element.63), channel_id=1, source_target_pairs={{0,2},{1,3},{2,0},{3,1},{4,6},{5,7},{6,4},{7,5},{8,10},{9,11},{10,... | collective-permute-start | bytes 393224 | tf_op jit(solution)/shard_map/ppermute | solution.py:146
  85.2 5.0 %collective-permute-start.23 = (bf16[32,2048]{1,0:T(8,128)(2,1)S(1)}, bf16[32,2048]{1,0:T(8,128)(2,1)S(1)}, u32[]{:S(2)}, u32[]{:S(2)}) collective-permute-start(bf16[32,2048]{1,0:T(8,128)(2,1)S(1)} %shard_map.133), channel_id=1, source_target_pairs={{0,4},{4,0},{8,12},{12,8},{1,5},{5,1},{9,13},{13,9},{2,6},{6,2},{1... | collective-permute-start | bytes 393224 | tf_op jit(solution)/shard_map/ppermute | solution.py:129
  85.7 7.3 %collective-permute-start.25 = (bf16[32,2048]{1,0:T(8,128)(2,1)S(1)}, bf16[32,2048]{1,0:T(8,128)(2,1)S(1)}, u32[]{:S(2)}, u32[]{:S(2)}) collective-permute-start(bf16[32,2048]{1,0:T(8,128)(2,1)S(1)} %shard_map.134), channel_id=1, source_target_pairs={{0,8},{4,12},{8,0},{12,4},{1,9},{5,13},{9,1},{13,5},{2,10},{6,14},... | collective-permute-start | bytes 393224 | tf_op jit(solution)/shard_map/ppermute | solution.py:129
  88.5 6.9 %collective-permute-start.27 = (bf16[32,2048]{1,0:T(8,128)(2,1)S(1)}, bf16[32,2048]{1,0:T(8,128)(2,1)S(1)}, u32[]{:S(2)}, u32[]{:S(2)}) collective-permute-start(bf16[32,2048]{1,0:T(8,128)(2,1)S(1)} %shard_map.135), channel_id=1, source_target_pairs={{0,12},{4,8},{8,4},{12,0},{1,13},{5,9},{9,5},{13,1},{2,14},{6,10},... | collective-permute-start | bytes 393224 | tf_op jit(solution)/shard_map/ppermute | solution.py:129
